TPU v7x, 32 devices: a whole 2x2x4 slice. The times are simulated.
32 devices in a mesh: groups: 2 (over x), seq: 16 (over z, y, core).
Axes of the slice: x: 2, y: 2, z: 4, core: 2. Of those that a mesh axis runs over, the one named last changes fastest.
Arguments:
- enc_input: bfloat16 [8192, 1408], P(('groups', 'seq')), parts along dimension 0, may hold values from -6 to 6
- enc_weight: bfloat16 [2816, 1536], P('seq'), may hold values from -0.109375 to 0.109375
- norm_gain: float32 [1536], replicated, may hold values from 0.5 to 1.5
- q_weight: bfloat16 [1536, 1024], replicated, may hold values from -1 to 1
- kv_weight: bfloat16 [1536, 320], replicated, may hold values from -1 to 1
- out_weight: bfloat16 [1536, 1536], replicated, may hold values from -0.15625 to 0.15625
- dec_weight: float32 [3, 1536], replicated, may hold values from -3 to 3
- track_weight: bfloat16 [192, 1536], P('seq'), may hold values from -0.15625 to 0.15625
- track_grad: bfloat16 [4096, 192], P('groups', 'seq'), parts along dimension 0, may hold values from -6 to 6
- track_index: int32 [384], P('groups'), parts along dimension 0, may hold values from 0 to 191, each once
- track_mask: int32 [384], P('groups'), parts along dimension 0, may hold values 0 or 1
Outputs:
- trunk_out: bfloat16 [4096, 1536], P(('groups', 'seq')), parts along dimension 0
- skip_grad: bfloat16 [4096, 1536], P(('groups', 'seq')), parts along dimension 0
- dec_weight_grad: float32 [6, 1536], P('groups'), parts along dimension 0
There are 2 independent parts, one for each index of `groups`. A program takes and returns all parts, laid end to end along the dimension named above; an argument that names none is the same for every part. Nothing has to cross between parts.
Inputs may be any that keep to these rules, and one draw needn't show every extreme that they name: `track_index`: names every track once.
All inputs are finite; a program needn't handle non-finite values.
Results may differ from a plain program's by a relative error of at most 0.02.
Values may be sent and summed in bfloat16 or wider, within the bound.
No kernel may reach another device: no remote copies, remote signals or barrier semaphores. Data moves between devices by JAX's collectives and lax.ppermute only.
A program may use at most 128 MiB of HBM per device.

v0:
```python
import math

import jax
import jax.numpy as jnp
from jax import lax
from jax.sharding import PartitionSpec as P

HEADS = 8
QK = 128
VDIM = 192
DILATION_SPAN = 8


def with_halo(cells, sides, width):
    for axis, dim in sides:
        count = lax.axis_size(axis)
        ends = count - 1
        head = lax.slice_in_dim(cells, 0, width, axis=dim)
        tail = lax.slice_in_dim(cells, cells.shape[dim] - width, cells.shape[dim], axis=dim)
        cells = jnp.concatenate(
            [
                lax.ppermute(tail, axis, [(i, (i + 1) % count) for i in range(ends)]),
                cells,
                lax.ppermute(head, axis, [((i + 1) % count, i) for i in range(ends)]),
            ],
            axis=dim,
        )
    return cells


def gelu_tanh(values):
    return jax.nn.gelu(values, approximate=True)


def attention(tokens, tok_f, norm_gain, q_weight, kv_weight, out_weight):
    token_rows = tokens.shape[0]
    normed = (
        tok_f * lax.rsqrt(jnp.mean(tok_f * tok_f, axis=-1, keepdims=True) + 1e-06) * norm_gain
    ).astype(jnp.bfloat16)
    query = jnp.dot(normed, q_weight, preferred_element_type=jnp.float32).astype(jnp.bfloat16)
    keyval = jnp.dot(normed, kv_weight, preferred_element_type=jnp.float32).astype(jnp.bfloat16)
    query_rows = query.reshape(token_rows * HEADS, QK)

    def block_update(carry, key_block):
        running_max, running_sum, weighted = carry
        scores = lax.dot_general(
            query_rows,
            key_block[:, :QK],
            (((1,), (1,)), ((), ())),
            preferred_element_type=jnp.float32,
        ) * QK ** (-0.5)
        new_max = jnp.maximum(running_max, jnp.max(scores, axis=1))
        shrink = jnp.exp(running_max - new_max)
        expw = jnp.exp(scores - new_max[:, None])
        running_sum = running_sum * shrink + jnp.sum(expw, axis=1)
        weighted = weighted * shrink[:, None] + jnp.dot(
            expw.astype(jnp.bfloat16), key_block[:, QK:], preferred_element_type=jnp.float32
        )
        return (new_max, running_sum, weighted)

    start_state = (
        jnp.full((token_rows * HEADS,), -1e30, jnp.float32),
        jnp.zeros((token_rows * HEADS,), jnp.float32),
        jnp.zeros((token_rows * HEADS, VDIM), jnp.float32),
    )
    carry = start_state
    piece = lax.all_gather(keyval, "seq", axis=0, tiled=True)
    count = piece.shape[0]

    def step_fn(inner, key_block):
        return (block_update(inner, key_block), 0)

    carry, unused = lax.scan(step_fn, carry, piece.reshape(count // 128, 128, piece.shape[1]))
    running_max, running_sum, weighted = carry
    context = (
        (weighted / running_sum[:, None]).reshape(token_rows, HEADS * VDIM).astype(jnp.bfloat16)
    )
    return (tok_f + jnp.dot(context, out_weight, preferred_element_type=jnp.float32)).astype(
        jnp.bfloat16
    )


def decoder_back(tok_f, dec_weight, track_weight, track_grad, track_index, track_mask):
    token_rows = tok_f.shape[0]
    exchanged = lax.all_to_all(track_grad, "seq", split_axis=0, concat_axis=1, tiled=True)
    masked = exchanged * track_mask.astype(jnp.bfloat16)[None, :]
    every_row = lax.all_gather(track_weight, "seq", axis=0, tiled=True)
    selected = jnp.take(every_row, track_index, axis=0)
    head_f = jnp.dot(masked, selected, preferred_element_type=jnp.float32)
    head_gradient = head_f.astype(jnp.bfloat16)
    padded_input = with_halo(head_gradient, (("seq", 0),), DILATION_SPAN).astype(jnp.float32)
    skip_act, pullback = jax.vjp(gelu_tanh, tok_f)
    convback = jnp.zeros(tok_f.shape, jnp.float32)
    tap_terms = []
    for shift_amount in range(3):
        shifted_rows = padded_input[
            DILATION_SPAN * (2 - shift_amount) : DILATION_SPAN * (2 - shift_amount) + token_rows
        ]
        convback = convback + dec_weight[shift_amount][None, :] * shifted_rows
        tap_terms.append(jnp.sum(skip_act * shifted_rows, axis=0))
    skip_grad = pullback(convback)[0].astype(jnp.bfloat16)
    summed = lax.psum(jnp.stack(tap_terms, axis=0), "seq")
    dec_weight_grad = summed / jnp.float32(math.sqrt(token_rows * lax.axis_size("seq")))
    return (skip_grad, dec_weight_grad)


def shards(
    enc_input,
    enc_weight,
    norm_gain,
    q_weight,
    kv_weight,
    out_weight,
    dec_weight,
    track_weight,
    track_grad,
    track_index,
    track_mask,
):
    token_rows = enc_input.shape[0] // 2
    patches = enc_input.reshape(token_rows, 2 * enc_input.shape[1])
    tok_sum = jnp.dot(
        patches,
        lax.all_gather(enc_weight, "seq", axis=0, tiled=True),
        preferred_element_type=jnp.float32,
    )
    tokens = tok_sum.astype(jnp.bfloat16)
    tok_f = tokens.astype(jnp.float32)
    trunk_out = attention(tokens, tok_f, norm_gain, q_weight, kv_weight, out_weight)
    skip_grad, dec_weight_grad = decoder_back(
        tok_f, dec_weight, track_weight, track_grad, track_index, track_mask
    )
    return (trunk_out, skip_grad, dec_weight_grad)


def solution(mesh):
    return jax.shard_map(
        shards,
        mesh=mesh,
        in_specs=(
            P(("groups", "seq"), None),
            P("seq", None),
            P(),
            P(),
            P(),
            P(),
            P(),
            P("seq", None),
            P("groups", "seq"),
            P("groups"),
            P("groups"),
        ),
        out_specs=(P(("groups", "seq"), None), P(("groups", "seq"), None), P("groups", None)),
        check_vma=False,
    )
```

profile of v0, /device:TPU:0, one launch (start us, length us, event | category | flops | bytes accessed | tf_op | source)
XLA Modules:
  0.0 272.7 jit_solution(8789962556055584525)
XLA Ops:
  9.6 7.4 %all-to-all-start = ((bf16[16,128,12]{1,2,0:T(8,128)(2,1)}), bf16[16,128,12]{1,2,0:T(8,128)(2,1)S(1)}, u32[]{:S(2)}, u32[]{:S(2)}) async-start(bf16[16,128,12]{1,2,0:T(8,128)(2,1)} %copy.20), calls=%async_computation | async-start | bytes 131072 | tf_op jit(solution)/shard_map/all_to_all | solution.py:85
  17.1 30.1 %all-gather = bf16[16,12,1536]{2,1,0:T(8,128)(2,1)} all-gather(bf16[1,12,1536]{2,1,0:T(8,128)(2,1)} %bitcast.28), channel_id=1, replica_groups=mesh['groups'=2,'seq'=16] {'seq'}, dimensions={0}, use_global_device_ids=true | all-gather | bytes 626688 | tf_op jit(solution)/shard_map/all_gather | solution.py:87
  47.2 2.0 reshape.51
  51.3 3.6 %gather_fusion = bf16[192,1536]{1,0:T(8,128)(2,1)} fusion(bf16[192,1536]{1,0:T(8,128)(2,1)} %reshape.51, s32[1024]{0:T(1024)S(1)} %pad_clamp_fusion), kind=kCustom, calls=%fused_computation | custom fusion | bytes 1180416 | tf_op jit(solution)/shard_map/jit(_take)/gather | solution.py:88
  57.7 2.8 %collective-permute-start = (bf16[8,1536]{1,0:T(8,128)(2,1)}, bf16[8,1536]{1,0:T(8,128)(2,1)}, u32[]{:S(2)}, u32[]{:S(2)}) collective-permute-start(bf16[8,1536]{1,0:T(8,128)(2,1)} %get-tuple-element.101), channel_id=1, source_target_pairs={{0,1},{1,2},{2,3},{3,4},{4,5},{5,6},{6,7},{7,8},{8,9},{9,10},{10,1... | collective-permute-start | bytes 73736 | tf_op jit(solution)/shard_map/ppermute | solution.py:22
  61.7 1.5 slice_reduce_fusion.2
  63.2 2.1 reshape.38
  65.4 1.8 maximum_convert_fusion
  67.2 26.1 %all-gather.4.cloned.1.call-done = bf16[2816,1536]{1,0:T(8,128)(2,1)} async-done(((bf16[176,1536]{1,0:T(8,128)(2,1)}), bf16[2816,1536]{1,0:T(8,128)(2,1)}) %all-gather.4.cloned.1.call-update) | async-done | bytes 8650768 | tf_op jit(solution)/shard_map/all_gather | solution.py:124
  93.3 7.5 %multiply_reduce_fusion.3 = (f32[1536]{0:T(1024)S(1)}, f32[1536]{0:T(1024)S(1)}, f32[1536]{0:T(1024)S(1)}, f32[128]{0:T(128)S(1)}, bf16[128,1536]{1,0:T(8,128)(2,1)}, /*index=5*/f32[128,1536]{1,0:T(8,128)S(1)}) fusion(f32[144,1536]{1,0:T(8,128)} %maximum_convert_fusion, f32[1536]{0:T(1024)S(1)} %get-tuple-element.82, f32[1536]{0:T(1024)} %get-tuple-element.83, ...), kind=kOutput, calls=%fused_computation.34 | convolution fusion | flops 1114172800 | bytes 12947968 | tf_op jit(solution)/shard_map/dot_general | solution.py:122
  102.8 2.5 convolution_convert_fusion.2
  106.4 59.2 %psum.7 = f32[3,1536]{1,0:T(4,128)S(1)} all-reduce(f32[3,1536]{1,0:T(4,128)S(1)} %pad_maximum_fusion), channel_id=1, replica_groups=mesh['groups'=2,'seq'=16] {'seq'}, use_global_device_ids=true, to_apply=%region_8.9 | all-reduce | flops 4608 | bytes 36864 | tf_op jit(solution)/shard_map/psum | solution.py:102
  166.2 2.6 copy.21
  168.7 89.4 %while.15 = (s32[]{:T(128)}, f32[1024]{0:T(1024)S(1)}, f32[1024]{0:T(1024)S(1)}, f32[1024,192]{0,1:T(8,128)}, bf16[16,128,320]{2,1,0:T(8,128)(2,1)}, /*index=5*/bf16[1024,128]{1,0:T(8,128)(2,1)S(1)}, s32[]{:T(128)}, s32[]{:T(128)}) while((s32[]{:T(128)}, f32[1024]{0:T(1024)S(1)}, f32[1024]{0:T(1024)S(1)}, f32[1024,192]{0,1:T(8,128)}, ...), condition=%wide.region_4.5_spmd.clone, body=%wide.region_1.4_spmd.clone.sunk | while | flops 85267456 | bytes 3735653 | solution.py:73
  171.9 2.2 convolution_add_fusion.3
  177.2 2.5 convolution_add_fusion.3
  182.8 2.5 convolution_add_fusion.3
  188.4 2.5 convolution_add_fusion.3
  194.0 2.5 convolution_add_fusion.3
  199.6 2.5 convolution_add_fusion.3
  205.2 2.5 convolution_add_fusion.3
  210.8 2.5 convolution_add_fusion.3
  216.4 2.5 convolution_add_fusion.3
  222.0 2.5 convolution_add_fusion.3
  227.6 2.5 convolution_add_fusion.3
  233.2 2.5 convolution_add_fusion.3
  238.8 2.5 convolution_add_fusion.3
  244.4 2.5 convolution_add_fusion.3
  250.0 2.5 convolution_add_fusion.3
  255.6 2.5 convolution_add_fusion.3
  260.3 1.5 convert_element_type.46
  261.8 4.1 %fusion.8 = bf16[128,1536]{1,0:T(8,128)(2,1)} fusion(f32[128,1536]{1,0:T(8,128)} %copy-done.1, bf16[128,1536]{1,0:T(8,128)(2,1)S(1)} %convert_element_type.46, bf16[1536,1536]{1,0:T(8,128)(2,1)} %param.18), kind=kOutput, calls=%fused_computation.19 | convolution fusion | flops 604372992 | bytes 6291456 | tf_op jit(solution)/shard_map/dot_general | solution.py:78
  (136 shorter events, 64.0 us)
Async XLA Ops:
  7.2 95.6 %copy-start = (bf16[1536,1024]{1,0:T(8,128)(2,1)S(1)}, bf16[1536,1024]{1,0:T(8,128)(2,1)}, u32[]{:S(2)}) copy-start(bf16[1536,1024]{1,0:T(8,128)(2,1)} %param.16) | copy-start | bytes 9437188
  7.2 86.1 %all-gather.4.cloned.1.call-start = ((), (), s32[]{:S(2)}) async-start(), calls=%async_computation.1 | async-start | bytes 9191424 | tf_op jit(solution)/shard_map/all_gather | solution.py:124
  9.6 45.3 %all-to-all-start = ((bf16[16,128,12]{1,2,0:T(8,128)(2,1)}), bf16[16,128,12]{1,2,0:T(8,128)(2,1)S(1)}, u32[]{:S(2)}, u32[]{:S(2)}) async-start(bf16[16,128,12]{1,2,0:T(8,128)(2,1)} %copy.20), calls=%async_computation | async-start | bytes 131072 | tf_op jit(solution)/shard_map/all_to_all | solution.py:85
  17.0 149.2 %all-gather.6.cloned.1.call-start = ((), (), s32[]{:S(2)}) async-start(), calls=%async_computation.2 | async-start | bytes 1392640 | tf_op jit(solution)/shard_map/all_gather | solution.py:67
  57.7 7.7 %collective-permute-start = (bf16[8,1536]{1,0:T(8,128)(2,1)}, bf16[8,1536]{1,0:T(8,128)(2,1)}, u32[]{:S(2)}, u32[]{:S(2)}) collective-permute-start(bf16[8,1536]{1,0:T(8,128)(2,1)} %get-tuple-element.101), channel_id=1, source_target_pairs={{0,1},{1,2},{2,3},{3,4},{4,5},{5,6},{6,7},{7,8},{8,9},{9,10},{10,1... | collective-permute-start | bytes 73736 | tf_op jit(solution)/shard_map/ppermute | solution.py:22
  60.5 4.9 %collective-permute-start.1 = (bf16[8,1536]{1,0:T(8,128)(2,1)}, bf16[8,1536]{1,0:T(8,128)(2,1)}, u32[]{:S(2)}, u32[]{:S(2)}) collective-permute-start(bf16[8,1536]{1,0:T(8,128)(2,1)} %get-tuple-element.102), channel_id=1, source_target_pairs={{1,0},{2,1},{3,2},{4,3},{5,4},{6,5},{7,6},{8,7},{9,8},{10,9},{11,1... | collective-permute-start | bytes 73736 | tf_op jit(solution)/shard_map/ppermute | solution.py:24
  93.3 8.3 %copy-start.2 = (bf16[1536,320]{0,1:T(8,128)(2,1)S(1)}, bf16[1536,320]{0,1:T(8,128)(2,1)}, u32[]{:S(2)}) copy-start(bf16[1536,320]{0,1:T(8,128)(2,1)} %param.17) | copy-start | bytes 2949124
  93.3 8.3 %copy-start.3 = (f32[1536]{0:T(1024)S(1)}, f32[1536]{0:T(1024)}, u32[]{:S(2)}) copy-start(f32[1536]{0:T(1024)} %param.15) | copy-start | bytes 18436
  100.7 0.9 copy-start.1
Sparse Core Ops, SparseCore 0:
  10.3 82.9 all-gather.3
  102.9 36.2 all-gather.5
where the time goes:
time: 275 us; the launch traced here: 273 us
  blocking collectives  89.3 us (32%)
  matrix products  72.9 us (27%)
  local copies, waits for them, and re-layouts  33.7 us (12%)
  waiting for transfers between devices  26.8 us (10%)
  other arithmetic  24.2 us (9%)
  between operations  14.2 us (5%)
  starting transfers between devices  11.6 us (4%)
    psum x1, blocking collectives, decoder_back(): summed = lax.psum(jnp.stack(tap_terms, axis=0), 'seq')  59.2 us
    dot_general x16, matrix products, block_update(): jnp.dot(expw.astype(jnp.bfloat16), key_block[:, QK:], preferred_element_t...  39.6 us
    all_gather x1, blocking collectives, decoder_back(): every_row = lax.all_gather(track_weight, 'seq', axis=0, tiled=True)  30.1 us
    all_gather x1, waiting for transfers between devices, shards(): lax.all_gather(enc_weight, 'seq', axis=0, tiled=True)  26.1 us
    reduce_sum x16, other arithmetic, block_update(): running_sum = running_sum * shrink + jnp.sum(expw, axis=1)  18.2 us
    dot_general x16, matrix products, block_update(): lax.dot_general(query_rows, key_block[:, :QK], (((1,), (1,)), ((), ())),...  16.7 us
    squeeze x16, local copies, waits for them, and re-layouts, attention(): lax.scan(step_fn, carry, piece.reshape(count // 128, 128, piece.shape[1]))  14.4 us
    dot_general x1, matrix products, shards(): jnp.dot(patches, lax.all_gather(enc_weight, 'seq', axis=0, tiled=True), p...  7.46 us
  transfers between devices with their start and end apart: 5, of which 1 were waited for; matrix products, arithmetic and copies ran while one was open for 8% of the time, Pallas kernels for 0%

commit v1 on v0

v1 whole, which is shorter than its diff:
```python
import functools
import math

import jax
import jax.numpy as jnp
from jax import lax
from jax.experimental import pallas as pl
from jax.experimental.pallas import tpu as pltpu
from jax.sharding import Mesh, PartitionSpec as P

HEADS = 8
QK = 128
VDIM = 192
SPAN = 8
MIB = 1 << 20
VMEM = pl.BlockSpec(memory_space=pltpu.VMEM)
SMEM = pl.BlockSpec(memory_space=pltpu.SMEM)
ANY = pl.BlockSpec(memory_space=pl.ANY)


def chip_swap(cells, mask):
    count = lax.axis_size("chip")
    return lax.ppermute(cells, "chip", [(i, i ^ mask) for i in range(count)])


def core_swap(cells):
    return lax.ppermute(cells, "core", [(0, 1), (1, 0)])


def group_swap(cells):
    return lax.ppermute(cells, "groups", [(0, 1), (1, 0)])


def after(value, *others):
    return lax.optimization_barrier((value, *others))[0]


def tokens_kernel(rows, extra, ids_ref, own_ref, partner_ref, *refs):
    blocks, (own_out, partner_out, tracks_out, x_s, w_s, sems) = refs[:-6], refs[-6:]
    copies = []
    for at, block in enumerate(blocks):
        spot = ids_ref[at]
        for which, (first, length, target) in enumerate(
            ((0, rows, w_s), (rows, extra, tracks_out))
        ):
            copy = pltpu.make_async_copy(
                block.at[pl.ds(first, length)],
                target.at[pl.ds(pl.multiple_of(spot * length, 8), length)],
                sems.at[at, which],
            )
            copy.start()
            copies.append(copy)
    pairs, width = own_ref.shape
    half = pairs // 2
    line = lax.broadcasted_iota(jnp.int32, (half, pairs), 0)
    column = lax.broadcasted_iota(jnp.int32, (half, pairs), 1)
    for tap in range(2):
        pick = (column == 2 * line + tap).astype(jnp.bfloat16)
        for part, ref in enumerate((own_ref, partner_ref)):
            x_s[part * half : (part + 1) * half, tap * width : (tap + 1) * width] = jnp.dot(
                pick, ref[...], preferred_element_type=jnp.float32
            ).astype(jnp.bfloat16)
    for copy in copies:
        copy.wait()
    total = jnp.dot(x_s[...], w_s[...], preferred_element_type=jnp.float32).astype(jnp.bfloat16)
    own_out[...] = total[:half]
    partner_out[...] = total[half:]


def windows_kernel(grad_ref, out_ref):
    tracks = grad_ref.shape[0]
    count, lines, lanes = out_ref.shape
    rows = grad_ref.shape[1] // count
    lane = lax.broadcasted_iota(jnp.int32, (tracks, rows), 1)
    zero = jnp.zeros((tracks, rows), jnp.float32)
    out_ref[...] = jnp.zeros_like(out_ref)
    tiles = [grad_ref[:, at * rows : (at + 1) * rows].astype(jnp.float32) for at in range(count)]
    for at in range(count):
        after_it = tiles[at + 1] if at + 1 < count else zero
        before_it = pltpu.roll(tiles[at - 1], 2 * SPAN, 1) if at else zero
        edge = jnp.where(lane < SPAN, after_it, jnp.where(lane < 2 * SPAN, before_it, zero))
        out_ref[at, 0:tracks, 0:rows] = tiles[at].astype(out_ref.dtype)
        out_ref[at, 0:tracks, rows : 2 * rows] = edge.astype(out_ref.dtype)


def keyval_kernel(group_ref, mine_ref, theirs_ref, gain_ref, kv_ref, tok_ref, normed_ref, keyval_ref):
    width = mine_ref.shape[1]
    group = group_ref[0]
    tok_ref[:, pl.ds(pl.multiple_of(group * width, width), width)] = mine_ref[...]
    tok_ref[:, pl.ds(pl.multiple_of((1 - group) * width, width), width)] = theirs_ref[...]
    tok_f = tok_ref[...].astype(jnp.float32)
    inverse = lax.rsqrt(jnp.mean(tok_f * tok_f, axis=-1, keepdims=True) + 1e-06)
    normed = (tok_f * inverse * gain_ref[...]).astype(jnp.bfloat16)
    normed_ref[...] = normed
    keyval_ref[...] = lax.dot_general(
        normed, kv_ref[...], (((1,), (1,)), ((), ())), preferred_element_type=jnp.float32
    ).astype(jnp.bfloat16)


def sweep(turns, step, body, carry):
    if turns <= 4:
        for turn in range(turns):
            carry = body(turn * step, carry)
        return carry
    return lax.fori_loop(
        0, turns, lambda turn, held: body(pl.multiple_of(turn * step, step), held), carry
    )


def query_kernel(normed_ref, weight_ref, out_ref):
    rows = normed_ref.shape[0]
    query = jnp.dot(normed_ref[...], weight_ref[...], preferred_element_type=jnp.float32).astype(
        jnp.bfloat16
    )
    for h in range(HEADS):
        out_ref[h * rows : (h + 1) * rows, :] = query[:, h * QK : (h + 1) * QK]


def attention_kernel(row_block, key_block, pieces, first, last, query_ref, *refs):
    kv_refs, refs = refs[:pieces], refs[pieces:]
    if not first:
        old_top_ref, old_weighted_ref = refs[:2]
        refs = refs[2:]
    if last:
        tok_ref, outw_ref, out_ref, k_s, v_s, s_s = refs
        token_rows = tok_ref.shape[0]
        total = tok_ref[...].astype(jnp.float32)
    else:
        top_ref, weighted_ref, k_s, v_s, s_s = refs
    at = 0
    for ref in kv_refs:
        count = ref.shape[0]
        k_s[at : at + count, :] = ref[:, :QK]
        v_s[at : at + count, 0:VDIM] = ref[:, QK:]
        at += count
    key_block = min(key_block, at)
    v_s[:, VDIM:] = jnp.ones((at, v_s.shape[1] - VDIM), jnp.bfloat16)
    scale = QK ** (-0.5) / math.log(2.0)
    for r in range(0, query_ref.shape[0], row_block):
        rows = query_ref[r : r + row_block, :]
        slot = (r // row_block) % 2

        def score(k, top):
            scores = lax.dot_general(
                rows,
                k_s[pl.ds(k, key_block), :],
                (((1,), (1,)), ((), ())),
                preferred_element_type=jnp.float32,
            )
            s_s[slot, :, pl.ds(k, key_block)] = scores
            return jnp.maximum(top, jnp.max(scores, axis=1, keepdims=True))

        def weigh(k, weighted):
            shifted = s_s[slot, :, pl.ds(k, key_block)] - top
            expw = jnp.exp2(shifted * scale).astype(jnp.bfloat16)
            return weighted + jnp.dot(
                expw, v_s[pl.ds(k, key_block), :], preferred_element_type=jnp.float32
            )

        if first:
            old_top = jnp.full((row_block, 1), -jnp.inf, jnp.float32)
            start = jnp.zeros((row_block, v_s.shape[1]), jnp.float32)
        else:
            old_top = old_top_ref[r : r + row_block, 0:1]
        top = sweep(at // key_block, key_block, score, old_top)
        if not first:
            start = old_weighted_ref[r : r + row_block, :] * jnp.exp2((old_top - top) * scale)
        weighted = sweep(at // key_block, key_block, weigh, start)
        if last:
            context = (weighted[:, :VDIM] / weighted[:, VDIM : VDIM + 1]).astype(jnp.bfloat16)
            for j in range(row_block // token_rows):
                h = r // token_rows + j
                total = total + jnp.dot(
                    context[j * token_rows : (j + 1) * token_rows],
                    outw_ref[h * VDIM : (h + 1) * VDIM, :],
                    preferred_element_type=jnp.float32,
                )
        else:
            top_ref[r : r + row_block, :] = jnp.broadcast_to(top, (row_block, top_ref.shape[1]))
            weighted_ref[r : r + row_block, :] = weighted
    if last:
        out_ref[...] = total.astype(jnp.bfloat16)


def decoder_kernel(extra, tok_ref, grads_ref, chosen_ref, tracks_ref, taps_ref, skip_ref, sums_ref):
    token_rows = tok_ref.shape[0]
    width = tracks_ref.shape[1]
    root = math.sqrt(2.0 / math.pi)
    masked = lax.dot_general(
        grads_ref[...],
        chosen_ref[...],
        (((0,), (0,)), ((), ())),
        preferred_element_type=jnp.float32,
    )[: token_rows + 2 * SPAN]
    column = lax.broadcasted_iota(jnp.int32, masked.shape, 1) % extra
    for side in range(2):
        at = side * width
        ours = (column < extra // 2) if side == 0 else (column >= extra // 2)
        rows = jnp.where(ours, masked, 0.0).astype(jnp.bfloat16)
        head = (
            jnp.dot(rows, tracks_ref[...], preferred_element_type=jnp.float32)
            .astype(jnp.bfloat16)
            .astype(jnp.float32)
        )
        own, later, earlier = (
            head[:token_rows],
            head[token_rows : token_rows + SPAN],
            head[token_rows + SPAN :],
        )
        shifted_rows = (
            jnp.concatenate([own[SPAN:], later], axis=0),
            own,
            jnp.concatenate([earlier, own[:-SPAN]], axis=0),
        )
        tok = tok_ref[:, at : at + width].astype(jnp.float32)
        square = tok * tok
        curve = jnp.tanh(root * (tok + 0.044715 * square * tok))
        gate = 0.5 * (1.0 + curve)
        act = tok * gate
        slope = gate + 0.5 * tok * (1.0 - curve * curve) * (root * (1.0 + 3 * 0.044715 * square))
        convback = jnp.zeros_like(tok)
        for tap, shifted in enumerate(shifted_rows):
            convback = convback + taps_ref[tap : tap + 1, at : at + width] * shifted
            sums_ref[tap : tap + 1, at : at + width] = jnp.sum(act * shifted, axis=0, keepdims=True)
        skip_ref[:, at : at + width] = (slope * convback).astype(jnp.bfloat16)


def call(body, out, specs, scratch=(), limit=32, name=None):
    return pl.pallas_call(
        body,
        out_shape=out,
        in_specs=specs,
        out_specs=jax.tree.map(lambda _: VMEM, out),
        scratch_shapes=list(scratch),
        compiler_params=pltpu.CompilerParams(vmem_limit_bytes=limit * MIB),
        name=name,
    )


def shards(
    enc_input,
    enc_weight,
    norm_gain,
    q_weight,
    kv_weight,
    out_weight,
    dec_weight,
    track_weight,
    track_grad,
    track_index,
    track_mask,
):
    chips = lax.axis_size("chip")
    count = 2 * chips
    pair = chips // 2
    token_rows = enc_input.shape[0] // 2
    rows, dim = enc_weight.shape
    width = dim // 2
    tracks = track_weight.shape[0]
    extra = 2 * tracks
    group = lax.axis_index("groups")
    me = lax.axis_index("chip") * 2 + lax.axis_index("core")
    shape = lambda *dims, kind=jnp.bfloat16: jax.ShapeDtypeStruct(dims, kind)
    direct = pair <= 4 and pair & (pair - 1) == 0 and rows % 16 == 0

    own_half = lax.dynamic_slice_in_dim(enc_weight, group * width, width, axis=1)
    packed = jnp.concatenate([own_half, track_weight[:, :width], track_weight[:, width:]], axis=0)
    if direct:
        lanes = {0: packed}
        for mask in range(1, pair):
            lanes[mask] = chip_swap(after(packed, lanes[1]) if mask == 3 else packed, 2 * mask)
        grads = after(track_grad, lanes[1]) if pair > 1 else track_grad
    else:
        grads = track_grad
    partner_input = group_swap(enc_input)

    lines = -(-tracks // 16) * 16
    windows = call(windows_kernel, shape(count, lines, 2 * token_rows), [VMEM], name="windows")(
        grads.T
    )
    exchanged = lax.all_to_all(windows, ("chip", "core"), 0, 0, tiled=True)
    slots = jnp.pad(
        track_index.reshape(count, tracks), ((0, 0), (0, lines - tracks)), constant_values=-1
    )
    measured = jnp.pad(track_mask.reshape(count, tracks), ((0, 0), (0, lines - tracks)))
    columns = jnp.arange(count * extra, dtype=jnp.int32)
    column_tracks = columns // extra * tracks + columns % tracks
    chosen = jnp.where(
        slots.reshape(-1, 1) == column_tracks[None, :],
        measured.reshape(-1, 1).astype(jnp.bfloat16),
        0,
    ).astype(jnp.bfloat16)

    if direct:
        blocks = []
        for mask in range(pair):
            near = lanes[mask]
            far = chip_swap(after(near, exchanged) if mask == 2 else near, 1)
            blocks += [
                (4 * mask, near),
                (4 * mask + 1, core_swap(near)),
                (4 * mask + 2, far),
                (4 * mask + 3, core_swap(far)),
            ]
        ids = me ^ jnp.array([mask for mask, _ in blocks], jnp.int32)
        mine, partner, track_rows = call(
            functools.partial(tokens_kernel, rows, extra),
            (
                shape(token_rows, width),
                shape(token_rows, width),
                shape(count * extra, width),
            ),
            [SMEM, VMEM, VMEM] + [ANY] * count,
            scratch=(
                pltpu.VMEM((2 * token_rows, count * rows), jnp.bfloat16),
                pltpu.VMEM((count * rows, width), jnp.bfloat16),
                pltpu.SemaphoreType.DMA((count, 2)),
            ),
            name="tokens",
        )(ids, enc_input, partner_input, *[block for _, block in blocks])
    else:
        gathered = lax.all_gather(packed, ("chip", "core"), axis=0)
        track_rows = gathered[:, rows:].reshape(count * extra, width)
        weight = gathered[:, :rows].reshape(count * rows, width)
        mine, partner = (
            jnp.dot(
                cells.reshape(token_rows, count * rows), weight, preferred_element_type=jnp.float32
            ).astype(jnp.bfloat16)
            for cells in (enc_input, partner_input)
        )
    theirs = group_swap(partner)
    tokens, normed, keyval = call(
        keyval_kernel,
        (shape(token_rows, dim), shape(token_rows, dim), shape(token_rows, QK + VDIM)),
        [SMEM] + [VMEM] * 4,
        name="keyval",
    )(group.reshape(1), mine, theirs, norm_gain.reshape(1, dim), kv_weight.T)

    if direct:
        early, late = [], []
        for mask in range(pair):
            near = chip_swap(keyval, 2 * mask) if mask else keyval
            far = chip_swap(near, 1)
            side = early if mask < max(1, pair // 2) else late
            side += [near, far, core_swap(near), core_swap(far)]
        stages = [side for side in (early, late) if side]
    else:
        stages = [[lax.all_gather(keyval, ("chip", "core"), axis=0, tiled=True)]]

    query = call(query_kernel, shape(HEADS * token_rows, QK), [VMEM] * 2, name="query")(
        normed, q_weight
    )
    skip_grad, sums = call(
        functools.partial(decoder_kernel, extra),
        (shape(token_rows, dim), shape(3, dim, kind=jnp.float32)),
        [VMEM] * 5,
        name="decoder",
    )(tokens, exchanged.reshape(count * lines, 2 * token_rows), chosen, track_rows, dec_weight)
    sums = sums + core_swap(sums)
    step = 1
    while step < chips:
        sums = sums + chip_swap(sums, step)
        step *= 2
    dec_weight_grad = sums / jnp.float32(math.sqrt(token_rows * count))

    row_block = 2 * token_rows if direct else token_rows
    state = []
    for turn, pieces in enumerate(stages):
        last = turn + 1 == len(stages)
        keys = sum(piece.shape[0] for piece in pieces)
        extras = [tokens, out_weight] if last else []
        held = (
            shape(token_rows, dim)
            if last
            else (
                shape(HEADS * token_rows, 128, kind=jnp.float32),
                shape(HEADS * token_rows, 256, kind=jnp.float32),
            )
        )
        state = call(
            functools.partial(attention_kernel, row_block, 512, len(pieces), turn == 0, last),
            held,
            [VMEM] * (1 + len(pieces) + len(state) + len(extras)),
            scratch=(
                pltpu.VMEM((keys, QK), jnp.bfloat16),
                pltpu.VMEM((keys, 256), jnp.bfloat16),
                pltpu.VMEM((2, row_block, keys), jnp.float32),
            ),
            limit=60 if len(stages) == 1 else 40,
            name="attention",
        )(query, *pieces, *state, *extras)
    return (state, skip_grad, dec_weight_grad)


def solution(mesh):
    groups, count = mesh.devices.shape
    inner = Mesh(mesh.devices.reshape(groups, count // 2, 2), ("groups", "chip", "core"))
    seq = ("chip", "core")
    every = ("groups", "chip", "core")
    return jax.shard_map(
        shards,
        mesh=inner,
        in_specs=(
            P(every, None),
            P(seq, None),
            P(),
            P(),
            P(),
            P(),
            P(),
            P(seq, None),
            P("groups", seq),
            P("groups"),
            P("groups"),
        ),
        out_specs=(P(every, None), P(every, None), P("groups", None)),
        check_vma=False,
    )
```

time: 275 us -> 117 us (0.43)
  blocking collectives: 89.3 us -> 0 us
  matrix products: 72.9 us -> 0 us
  starting transfers between devices: 11.6 us -> 37.9 us
  local copies, waits for them, and re-layouts: 33.7 us -> 8.28 us
  waiting for transfers between devices: 26.8 us -> 51.7 us
  other arithmetic: 24.2 us -> 1.5 us
  Pallas kernels: 0 us -> 15.9 us
  between operations: 14.2 us -> 0.97 us
    dot_general x37 -> x0, matrix products: 72.9 us -> none  [the longest x16 39.6 us: block_update(): jnp.dot(expw.astype(jnp.bfloat16), key_block[:, QK:], preferred_element_t...]
    psum x1 -> x0, blocking collectives: 59.2 us -> none  [decoder_back(): summed = lax.psum(jnp.stack(tap_terms, axis=0), 'seq')]
    ppermute x2 -> x36, waiting for transfers between devices: 0.01 us -> 45.4 us  [the longest x17 38.4 us: chip_swap(): return lax.ppermute(cells, 'chip', [(i, i ^ mask) for i in range(count)])]
    all_gather x1 -> x0, blocking collectives: 30.1 us -> none  [decoder_back(): every_row = lax.all_gather(track_weight, 'seq', axis=0, tiled=True)]
    all_gather x2 -> x0, waiting for transfers between devices: 26.1 us -> none  [the longest x1 26.1 us: shards(): lax.all_gather(enc_weight, 'seq', axis=0, tiled=True)]
    ppermute x2 -> x36, starting transfers between devices: 4.09 us -> 26.9 us  [the longest x17 21.6 us: chip_swap(): return lax.ppermute(cells, 'chip', [(i, i ^ mask) for i in range(count)])]
    reduce_sum x16 -> x0, other arithmetic: 18.2 us -> none  [block_update(): running_sum = running_sum * shrink + jnp.sum(expw, axis=1)]
    pallas_call x0 -> x7, Pallas kernels: none -> 15.9 us  [the longest x2 7.45 us: shards(): call(functools.partial(attention_kernel, row_block, 512, len(pieces), tur...]
  transfers between devices with their start and end apart: 5 -> 37, of which waited for: 1 -> 12; matrix products, arithmetic and copies ran while one was open for 8% -> 3% of each run, Pallas kernels for 0% -> 3%
where the time goes in v1:
time: 117 us; the launch traced here: 116 us
  waiting for transfers between devices  51.7 us (44%)
  starting transfers between devices  37.9 us (32%)
  Pallas kernels  15.9 us (14%)
  local copies, waits for them, and re-layouts  8.28 us (7%)
  other arithmetic  1.5 us (1%)
    ppermute x17, waiting for transfers between devices, chip_swap(): return lax.ppermute(cells, 'chip', [(i, i ^ mask) for i in range(count)])  38.4 us
    ppermute x17, starting transfers between devices, chip_swap(): return lax.ppermute(cells, 'chip', [(i, i ^ mask) for i in range(count)])  21.6 us
    all_to_all x1, starting transfers between devices, shards(): exchanged = lax.all_to_all(windows, ('chip', 'core'), 0, 0, tiled=True)  11 us
    pallas_call x2, Pallas kernels, shards(): call(functools.partial(attention_kernel, row_block, 512, len(pieces), tur...  7.45 us
    all_to_all x1, waiting for transfers between devices, shards(): exchanged = lax.all_to_all(windows, ('chip', 'core'), 0, 0, tiled=True)  6.37 us
    ppermute x2, waiting for transfers between devices, group_swap(): return lax.ppermute(cells, 'groups', [(0, 1), (1, 0)])  5.68 us
    unnamed x24, local copies, waits for them, and re-layouts  5.67 us
    pallas_call x1, Pallas kernels, shards(): call(functools.partial(tokens_kernel, rows, extra), (shape(token_rows, wi...  4.58 us
  transfers between devices with their start and end apart: 37, of which 12 were waited for; matrix products, arithmetic and copies ran while one was open for 3% of the time, Pallas kernels for 3%

profile of v1, /device:TPU:0, one launch (start us, length us, event | category | flops | bytes accessed | tf_op | source)
XLA Modules:
  0.0 116.3 jit_solution(4046983277984823063)
XLA Ops:
  1.8 3.1 %collective-permute-start.4 = (bf16[200,768]{1,0:T(8,128)(2,1)S(1)}, bf16[200,768]{1,0:T(8,128)(2,1)S(1)}, u32[]{:S(2)}, u32[]{:S(2)}) collective-permute-start(bf16[200,768]{1,0:T(8,128)(2,1)S(1)} %pad_maximum_fusion.refs_0_), channel_id=1, source_target_pairs={{0,4},{2,6},{4,0},{6,2},{8,12},{10,14},{12,8},{14,10},{1,5},{3,7},... | collective-permute-start | bytes 921608 | tf_op jit(solution)/shard_map/ppermute | solution.py:23
  4.9 2.6 %collective-permute-start.8 = (bf16[200,768]{1,0:T(8,128)(2,1)S(1)}, bf16[200,768]{1,0:T(8,128)(2,1)S(1)}, u32[]{:S(2)}, u32[]{:S(2)}) collective-permute-start(bf16[200,768]{1,0:T(8,128)(2,1)S(1)} %pad_maximum_fusion.refs_0_), channel_id=1, source_target_pairs={{0,8},{2,10},{4,12},{6,14},{8,0},{10,2},{12,4},{14,6},{1,9},{3,11}... | collective-permute-start | bytes 921608 | tf_op jit(solution)/shard_map/ppermute | solution.py:23
  7.5 1.5 %collective-permute-start.2 = (bf16[200,768]{1,0:T(8,128)(2,1)S(1)}, bf16[200,768]{1,0:T(8,128)(2,1)}, u32[]{:S(2)}, u32[]{:S(2)}) collective-permute-start(bf16[200,768]{1,0:T(8,128)(2,1)S(1)} %pad_maximum_fusion.refs_0_), channel_id=1, source_target_pairs={{0,2},{2,0},{4,6},{6,4},{8,10},{10,8},{12,14},{14,12},{1,3},{3,1},... | collective-permute-start | bytes 921608 | tf_op jit(solution)/shard_map/ppermute | solution.py:23
  9.0 9.6 %collective-permute-done.4.refs_4_ = bf16[200,768]{1,0:T(8,128)(2,1)S(1)} collective-permute-done((bf16[200,768]{1,0:T(8,128)(2,1)S(1)}, bf16[200,768]{1,0:T(8,128)(2,1)S(1)}, u32[]{:S(2)}, u32[]{:S(2)}) %collective-permute-start.4) | collective-permute-done | bytes 307232 | tf_op jit(solution)/shard_map/ppermute | solution.py:23
  18.6 2.6 %collective-permute-start.12 = (bf16[200,768]{1,0:T(8,128)(2,1)S(1)}, bf16[200,768]{1,0:T(8,128)(2,1)}, u32[]{:S(2)}, u32[]{:S(2)}) collective-permute-start(bf16[200,768]{1,0:T(8,128)(2,1)S(1)} %pad_maximum_fusion.refs_0_), channel_id=1, source_target_pairs={{0,12},{2,14},{4,8},{6,10},{8,4},{10,6},{12,0},{14,2},{1,13},{3,15... | collective-permute-start | bytes 921608 | tf_op jit(solution)/shard_map/ppermute | solution.py:23
  21.2 1.5 %collective-permute-start.6 = (bf16[200,768]{1,0:T(8,128)(2,1)S(1)}, bf16[200,768]{1,0:T(8,128)(2,1)}, u32[]{:S(2)}, u32[]{:S(2)}) collective-permute-start(bf16[200,768]{1,0:T(8,128)(2,1)S(1)} %collective-permute-done.4.refs_4_), channel_id=1, source_target_pairs={{0,2},{2,0},{4,6},{6,4},{8,10},{10,8},{12,14},{14,12},{1,3},{3,1},... | collective-permute-start | bytes 921608 | tf_op jit(solution)/shard_map/ppermute | solution.py:23
  24.4 11.0 %all-to-all-start = ((bf16[16,16,256]{2,1,0:T(8,128)(2,1)}), bf16[16,16,256]{2,1,0:T(8,128)(2,1)S(1)}, u32[]{:S(2)}, u32[]{:S(2)}) async-start(bf16[16,16,256]{2,1,0:T(8,128)(2,1)} %windows.1), calls=%async_computation | async-start | bytes 262144 | tf_op jit(solution)/shard_map/all_to_all | solution.py:281
  35.4 1.6 %collective-permute-start = (bf16[256,1408]{1,0:T(8,128)(2,1)}, bf16[256,1408]{1,0:T(8,128)(2,1)S(1)}, u32[]{:S(2)}, u32[]{:S(2)}) collective-permute-start(bf16[256,1408]{1,0:T(8,128)(2,1)} %own_ref.1), channel_id=1, source_target_pairs={{0,16},{16,0},{1,17},{17,1},{2,18},{18,2},{3,19},{19,3},{4,20},{20... | collective-permute-start | bytes 2162696 | tf_op jit(solution)/shard_map/ppermute | solution.py:31
  37.0 6.4 %all-to-all-done = bf16[16,16,256]{2,1,0:T(8,128)(2,1)S(1)} async-done(((bf16[16,16,256]{2,1,0:T(8,128)(2,1)}), bf16[16,16,256]{2,1,0:T(8,128)(2,1)S(1)}, u32[]{:S(2)}, u32[]{:S(2)}) %all-to-all-start) | async-done | bytes 131104 | tf_op jit(solution)/shard_map/all_to_all | solution.py:281
  43.9 2.0 %collective-permute-start.14 = (bf16[200,768]{1,0:T(8,128)(2,1)}, bf16[200,768]{1,0:T(8,128)(2,1)}, u32[]{:S(2)}, u32[]{:S(2)}) collective-permute-start(bf16[200,768]{1,0:T(8,128)(2,1)} %collective-permute-done.12.refs_12_), channel_id=1, source_target_pairs={{0,2},{2,0},{4,6},{6,4},{8,10},{10,8},{12,14},{14,12},{1,3},{3,1},... | collective-permute-start | bytes 921608 | tf_op jit(solution)/shard_map/ppermute | solution.py:23
  47.8 6.2 %collective-permute-done.10.refs_10_ = bf16[200,768]{1,0:T(8,128)(2,1)} collective-permute-done((bf16[200,768]{1,0:T(8,128)(2,1)S(1)}, bf16[200,768]{1,0:T(8,128)(2,1)}, u32[]{:S(2)}, u32[]{:S(2)}) %collective-permute-start.10) | collective-permute-done | bytes 307232 | tf_op jit(solution)/shard_map/ppermute | solution.py:23
  54.1 5.7 %collective-permute-done.14.refs_14_ = bf16[200,768]{1,0:T(8,128)(2,1)} collective-permute-done((bf16[200,768]{1,0:T(8,128)(2,1)}, bf16[200,768]{1,0:T(8,128)(2,1)}, u32[]{:S(2)}, u32[]{:S(2)}) %collective-permute-start.14) | collective-permute-done | bytes 307232 | tf_op jit(solution)/shard_map/ppermute | solution.py:23
  62.3 1.3 %copy-done.3 = bf16[256,1408]{1,0:T(8,128)(2,1)S(1)} copy-done((bf16[256,1408]{1,0:T(8,128)(2,1)S(1)}, bf16[256,1408]{1,0:T(8,128)(2,1)}, u32[]{:S(2)}) %copy-start.3) | copy-done | bytes 720920
  63.6 1.0 copy-done.5
  64.6 1.0 copy-done.7
  65.5 4.6 %tokens.1 = (bf16[128,768]{1,0:T(8,128)(2,1)S(1)}, bf16[128,768]{1,0:T(8,128)(2,1)S(1)}, bf16[384,768]{1,0:T(8,128)(2,1)S(1)}) custom-call(s32[16]{0:T(128)S(1)} %iota_xor_fusion.ids_ref, bf16[256,1408]{1,0:T(8,128)(2,1)S(1)} %copy-done.3, bf16[256,1408]{1,0:T(8,128)(2,1)S(1)} %collective-permute-done.partner_ref, ...), custom_call_target="tpu_custom_call" | custom-call | tf_op jit(solution)/shard_map/tokens/pallas_call | solution.py:306
  70.1 1.6 %collective-permute-start.16 = (bf16[128,768]{1,0:T(8,128)(2,1)S(1)}, bf16[128,768]{1,0:T(8,128)(2,1)S(1)}, u32[]{:S(2)}, u32[]{:S(2)}) collective-permute-start(bf16[128,768]{1,0:T(8,128)(2,1)S(1)} %get-tuple-element.20), channel_id=1, source_target_pairs={{0,16},{16,0},{1,17},{17,1},{2,18},{18,2},{3,19},{19,3},{4,20},{20... | collective-permute-start | bytes 589832 | tf_op jit(solution)/shard_map/ppermute | solution.py:31
  71.8 5.7 %collective-permute-done.16.theirs_ref = bf16[128,768]{1,0:T(8,128)(2,1)S(1)} collective-permute-done((bf16[128,768]{1,0:T(8,128)(2,1)S(1)}, bf16[128,768]{1,0:T(8,128)(2,1)S(1)}, u32[]{:S(2)}, u32[]{:S(2)}) %collective-permute-start.16) | collective-permute-done | bytes 196640 | tf_op jit(solution)/shard_map/ppermute | solution.py:31
  78.1 2.0 %decoder.1 = (bf16[128,1536]{1,0:T(8,128)(2,1)}, f32[3,1536]{1,0:T(4,128)S(1)}) custom-call(bf16[128,1536]{1,0:T(8,128)(2,1)S(1)} %get-tuple-element.25.refs_10_.tok_ref, bf16[256,256]{1,0:T(8,128)(2,1)S(1)} %bitcast.7, bf16[256,384]{1,0:T(8,128)(2,1)S(1)} %compare_select_fusion.chosen_ref, bf16[384,768]{1,0:T(8,128)(2,1)S(1)} %get-tuple-element.26.tracks_ref, ...), custom_call_target="tpu_custom_call" | custom-call | tf_op jit(solution)/shard_map/decoder/pallas_call | solution.py:353
  80.0 1.2 %collective-permute-done.32 = f32[3,1536]{1,0:T(4,128)S(1)} collective-permute-done((f32[3,1536]{1,0:T(4,128)S(1)}, f32[3,1536]{1,0:T(4,128)S(1)}, u32[]{:S(2)}, u32[]{:S(2)}) %collective-permute-start.32) | collective-permute-done | bytes 18464 | tf_op jit(solution)/shard_map/ppermute | solution.py:27
  81.6 3.5 %collective-permute-done.33 = f32[3,1536]{1,0:T(4,128)S(1)} collective-permute-done((f32[3,1536]{1,0:T(4,128)S(1)}, f32[3,1536]{1,0:T(4,128)S(1)}, u32[]{:S(2)}, u32[]{:S(2)}) %collective-permute-start.33) | collective-permute-done | bytes 18464 | tf_op jit(solution)/shard_map/ppermute | solution.py:23
  85.2 3.8 %collective-permute-done.34 = f32[3,1536]{1,0:T(4,128)S(1)} collective-permute-done((f32[3,1536]{1,0:T(4,128)S(1)}, f32[3,1536]{1,0:T(4,128)S(1)}, u32[]{:S(2)}, u32[]{:S(2)}) %collective-permute-start.34) | collective-permute-done | bytes 18464 | tf_op jit(solution)/shard_map/ppermute | solution.py:23
  89.6 1.0 collective-permute-start.28
  91.3 1.5 %collective-permute-start.17 = (bf16[128,320]{1,0:T(8,128)(2,1)S(1)}, bf16[128,320]{1,0:T(8,128)(2,1)S(1)}, u32[]{:S(2)}, u32[]{:S(2)}) collective-permute-start(bf16[128,320]{1,0:T(8,128)(2,1)S(1)} %get-tuple-element.22.refs_0_), channel_id=1, source_target_pairs={{0,8},{2,10},{4,12},{6,14},{8,0},{10,2},{12,4},{14,6},{1,9},{3,11}... | collective-permute-start | bytes 245768 | tf_op jit(solution)/shard_map/ppermute | solution.py:23
  92.8 1.2 %collective-permute-done.35 = f32[3,1536]{1,0:T(4,128)S(1)} collective-permute-done((f32[3,1536]{1,0:T(4,128)S(1)}, f32[3,1536]{1,0:T(4,128)S(1)}, u32[]{:S(2)}, u32[]{:S(2)}) %collective-permute-start.35) | collective-permute-done | bytes 18464 | tf_op jit(solution)/shard_map/ppermute | solution.py:23
  94.7 1.3 %collective-permute-start.29 = (bf16[128,320]{1,0:T(8,128)(2,1)S(1)}, bf16[128,320]{1,0:T(8,128)(2,1)S(1)}, u32[]{:S(2)}, u32[]{:S(2)}) collective-permute-start(bf16[128,320]{1,0:T(8,128)(2,1)S(1)} %collective-permute-done.28.refs_4_), channel_id=1, source_target_pairs={{0,2},{2,0},{4,6},{6,4},{8,10},{10,8},{12,14},{14,12},{1,3},{3,1},... | collective-permute-start | bytes 245768 | tf_op jit(solution)/shard_map/ppermute | solution.py:23
  96.5 5.5 %collective-permute-done.17.refs_0_ = bf16[128,320]{1,0:T(8,128)(2,1)S(1)} collective-permute-done((bf16[128,320]{1,0:T(8,128)(2,1)S(1)}, bf16[128,320]{1,0:T(8,128)(2,1)S(1)}, u32[]{:S(2)}, u32[]{:S(2)}) %collective-permute-start.17) | collective-permute-done | bytes 81952 | tf_op jit(solution)/shard_map/ppermute | solution.py:23
  102.0 1.3 %collective-permute-start.18 = (bf16[128,320]{1,0:T(8,128)(2,1)S(1)}, bf16[128,320]{1,0:T(8,128)(2,1)S(1)}, u32[]{:S(2)}, u32[]{:S(2)}) collective-permute-start(bf16[128,320]{1,0:T(8,128)(2,1)S(1)} %collective-permute-done.17.refs_0_), channel_id=1, source_target_pairs={{0,2},{2,0},{4,6},{6,4},{8,10},{10,8},{12,14},{14,12},{1,3},{3,1},... | collective-permute-start | bytes 245768 | tf_op jit(solution)/shard_map/ppermute | solution.py:23
  105.3 1.8 %collective-permute-done.18.refs_1_ = bf16[128,320]{1,0:T(8,128)(2,1)S(1)} collective-permute-done((bf16[128,320]{1,0:T(8,128)(2,1)S(1)}, bf16[128,320]{1,0:T(8,128)(2,1)S(1)}, u32[]{:S(2)}, u32[]{:S(2)}) %collective-permute-start.18) | collective-permute-done | bytes 81952 | tf_op jit(solution)/shard_map/ppermute | solution.py:23
  107.1 1.1 collective-permute-done.22.refs_5_
  108.8 1.8 %attention.2 = (f32[1024,128]{1,0:T(8,128)S(1)}, f32[1024,256]{1,0:T(8,128)S(1)}) custom-call(bf16[1024,128]{1,0:T(8,128)(2,1)S(1)} %query.1.query_ref, bf16[128,320]{1,0:T(8,128)(2,1)S(1)} %get-tuple-element.22.refs_0_, bf16[128,320]{1,0:T(8,128)(2,1)S(1)} %collective-permute-done.25.refs_1_, bf16[128,320]{1,0:T(8,128)(2,1)S(1)} %collective-permute-done.26.refs_2_, ...), custom_call_target="tpu_custom_call" | custom-call | tf_op jit(solution)/shard_map/attention/pallas_call | solution.py:380
  110.6 5.7 %attention.3 = bf16[128,1536]{1,0:T(8,128)(2,1)} custom-call(bf16[1024,128]{1,0:T(8,128)(2,1)S(1)} %query.1.query_ref, bf16[128,320]{1,0:T(8,128)(2,1)S(1)} %collective-permute-done.17.refs_0_, bf16[128,320]{1,0:T(8,128)(2,1)S(1)} %collective-permute-done.18.refs_1_, bf16[128,320]{1,0:T(8,128)(2,1)S(1)} %collective-permute-done.19.refs_2_, ...), custom_call_target="tpu_custom_call" | custom-call | tf_op jit(solution)/shard_map/attention/pallas_call | solution.py:380
  (92 shorter events, 13.9 us)
Async XLA Ops:
  1.8 16.8 %collective-permute-start.4 = (bf16[200,768]{1,0:T(8,128)(2,1)S(1)}, bf16[200,768]{1,0:T(8,128)(2,1)S(1)}, u32[]{:S(2)}, u32[]{:S(2)}) collective-permute-start(bf16[200,768]{1,0:T(8,128)(2,1)S(1)} %pad_maximum_fusion.refs_0_), channel_id=1, source_target_pairs={{0,4},{2,6},{4,0},{6,2},{8,12},{10,14},{12,8},{14,10},{1,5},{3,7},... | collective-permute-start | bytes 921608 | tf_op jit(solution)/shard_map/ppermute | solution.py:23
  4.9 17.9 %collective-permute-start.8 = (bf16[200,768]{1,0:T(8,128)(2,1)S(1)}, bf16[200,768]{1,0:T(8,128)(2,1)S(1)}, u32[]{:S(2)}, u32[]{:S(2)}) collective-permute-start(bf16[200,768]{1,0:T(8,128)(2,1)S(1)} %pad_maximum_fusion.refs_0_), channel_id=1, source_target_pairs={{0,8},{2,10},{4,12},{6,14},{8,0},{10,2},{12,4},{14,6},{1,9},{3,11}... | collective-permute-start | bytes 921608 | tf_op jit(solution)/shard_map/ppermute | solution.py:23
  7.5 28.0 %collective-permute-start.2 = (bf16[200,768]{1,0:T(8,128)(2,1)S(1)}, bf16[200,768]{1,0:T(8,128)(2,1)}, u32[]{:S(2)}, u32[]{:S(2)}) collective-permute-start(bf16[200,768]{1,0:T(8,128)(2,1)S(1)} %pad_maximum_fusion.refs_0_), channel_id=1, source_target_pairs={{0,2},{2,0},{4,6},{6,4},{8,10},{10,8},{12,14},{14,12},{1,3},{3,1},... | collective-permute-start | bytes 921608 | tf_op jit(solution)/shard_map/ppermute | solution.py:23
  9.0 34.4 %collective-permute-start.1 = (bf16[200,768]{1,0:T(8,128)(2,1)S(1)}, bf16[200,768]{1,0:T(8,128)(2,1)}, u32[]{:S(2)}, u32[]{:S(2)}) collective-permute-start(bf16[200,768]{1,0:T(8,128)(2,1)S(1)} %pad_maximum_fusion.refs_0_), channel_id=1, source_target_pairs={{0,1},{1,0},{2,3},{3,2},{4,5},{5,4},{6,7},{7,6},{8,9},{9,8},{10,11... | collective-permute-start | bytes 921608 | tf_op jit(solution)/shard_map/ppermute | solution.py:27
  18.6 24.7 %collective-permute-start.12 = (bf16[200,768]{1,0:T(8,128)(2,1)S(1)}, bf16[200,768]{1,0:T(8,128)(2,1)}, u32[]{:S(2)}, u32[]{:S(2)}) collective-permute-start(bf16[200,768]{1,0:T(8,128)(2,1)S(1)} %pad_maximum_fusion.refs_0_), channel_id=1, source_target_pairs={{0,12},{2,14},{4,8},{6,10},{8,4},{10,6},{12,0},{14,2},{1,13},{3,15... | collective-permute-start | bytes 921608 | tf_op jit(solution)/shard_map/ppermute | solution.py:23
  21.2 22.6 %collective-permute-start.6 = (bf16[200,768]{1,0:T(8,128)(2,1)S(1)}, bf16[200,768]{1,0:T(8,128)(2,1)}, u32[]{:S(2)}, u32[]{:S(2)}) collective-permute-start(bf16[200,768]{1,0:T(8,128)(2,1)S(1)} %collective-permute-done.4.refs_4_), channel_id=1, source_target_pairs={{0,2},{2,0},{4,6},{6,4},{8,10},{10,8},{12,14},{14,12},{1,3},{3,1},... | collective-permute-start | bytes 921608 | tf_op jit(solution)/shard_map/ppermute | solution.py:23
  22.8 21.1 %collective-permute-start.5 = (bf16[200,768]{1,0:T(8,128)(2,1)S(1)}, bf16[200,768]{1,0:T(8,128)(2,1)}, u32[]{:S(2)}, u32[]{:S(2)}) collective-permute-start(bf16[200,768]{1,0:T(8,128)(2,1)S(1)} %collective-permute-done.4.refs_4_), channel_id=1, source_target_pairs={{0,1},{1,0},{2,3},{3,2},{4,5},{5,4},{6,7},{7,6},{8,9},{9,8},{10,11... | collective-permute-start | bytes 921608 | tf_op jit(solution)/shard_map/ppermute | solution.py:27
  24.4 19.0 %all-to-all-start = ((bf16[16,16,256]{2,1,0:T(8,128)(2,1)}), bf16[16,16,256]{2,1,0:T(8,128)(2,1)S(1)}, u32[]{:S(2)}, u32[]{:S(2)}) async-start(bf16[16,16,256]{2,1,0:T(8,128)(2,1)} %windows.1), calls=%async_computation | async-start | bytes 262144 | tf_op jit(solution)/shard_map/all_to_all | solution.py:281
  35.4 26.9 %collective-permute-start = (bf16[256,1408]{1,0:T(8,128)(2,1)}, bf16[256,1408]{1,0:T(8,128)(2,1)S(1)}, u32[]{:S(2)}, u32[]{:S(2)}) collective-permute-start(bf16[256,1408]{1,0:T(8,128)(2,1)} %own_ref.1), channel_id=1, source_target_pairs={{0,16},{16,0},{1,17},{17,1},{2,18},{18,2},{3,19},{19,3},{4,20},{20... | collective-permute-start | bytes 2162696 | tf_op jit(solution)/shard_map/ppermute | solution.py:31
  43.9 10.2 %collective-permute-start.10 = (bf16[200,768]{1,0:T(8,128)(2,1)S(1)}, bf16[200,768]{1,0:T(8,128)(2,1)}, u32[]{:S(2)}, u32[]{:S(2)}) collective-permute-start(bf16[200,768]{1,0:T(8,128)(2,1)S(1)} %collective-permute-done.8.refs_8_), channel_id=1, source_target_pairs={{0,2},{2,0},{4,6},{6,4},{8,10},{10,8},{12,14},{14,12},{1,3},{3,1},... | collective-permute-start | bytes 921608 | tf_op jit(solution)/shard_map/ppermute | solution.py:23
  43.9 15.9 %collective-permute-start.14 = (bf16[200,768]{1,0:T(8,128)(2,1)}, bf16[200,768]{1,0:T(8,128)(2,1)}, u32[]{:S(2)}, u32[]{:S(2)}) collective-permute-start(bf16[200,768]{1,0:T(8,128)(2,1)} %collective-permute-done.12.refs_12_), channel_id=1, source_target_pairs={{0,2},{2,0},{4,6},{6,4},{8,10},{10,8},{12,14},{14,12},{1,3},{3,1},... | collective-permute-start | bytes 921608 | tf_op jit(solution)/shard_map/ppermute | solution.py:23
  46.6 15.7 %collective-permute-start.13 = (bf16[200,768]{1,0:T(8,128)(2,1)}, bf16[200,768]{1,0:T(8,128)(2,1)}, u32[]{:S(2)}, u32[]{:S(2)}) collective-permute-start(bf16[200,768]{1,0:T(8,128)(2,1)} %collective-permute-done.12.refs_12_), channel_id=1, source_target_pairs={{0,1},{1,0},{2,3},{3,2},{4,5},{5,4},{6,7},{7,6},{8,9},{9,8},{10,11... | collective-permute-start | bytes 921608 | tf_op jit(solution)/shard_map/ppermute | solution.py:27
  47.3 15.0 %collective-permute-start.7 = (bf16[200,768]{1,0:T(8,128)(2,1)}, bf16[200,768]{1,0:T(8,128)(2,1)}, u32[]{:S(2)}, u32[]{:S(2)}) collective-permute-start(bf16[200,768]{1,0:T(8,128)(2,1)} %collective-permute-done.6.refs_6_), channel_id=1, source_target_pairs={{0,1},{1,0},{2,3},{3,2},{4,5},{5,4},{6,7},{7,6},{8,9},{9,8},{10,11... | collective-permute-start | bytes 921608 | tf_op jit(solution)/shard_map/ppermute | solution.py:27
  54.1 8.2 %collective-permute-start.11 = (bf16[200,768]{1,0:T(8,128)(2,1)}, bf16[200,768]{1,0:T(8,128)(2,1)}, u32[]{:S(2)}, u32[]{:S(2)}) collective-permute-start(bf16[200,768]{1,0:T(8,128)(2,1)} %collective-permute-done.10.refs_10_), channel_id=1, source_target_pairs={{0,1},{1,0},{2,3},{3,2},{4,5},{5,4},{6,7},{7,6},{8,9},{9,8},{10,11... | collective-permute-start | bytes 921608 | tf_op jit(solution)/shard_map/ppermute | solution.py:27
  70.1 7.4 %collective-permute-start.16 = (bf16[128,768]{1,0:T(8,128)(2,1)S(1)}, bf16[128,768]{1,0:T(8,128)(2,1)S(1)}, u32[]{:S(2)}, u32[]{:S(2)}) collective-permute-start(bf16[128,768]{1,0:T(8,128)(2,1)S(1)} %get-tuple-element.20), channel_id=1, source_target_pairs={{0,16},{16,0},{1,17},{17,1},{2,18},{18,2},{3,19},{19,3},{4,20},{20... | collective-permute-start | bytes 589832 | tf_op jit(solution)/shard_map/ppermute | solution.py:31
  81.3 3.9 %collective-permute-start.33 = (f32[3,1536]{1,0:T(4,128)S(1)}, f32[3,1536]{1,0:T(4,128)S(1)}, u32[]{:S(2)}, u32[]{:S(2)}) collective-permute-start(f32[3,1536]{1,0:T(4,128)S(1)} %add.48), channel_id=1, source_target_pairs={{0,2},{2,0},{4,6},{6,4},{8,10},{10,8},{12,14},{14,12},{1,3},{3,1},... | collective-permute-start | bytes 55304 | tf_op jit(solution)/shard_map/ppermute | solution.py:23
  85.2 3.9 %collective-permute-start.34 = (f32[3,1536]{1,0:T(4,128)S(1)}, f32[3,1536]{1,0:T(4,128)S(1)}, u32[]{:S(2)}, u32[]{:S(2)}) collective-permute-start(f32[3,1536]{1,0:T(4,128)S(1)} %add.49), channel_id=1, source_target_pairs={{0,4},{2,6},{4,0},{6,2},{8,12},{10,14},{12,8},{14,10},{1,5},{3,7},... | collective-permute-start | bytes 55304 | tf_op jit(solution)/shard_map/ppermute | solution.py:23
  89.1 4.9 %collective-permute-start.35 = (f32[3,1536]{1,0:T(4,128)S(1)}, f32[3,1536]{1,0:T(4,128)S(1)}, u32[]{:S(2)}, u32[]{:S(2)}) collective-permute-start(f32[3,1536]{1,0:T(4,128)S(1)} %add.50), channel_id=1, source_target_pairs={{0,8},{2,10},{4,12},{6,14},{8,0},{10,2},{12,4},{14,6},{1,9},{3,11}... | collective-permute-start | bytes 55304 | tf_op jit(solution)/shard_map/ppermute | solution.py:23
  89.6 5.1 %collective-permute-start.28 = (bf16[128,320]{1,0:T(8,128)(2,1)S(1)}, bf16[128,320]{1,0:T(8,128)(2,1)S(1)}, u32[]{:S(2)}, u32[]{:S(2)}) collective-permute-start(bf16[128,320]{1,0:T(8,128)(2,1)S(1)} %get-tuple-element.22.refs_0_), channel_id=1, source_target_pairs={{0,4},{2,6},{4,0},{6,2},{8,12},{10,14},{12,8},{14,10},{1,5},{3,7},... | collective-permute-start | bytes 245768 | tf_op jit(solution)/shard_map/ppermute | solution.py:23
  90.5 5.5 %collective-permute-start.25 = (bf16[128,320]{1,0:T(8,128)(2,1)S(1)}, bf16[128,320]{1,0:T(8,128)(2,1)S(1)}, u32[]{:S(2)}, u32[]{:S(2)}) collective-permute-start(bf16[128,320]{1,0:T(8,128)(2,1)S(1)} %get-tuple-element.22.refs_0_), channel_id=1, source_target_pairs={{0,2},{2,0},{4,6},{6,4},{8,10},{10,8},{12,14},{14,12},{1,3},{3,1},... | collective-permute-start | bytes 245768 | tf_op jit(solution)/shard_map/ppermute | solution.py:23
  91.3 4.7 %collective-permute-start.26 = (bf16[128,320]{1,0:T(8,128)(2,1)S(1)}, bf16[128,320]{1,0:T(8,128)(2,1)S(1)}, u32[]{:S(2)}, u32[]{:S(2)}) collective-permute-start(bf16[128,320]{1,0:T(8,128)(2,1)S(1)} %get-tuple-element.22.refs_0_), channel_id=1, source_target_pairs={{0,1},{1,0},{2,3},{3,2},{4,5},{5,4},{6,7},{7,6},{8,9},{9,8},{10,11... | collective-permute-start | bytes 245768 | tf_op jit(solution)/shard_map/ppermute | solution.py:27
  91.3 10.7 %collective-permute-start.17 = (bf16[128,320]{1,0:T(8,128)(2,1)S(1)}, bf16[128,320]{1,0:T(8,128)(2,1)S(1)}, u32[]{:S(2)}, u32[]{:S(2)}) collective-permute-start(bf16[128,320]{1,0:T(8,128)(2,1)S(1)} %get-tuple-element.22.refs_0_), channel_id=1, source_target_pairs={{0,8},{2,10},{4,12},{6,14},{8,0},{10,2},{12,4},{14,6},{1,9},{3,11}... | collective-permute-start | bytes 245768 | tf_op jit(solution)/shard_map/ppermute | solution.py:23
  94.0 9.3 %collective-permute-start.21 = (bf16[128,320]{1,0:T(8,128)(2,1)S(1)}, bf16[128,320]{1,0:T(8,128)(2,1)S(1)}, u32[]{:S(2)}, u32[]{:S(2)}) collective-permute-start(bf16[128,320]{1,0:T(8,128)(2,1)S(1)} %get-tuple-element.22.refs_0_), channel_id=1, source_target_pairs={{0,12},{2,14},{4,8},{6,10},{8,4},{10,6},{12,0},{14,2},{1,13},{3,15... | collective-permute-start | bytes 245768 | tf_op jit(solution)/shard_map/ppermute | solution.py:23
  94.7 9.9 %collective-permute-start.29 = (bf16[128,320]{1,0:T(8,128)(2,1)S(1)}, bf16[128,320]{1,0:T(8,128)(2,1)S(1)}, u32[]{:S(2)}, u32[]{:S(2)}) collective-permute-start(bf16[128,320]{1,0:T(8,128)(2,1)S(1)} %collective-permute-done.28.refs_4_), channel_id=1, source_target_pairs={{0,2},{2,0},{4,6},{6,4},{8,10},{10,8},{12,14},{14,12},{1,3},{3,1},... | collective-permute-start | bytes 245768 | tf_op jit(solution)/shard_map/ppermute | solution.py:23
  96.0 8.7 %collective-permute-start.27 = (bf16[128,320]{1,0:T(8,128)(2,1)S(1)}, bf16[128,320]{1,0:T(8,128)(2,1)S(1)}, u32[]{:S(2)}, u32[]{:S(2)}) collective-permute-start(bf16[128,320]{1,0:T(8,128)(2,1)S(1)} %collective-permute-done.25.refs_1_), channel_id=1, source_target_pairs={{0,1},{1,0},{2,3},{3,2},{4,5},{5,4},{6,7},{7,6},{8,9},{9,8},{10,11... | collective-permute-start | bytes 245768 | tf_op jit(solution)/shard_map/ppermute | solution.py:27
  96.0 9.2 %collective-permute-start.30 = (bf16[128,320]{1,0:T(8,128)(2,1)S(1)}, bf16[128,320]{1,0:T(8,128)(2,1)S(1)}, u32[]{:S(2)}, u32[]{:S(2)}) collective-permute-start(bf16[128,320]{1,0:T(8,128)(2,1)S(1)} %collective-permute-done.28.refs_4_), channel_id=1, source_target_pairs={{0,1},{1,0},{2,3},{3,2},{4,5},{5,4},{6,7},{7,6},{8,9},{9,8},{10,11... | collective-permute-start | bytes 245768 | tf_op jit(solution)/shard_map/ppermute | solution.py:27
  102.0 5.1 %collective-permute-start.18 = (bf16[128,320]{1,0:T(8,128)(2,1)S(1)}, bf16[128,320]{1,0:T(8,128)(2,1)S(1)}, u32[]{:S(2)}, u32[]{:S(2)}) collective-permute-start(bf16[128,320]{1,0:T(8,128)(2,1)S(1)} %collective-permute-done.17.refs_0_), channel_id=1, source_target_pairs={{0,2},{2,0},{4,6},{6,4},{8,10},{10,8},{12,14},{14,12},{1,3},{3,1},... | collective-permute-start | bytes 245768 | tf_op jit(solution)/shard_map/ppermute | solution.py:23
  103.3 4.9 %collective-permute-start.22 = (bf16[128,320]{1,0:T(8,128)(2,1)S(1)}, bf16[128,320]{1,0:T(8,128)(2,1)S(1)}, u32[]{:S(2)}, u32[]{:S(2)}) collective-permute-start(bf16[128,320]{1,0:T(8,128)(2,1)S(1)} %collective-permute-done.21.refs_4_), channel_id=1, source_target_pairs={{0,2},{2,0},{4,6},{6,4},{8,10},{10,8},{12,14},{14,12},{1,3},{3,1},... | collective-permute-start | bytes 245768 | tf_op jit(solution)/shard_map/ppermute | solution.py:23
  104.6 5.9 %collective-permute-start.19 = (bf16[128,320]{1,0:T(8,128)(2,1)S(1)}, bf16[128,320]{1,0:T(8,128)(2,1)S(1)}, u32[]{:S(2)}, u32[]{:S(2)}) collective-permute-start(bf16[128,320]{1,0:T(8,128)(2,1)S(1)} %collective-permute-done.17.refs_0_), channel_id=1, source_target_pairs={{0,1},{1,0},{2,3},{3,2},{4,5},{5,4},{6,7},{7,6},{8,9},{9,8},{10,11... | collective-permute-start | bytes 245768 | tf_op jit(solution)/shard_map/ppermute | solution.py:27
  104.7 5.8 %collective-permute-start.23 = (bf16[128,320]{1,0:T(8,128)(2,1)S(1)}, bf16[128,320]{1,0:T(8,128)(2,1)S(1)}, u32[]{:S(2)}, u32[]{:S(2)}) collective-permute-start(bf16[128,320]{1,0:T(8,128)(2,1)S(1)} %collective-permute-done.21.refs_4_), channel_id=1, source_target_pairs={{0,1},{1,0},{2,3},{3,2},{4,5},{5,4},{6,7},{7,6},{8,9},{9,8},{10,11... | collective-permute-start | bytes 245768 | tf_op jit(solution)/shard_map/ppermute | solution.py:27
  105.2 3.6 %collective-permute-start.31 = (bf16[128,320]{1,0:T(8,128)(2,1)S(1)}, bf16[128,320]{1,0:T(8,128)(2,1)S(1)}, u32[]{:S(2)}, u32[]{:S(2)}) collective-permute-start(bf16[128,320]{1,0:T(8,128)(2,1)S(1)} %collective-permute-done.29.refs_5_), channel_id=1, source_target_pairs={{0,1},{1,0},{2,3},{3,2},{4,5},{5,4},{6,7},{7,6},{8,9},{9,8},{10,11... | collective-permute-start | bytes 245768 | tf_op jit(solution)/shard_map/ppermute | solution.py:27
  107.1 3.5 %collective-permute-start.20 = (bf16[128,320]{1,0:T(8,128)(2,1)S(1)}, bf16[128,320]{1,0:T(8,128)(2,1)S(1)}, u32[]{:S(2)}, u32[]{:S(2)}) collective-permute-start(bf16[128,320]{1,0:T(8,128)(2,1)S(1)} %collective-permute-done.18.refs_1_), channel_id=1, source_target_pairs={{0,1},{1,0},{2,3},{3,2},{4,5},{5,4},{6,7},{7,6},{8,9},{9,8},{10,11... | collective-permute-start | bytes 245768 | tf_op jit(solution)/shard_map/ppermute | solution.py:27
  (17 other events, 291.6 us)

commit v2 on v1

--- a/solution.py
+++ b/solution.py
@@ -15,7 +15,7 @@
 MIB = 1 << 20
 VMEM = pl.BlockSpec(memory_space=pltpu.VMEM)
 SMEM = pl.BlockSpec(memory_space=pltpu.SMEM)
-ANY = pl.BlockSpec(memory_space=pl.ANY)
+HBM = pl.BlockSpec(memory_space=pltpu.HBM)
 
 
 def chip_swap(cells, mask):
@@ -269,16 +269,12 @@
         lanes = {0: packed}
         for mask in range(1, pair):
             lanes[mask] = chip_swap(after(packed, lanes[1]) if mask == 3 else packed, 2 * mask)
-        grads = after(track_grad, lanes[1]) if pair > 1 else track_grad
-    else:
-        grads = track_grad
     partner_input = group_swap(enc_input)
 
     lines = -(-tracks // 16) * 16
-    windows = call(windows_kernel, shape(count, lines, 2 * token_rows), [VMEM], name="windows")(
-        grads.T
-    )
-    exchanged = lax.all_to_all(windows, ("chip", "core"), 0, 0, tiled=True)
+    windows = call(
+        windows_kernel, shape(count, lines, 2 * token_rows), [VMEM], limit=16, name="windows"
+    )(track_grad.T)
     slots = jnp.pad(
         track_index.reshape(count, tracks), ((0, 0), (0, lines - tracks)), constant_values=-1
     )
@@ -295,7 +291,7 @@
         blocks = []
         for mask in range(pair):
             near = lanes[mask]
-            far = chip_swap(after(near, exchanged) if mask == 2 else near, 1)
+            far = chip_swap(near, 1)
             blocks += [
                 (4 * mask, near),
                 (4 * mask + 1, core_swap(near)),
@@ -310,14 +306,15 @@
                 shape(token_rows, width),
                 shape(count * extra, width),
             ),
-            [SMEM, VMEM, VMEM] + [ANY] * count,
+            [SMEM, VMEM, VMEM] + [HBM] * count,
             scratch=(
                 pltpu.VMEM((2 * token_rows, count * rows), jnp.bfloat16),
                 pltpu.VMEM((count * rows, width), jnp.bfloat16),
                 pltpu.SemaphoreType.DMA((count, 2)),
             ),
+            limit=16,
             name="tokens",
-        )(ids, enc_input, partner_input, *[block for _, block in blocks])
+        )(ids, enc_input, partner_input, *[pltpu.with_memory_space_constraint(block, pltpu.HBM) for _, block in blocks])
     else:
         gathered = lax.all_gather(packed, ("chip", "core"), axis=0)
         track_rows = gathered[:, rows:].reshape(count * extra, width)
@@ -329,40 +326,38 @@
             for cells in (enc_input, partner_input)
         )
     theirs = group_swap(partner)
+    exchanged = lax.all_to_all(after(windows, partner), ("chip", "core"), 0, 0, tiled=True)
     tokens, normed, keyval = call(
         keyval_kernel,
         (shape(token_rows, dim), shape(token_rows, dim), shape(token_rows, QK + VDIM)),
         [SMEM] + [VMEM] * 4,
+        limit=8,
         name="keyval",
     )(group.reshape(1), mine, theirs, norm_gain.reshape(1, dim), kv_weight.T)
 
     if direct:
-        early, late = [], []
-        for mask in range(pair):
-            near = chip_swap(keyval, 2 * mask) if mask else keyval
-            far = chip_swap(near, 1)
-            side = early if mask < max(1, pair // 2) else late
-            side += [near, far, core_swap(near), core_swap(far)]
-        stages = [side for side in (early, late) if side]
+        nears = [chip_swap(keyval, 2 * mask) if mask else keyval for mask in range(pair)]
+        fars = [chip_swap(near, 1) for near in nears]
+        cut = max(1, pair // 2)
+        stages = [
+            [cells for piece in side for cells in (piece, core_swap(piece))]
+            for side in (nears[:cut] + fars[:cut], nears[cut:] + fars[cut:])
+            if side
+        ]
     else:
-        stages = [[lax.all_gather(keyval, ("chip", "core"), axis=0, tiled=True)]]
-
-    query = call(query_kernel, shape(HEADS * token_rows, QK), [VMEM] * 2, name="query")(
+        nears = fars = [lax.all_gather(keyval, ("chip", "core"), axis=0, tiled=True)]
+        stages = [nears]
+
+    query = call(query_kernel, shape(HEADS * token_rows, QK), [VMEM] * 2, limit=8, name="query")(
         normed, q_weight
     )
     skip_grad, sums = call(
         functools.partial(decoder_kernel, extra),
         (shape(token_rows, dim), shape(3, dim, kind=jnp.float32)),
         [VMEM] * 5,
+        limit=16,
         name="decoder",
-    )(tokens, exchanged.reshape(count * lines, 2 * token_rows), chosen, track_rows, dec_weight)
-    sums = sums + core_swap(sums)
-    step = 1
-    while step < chips:
-        sums = sums + chip_swap(sums, step)
-        step *= 2
-    dec_weight_grad = sums / jnp.float32(math.sqrt(token_rows * count))
-
+    )(after(tokens, nears[min(1, len(nears) - 1)]), exchanged.reshape(count * lines, 2 * token_rows), chosen, track_rows, dec_weight)
     row_block = 2 * token_rows if direct else token_rows
     state = []
     for turn, pieces in enumerate(stages):
@@ -386,9 +381,19 @@
                 pltpu.VMEM((keys, 256), jnp.bfloat16),
                 pltpu.VMEM((2, row_block, keys), jnp.float32),
             ),
-            limit=60 if len(stages) == 1 else 40,
+            limit=60 if len(stages) == 1 else 12,
             name="attention",
         )(query, *pieces, *state, *extras)
+        if turn == 0:
+            scored = state
+    sums = sums + core_swap(sums)
+    waits = [nears[-1], scored if direct else nears[-1]]
+    step = 1
+    while step < chips:
+        held = after(sums, waits.pop(0)) if waits and len(stages) > 1 else sums
+        sums = sums + chip_swap(held, step)
+        step *= 2
+    dec_weight_grad = sums / jnp.float32(math.sqrt(token_rows * count))
     return (state, skip_grad, dec_weight_grad)
 
 

time: 117 us -> 103 us (0.88)
  waiting for transfers between devices: 51.7 us -> 37.2 us
    all_to_all x1, waiting for transfers between devices: 6.37 us -> 0.01 us  [shards(): lax.all_to_all(after(windows, partner), ('chip', 'core'), 0, 0, tiled=True)]
    ppermute x2, waiting for transfers between devices: 5.68 us -> 0.01 us  [group_swap(): return lax.ppermute(cells, 'groups', [(0, 1), (1, 0)])]
    ppermute x17, starting transfers between devices: 21.6 us -> 26.3 us  [chip_swap(): return lax.ppermute(cells, 'chip', [(i, i ^ mask) for i in range(count)])]
    all_to_all x1, starting transfers between devices: 11 us -> 6.43 us  [shards(): lax.all_to_all(after(windows, partner), ('chip', 'core'), 0, 0, tiled=True)]
    ppermute x17, waiting for transfers between devices: 38.4 us -> 34.4 us  [chip_swap(): return lax.ppermute(cells, 'chip', [(i, i ^ mask) for i in range(count)])]
    ppermute x17, waiting for transfers between devices: 1.23 us -> 2.74 us  [core_swap(): return lax.ppermute(cells, 'core', [(0, 1), (1, 0)])]
    unnamed x24 -> x36, local copies, waits for them, and re-layouts: 5.67 us -> 5.55 us
  transfers between devices with their start and end apart: 37 -> 37, of which waited for: 12 -> 12; matrix products, arithmetic and copies ran while one was open for 3% -> 3% of each run, Pallas kernels for 3% -> 11%
where the time goes in v2:
time: 103 us; the launch traced here: 102 us
  starting transfers between devices  38 us (37%)
  waiting for transfers between devices  37.2 us (36%)
  Pallas kernels  16.2 us (16%)
  local copies, waits for them, and re-layouts  7.85 us (8%)
  other arithmetic  2.1 us (2%)
    ppermute x17, waiting for transfers between devices, chip_swap(): return lax.ppermute(cells, 'chip', [(i, i ^ mask) for i in range(count)])  34.4 us
    ppermute x17, starting transfers between devices, chip_swap(): return lax.ppermute(cells, 'chip', [(i, i ^ mask) for i in range(count)])  26.3 us
    pallas_call x2, Pallas kernels, shards(): call(functools.partial(attention_kernel, row_block, 512, len(pieces), tur...  7.43 us
    all_to_all x1, starting transfers between devices, shards(): lax.all_to_all(after(windows, partner), ('chip', 'core'), 0, 0, tiled=True)  6.43 us
    unnamed x36, local copies, waits for them, and re-layouts  5.55 us
    pallas_call x1, Pallas kernels, shards(): call(functools.partial(tokens_kernel, rows, extra), (shape(token_rows, wi...  4.96 us
    ppermute x2, starting transfers between devices, group_swap(): return lax.ppermute(cells, 'groups', [(0, 1), (1, 0)])  3.05 us
    ppermute x17, waiting for transfers between devices, core_swap(): return lax.ppermute(cells, 'core', [(0, 1), (1, 0)])  2.74 us
  transfers between devices with their start and end apart: 37, of which 12 were waited for; matrix products, arithmetic and copies ran while one was open for 3% of the time, Pallas kernels for 11%

profile of v2, /device:TPU:0, one launch (start us, length us, event | category | flops | bytes accessed | tf_op | source)
XLA Modules:
  0.0 102.4 jit_solution(4215831216749982750)
XLA Ops:
  1.8 3.1 %collective-permute-start.4 = (bf16[200,768]{1,0:T(8,128)(2,1)S(1)}, bf16[200,768]{1,0:T(8,128)(2,1)S(1)}, u32[]{:S(2)}, u32[]{:S(2)}) collective-permute-start(bf16[200,768]{1,0:T(8,128)(2,1)S(1)} %pad_maximum_fusion.refs_0_), channel_id=1, source_target_pairs={{0,4},{2,6},{4,0},{6,2},{8,12},{10,14},{12,8},{14,10},{1,5},{3,7},... | collective-permute-start | bytes 921608 | tf_op jit(solution)/shard_map/ppermute | solution.py:23
  4.8 2.6 %collective-permute-start.8 = (bf16[200,768]{1,0:T(8,128)(2,1)S(1)}, bf16[200,768]{1,0:T(8,128)(2,1)S(1)}, u32[]{:S(2)}, u32[]{:S(2)}) collective-permute-start(bf16[200,768]{1,0:T(8,128)(2,1)S(1)} %pad_maximum_fusion.refs_0_), channel_id=1, source_target_pairs={{0,8},{2,10},{4,12},{6,14},{8,0},{10,2},{12,4},{14,6},{1,9},{3,11}... | collective-permute-start | bytes 921608 | tf_op jit(solution)/shard_map/ppermute | solution.py:23
  7.4 1.5 %collective-permute-start.2 = (bf16[200,768]{1,0:T(8,128)(2,1)S(1)}, bf16[200,768]{1,0:T(8,128)(2,1)S(1)}, u32[]{:S(2)}, u32[]{:S(2)}) collective-permute-start(bf16[200,768]{1,0:T(8,128)(2,1)S(1)} %pad_maximum_fusion.refs_0_), channel_id=1, source_target_pairs={{0,2},{2,0},{4,6},{6,4},{8,10},{10,8},{12,14},{14,12},{1,3},{3,1},... | collective-permute-start | bytes 921608 | tf_op jit(solution)/shard_map/ppermute | solution.py:23
  9.0 9.6 %collective-permute-done.4.refs_4_ = bf16[200,768]{1,0:T(8,128)(2,1)S(1)} collective-permute-done((bf16[200,768]{1,0:T(8,128)(2,1)S(1)}, bf16[200,768]{1,0:T(8,128)(2,1)S(1)}, u32[]{:S(2)}, u32[]{:S(2)}) %collective-permute-start.4) | collective-permute-done | bytes 307232 | tf_op jit(solution)/shard_map/ppermute | solution.py:23
  18.6 2.6 %collective-permute-start.12 = (bf16[200,768]{1,0:T(8,128)(2,1)S(1)}, bf16[200,768]{1,0:T(8,128)(2,1)}, u32[]{:S(2)}, u32[]{:S(2)}) collective-permute-start(bf16[200,768]{1,0:T(8,128)(2,1)S(1)} %pad_maximum_fusion.refs_0_), channel_id=1, source_target_pairs={{0,12},{2,14},{4,8},{6,10},{8,4},{10,6},{12,0},{14,2},{1,13},{3,15... | collective-permute-start | bytes 921608 | tf_op jit(solution)/shard_map/ppermute | solution.py:23
  21.2 1.5 %collective-permute-start.6 = (bf16[200,768]{1,0:T(8,128)(2,1)S(1)}, bf16[200,768]{1,0:T(8,128)(2,1)}, u32[]{:S(2)}, u32[]{:S(2)}) collective-permute-start(bf16[200,768]{1,0:T(8,128)(2,1)S(1)} %collective-permute-done.4.refs_4_), channel_id=1, source_target_pairs={{0,2},{2,0},{4,6},{6,4},{8,10},{10,8},{12,14},{14,12},{1,3},{3,1},... | collective-permute-start | bytes 921608 | tf_op jit(solution)/shard_map/ppermute | solution.py:23
  23.3 1.5 %collective-permute-start = (bf16[256,1408]{1,0:T(8,128)(2,1)}, bf16[256,1408]{1,0:T(8,128)(2,1)S(1)}, u32[]{:S(2)}, u32[]{:S(2)}) collective-permute-start(bf16[256,1408]{1,0:T(8,128)(2,1)} %own_ref.1), channel_id=1, source_target_pairs={{0,16},{16,0},{1,17},{17,1},{2,18},{18,2},{3,19},{19,3},{4,20},{20... | collective-permute-start | bytes 2162696 | tf_op jit(solution)/shard_map/ppermute | solution.py:31
  24.8 4.3 %collective-permute-done.12.refs_12_ = bf16[200,768]{1,0:T(8,128)(2,1)} collective-permute-done((bf16[200,768]{1,0:T(8,128)(2,1)S(1)}, bf16[200,768]{1,0:T(8,128)(2,1)}, u32[]{:S(2)}, u32[]{:S(2)}) %collective-permute-start.12) | collective-permute-done | bytes 307232 | tf_op jit(solution)/shard_map/ppermute | solution.py:23
  29.1 2.5 %collective-permute-done.6.refs_6_ = bf16[200,768]{1,0:T(8,128)(2,1)} collective-permute-done((bf16[200,768]{1,0:T(8,128)(2,1)S(1)}, bf16[200,768]{1,0:T(8,128)(2,1)}, u32[]{:S(2)}, u32[]{:S(2)}) %collective-permute-start.6) | collective-permute-done | bytes 307232 | tf_op jit(solution)/shard_map/ppermute | solution.py:23
  31.5 4.2 %collective-permute-done.10.refs_10_ = bf16[200,768]{1,0:T(8,128)(2,1)} collective-permute-done((bf16[200,768]{1,0:T(8,128)(2,1)S(1)}, bf16[200,768]{1,0:T(8,128)(2,1)}, u32[]{:S(2)}, u32[]{:S(2)}) %collective-permute-start.10) | collective-permute-done | bytes 307232 | tf_op jit(solution)/shard_map/ppermute | solution.py:23
  35.8 1.5 %collective-permute-start.14 = (bf16[200,768]{1,0:T(8,128)(2,1)}, bf16[200,768]{1,0:T(8,128)(2,1)}, u32[]{:S(2)}, u32[]{:S(2)}) collective-permute-start(bf16[200,768]{1,0:T(8,128)(2,1)} %collective-permute-done.12.refs_12_), channel_id=1, source_target_pairs={{0,2},{2,0},{4,6},{6,4},{8,10},{10,8},{12,14},{14,12},{1,3},{3,1},... | collective-permute-start | bytes 921608 | tf_op jit(solution)/shard_map/ppermute | solution.py:23
  38.0 5.0 %collective-permute-done.14.refs_14_ = bf16[200,768]{1,0:T(8,128)(2,1)} collective-permute-done((bf16[200,768]{1,0:T(8,128)(2,1)}, bf16[200,768]{1,0:T(8,128)(2,1)}, u32[]{:S(2)}, u32[]{:S(2)}) %collective-permute-start.14) | collective-permute-done | bytes 307232 | tf_op jit(solution)/shard_map/ppermute | solution.py:23
  43.2 1.8 %collective-permute-done.15.refs_15_ = bf16[200,768]{1,0:T(8,128)(2,1)} collective-permute-done((bf16[200,768]{1,0:T(8,128)(2,1)}, bf16[200,768]{1,0:T(8,128)(2,1)}, u32[]{:S(2)}, u32[]{:S(2)}) %collective-permute-start.15) | collective-permute-done | bytes 307232 | tf_op jit(solution)/shard_map/ppermute | solution.py:27
  45.0 1.1 %copy-done.4 = bf16[256,1408]{1,0:T(8,128)(2,1)S(1)} copy-done((bf16[256,1408]{1,0:T(8,128)(2,1)S(1)}, bf16[256,1408]{1,0:T(8,128)(2,1)}, u32[]{:S(2)}) %copy-start.4) | copy-done | bytes 720920
  46.1 5.0 %tokens.1 = (bf16[128,768]{1,0:T(8,128)(2,1)S(1)}, bf16[128,768]{1,0:T(8,128)(2,1)S(1)}, bf16[384,768]{1,0:T(8,128)(2,1)S(1)}) custom-call(s32[16]{0:T(128)S(1)} %iota_xor_fusion.ids_ref, bf16[256,1408]{1,0:T(8,128)(2,1)S(1)} %copy-done.4, bf16[256,1408]{1,0:T(8,128)(2,1)S(1)} %collective-permute-done.partner_ref, bf16[200,768]{1,0:T(8,128)(2,1)} %copy-done.7, ...), custom_call_target="tpu_custom_call" | custom-call | tf_op jit(solution)/shard_map/tokens/pallas_call | solution.py:302
  51.1 1.6 %collective-permute-start.16 = (bf16[128,768]{1,0:T(8,128)(2,1)S(1)}, bf16[128,768]{1,0:T(8,128)(2,1)S(1)}, u32[]{:S(2)}, u32[]{:S(2)}) collective-permute-start(bf16[128,768]{1,0:T(8,128)(2,1)S(1)} %get-tuple-element.20), channel_id=1, source_target_pairs={{0,16},{16,0},{1,17},{17,1},{2,18},{18,2},{3,19},{19,3},{4,20},{20... | collective-permute-start | bytes 589832 | tf_op jit(solution)/shard_map/ppermute | solution.py:31
  53.4 6.4 %all-to-all-start = ((bf16[16,16,256]{2,1,0:T(8,128)(2,1)}), bf16[16,16,256]{2,1,0:T(8,128)(2,1)S(1)}, u32[]{:S(2)}, u32[]{:S(2)}) async-start(bf16[16,16,256]{2,1,0:T(8,128)(2,1)} %windows.1), calls=%async_computation | async-start | bytes 262144 | tf_op jit(solution)/shard_map/all_to_all | solution.py:329
  62.4 2.0 %collective-permute-start.26 = (bf16[128,320]{1,0:T(8,128)(2,1)S(1)}, bf16[128,320]{1,0:T(8,128)(2,1)S(1)}, u32[]{:S(2)}, u32[]{:S(2)}) collective-permute-start(bf16[128,320]{1,0:T(8,128)(2,1)S(1)} %get-tuple-element.22.refs_0_), channel_id=1, source_target_pairs={{0,4},{2,6},{4,0},{6,2},{8,12},{10,14},{12,8},{14,10},{1,5},{3,7},... | collective-permute-start | bytes 245768 | tf_op jit(solution)/shard_map/ppermute | solution.py:23
  64.4 2.4 %collective-permute-start.19 = (bf16[128,320]{1,0:T(8,128)(2,1)S(1)}, bf16[128,320]{1,0:T(8,128)(2,1)S(1)}, u32[]{:S(2)}, u32[]{:S(2)}) collective-permute-start(bf16[128,320]{1,0:T(8,128)(2,1)S(1)} %get-tuple-element.22.refs_0_), channel_id=1, source_target_pairs={{0,12},{2,14},{4,8},{6,10},{8,4},{10,6},{12,0},{14,2},{1,13},{3,15... | collective-permute-start | bytes 245768 | tf_op jit(solution)/shard_map/ppermute | solution.py:23
  66.8 1.5 %collective-permute-start.28 = (bf16[128,320]{1,0:T(8,128)(2,1)S(1)}, bf16[128,320]{1,0:T(8,128)(2,1)S(1)}, u32[]{:S(2)}, u32[]{:S(2)}) collective-permute-start(bf16[128,320]{1,0:T(8,128)(2,1)S(1)} %get-tuple-element.22.refs_0_), channel_id=1, source_target_pairs={{0,2},{2,0},{4,6},{6,4},{8,10},{10,8},{12,14},{14,12},{1,3},{3,1},... | collective-permute-start | bytes 245768 | tf_op jit(solution)/shard_map/ppermute | solution.py:23
  69.1 1.9 %decoder.1 = (bf16[128,1536]{1,0:T(8,128)(2,1)}, f32[3,1536]{1,0:T(4,128)S(1)}) custom-call(bf16[128,1536]{1,0:T(8,128)(2,1)S(1)} %get-tuple-element.26.refs_10_.tok_ref, bf16[256,256]{1,0:T(8,128)(2,1)S(1)} %bitcast.5, bf16[256,384]{1,0:T(8,128)(2,1)S(1)} %compare_select_fusion.chosen_ref, bf16[384,768]{1,0:T(8,128)(2,1)S(1)} %get-tuple-element.28.tracks_ref, ...), custom_call_target="tpu_custom_call" | custom-call | tf_op jit(solution)/shard_map/decoder/pallas_call | solution.py:354
  73.0 1.5 %collective-permute-start.33 = (f32[3,1536]{1,0:T(4,128)S(1)}, f32[3,1536]{1,0:T(4,128)S(1)}, u32[]{:S(2)}, u32[]{:S(2)}) collective-permute-start(f32[3,1536]{1,0:T(4,128)S(1)} %add.48), channel_id=1, source_target_pairs={{0,2},{2,0},{4,6},{6,4},{8,10},{10,8},{12,14},{14,12},{1,3},{3,1},... | collective-permute-start | bytes 55304 | tf_op jit(solution)/shard_map/ppermute | solution.py:23
  75.1 1.4 %collective-permute-done.17.refs_0_ = bf16[128,320]{1,0:T(8,128)(2,1)S(1)} collective-permute-done((bf16[128,320]{1,0:T(8,128)(2,1)S(1)}, bf16[128,320]{1,0:T(8,128)(2,1)S(1)}, u32[]{:S(2)}, u32[]{:S(2)}) %collective-permute-start.17) | collective-permute-done | bytes 81952 | tf_op jit(solution)/shard_map/ppermute | solution.py:23
  79.2 3.0 %collective-permute-done.21.refs_4_ = bf16[128,320]{1,0:T(8,128)(2,1)S(1)} collective-permute-done((bf16[128,320]{1,0:T(8,128)(2,1)S(1)}, bf16[128,320]{1,0:T(8,128)(2,1)S(1)}, u32[]{:S(2)}, u32[]{:S(2)}) %collective-permute-start.21) | collective-permute-done | bytes 81952 | tf_op jit(solution)/shard_map/ppermute | solution.py:23
  82.1 1.2 %collective-permute-done.23.refs_6_ = bf16[128,320]{1,0:T(8,128)(2,1)S(1)} collective-permute-done((bf16[128,320]{1,0:T(8,128)(2,1)S(1)}, bf16[128,320]{1,0:T(8,128)(2,1)S(1)}, u32[]{:S(2)}, u32[]{:S(2)}) %collective-permute-start.23) | collective-permute-done | bytes 81952 | tf_op jit(solution)/shard_map/ppermute | solution.py:23
  83.3 1.9 %copy-done.2 = bf16[1536,1024]{1,0:T(8,128)(2,1)S(1)} copy-done((bf16[1536,1024]{1,0:T(8,128)(2,1)S(1)}, bf16[1536,1024]{1,0:T(8,128)(2,1)}, u32[]{:S(2)}) %copy-start.2) | copy-done | bytes 3145752
  85.8 1.8 %attention.2 = (f32[1024,128]{1,0:T(8,128)S(1)}, f32[1024,256]{1,0:T(8,128)S(1)}) custom-call(bf16[1024,128]{1,0:T(8,128)(2,1)S(1)} %query.1.query_ref, bf16[128,320]{1,0:T(8,128)(2,1)S(1)} %get-tuple-element.22.refs_0_, bf16[128,320]{1,0:T(8,128)(2,1)S(1)} %collective-permute-done.25.refs_1_, bf16[128,320]{1,0:T(8,128)(2,1)S(1)} %collective-permute-done.26.refs_2_, ...), custom_call_target="tpu_custom_call" | custom-call | tf_op jit(solution)/shard_map/attention/pallas_call | solution.py:375
  87.6 1.3 %collective-permute-start.34 = (f32[3,1536]{1,0:T(4,128)S(1)}, f32[3,1536]{1,0:T(4,128)S(1)}, u32[]{:S(2)}, u32[]{:S(2)}) collective-permute-start(f32[3,1536]{1,0:T(4,128)S(1)} %add.49), channel_id=1, source_target_pairs={{0,4},{2,6},{4,0},{6,2},{8,12},{10,14},{12,8},{14,10},{1,5},{3,7},... | collective-permute-start | bytes 55304 | tf_op jit(solution)/shard_map/ppermute | solution.py:23
  88.8 2.6 %collective-permute-done.34 = f32[3,1536]{1,0:T(4,128)S(1)} collective-permute-done((f32[3,1536]{1,0:T(4,128)S(1)}, f32[3,1536]{1,0:T(4,128)S(1)}, u32[]{:S(2)}, u32[]{:S(2)}) %collective-permute-start.34) | collective-permute-done | bytes 18464 | tf_op jit(solution)/shard_map/ppermute | solution.py:23
  91.5 2.2 %collective-permute-start.35 = (f32[3,1536]{1,0:T(4,128)S(1)}, f32[3,1536]{1,0:T(4,128)S(1)}, u32[]{:S(2)}, u32[]{:S(2)}) collective-permute-start(f32[3,1536]{1,0:T(4,128)S(1)} %add.50), channel_id=1, source_target_pairs={{0,8},{2,10},{4,12},{6,14},{8,0},{10,2},{12,4},{14,6},{1,9},{3,11}... | collective-permute-start | bytes 55304 | tf_op jit(solution)/shard_map/ppermute | solution.py:23
  93.7 2.3 %copy-done.1 = bf16[1536,1536]{1,0:T(8,128)(2,1)S(1)} copy-done((bf16[1536,1536]{1,0:T(8,128)(2,1)S(1)}, bf16[1536,1536]{1,0:T(8,128)(2,1)}, u32[]{:S(2)}) %copy-start.1) | copy-done | bytes 4718616
  96.1 5.7 %attention.3 = bf16[128,1536]{1,0:T(8,128)(2,1)} custom-call(bf16[1024,128]{1,0:T(8,128)(2,1)S(1)} %query.1.query_ref, bf16[128,320]{1,0:T(8,128)(2,1)S(1)} %collective-permute-done.17.refs_0_, bf16[128,320]{1,0:T(8,128)(2,1)S(1)} %collective-permute-done.18.refs_1_, bf16[128,320]{1,0:T(8,128)(2,1)S(1)} %collective-permute-done.19.refs_2_, ...), custom_call_target="tpu_custom_call" | custom-call | tf_op jit(solution)/shard_map/attention/pallas_call | solution.py:375
  (103 shorter events, 12.9 us)
Async XLA Ops:
  1.8 16.8 %collective-permute-start.4 = (bf16[200,768]{1,0:T(8,128)(2,1)S(1)}, bf16[200,768]{1,0:T(8,128)(2,1)S(1)}, u32[]{:S(2)}, u32[]{:S(2)}) collective-permute-start(bf16[200,768]{1,0:T(8,128)(2,1)S(1)} %pad_maximum_fusion.refs_0_), channel_id=1, source_target_pairs={{0,4},{2,6},{4,0},{6,2},{8,12},{10,14},{12,8},{14,10},{1,5},{3,7},... | collective-permute-start | bytes 921608 | tf_op jit(solution)/shard_map/ppermute | solution.py:23
  4.8 17.9 %collective-permute-start.8 = (bf16[200,768]{1,0:T(8,128)(2,1)S(1)}, bf16[200,768]{1,0:T(8,128)(2,1)S(1)}, u32[]{:S(2)}, u32[]{:S(2)}) collective-permute-start(bf16[200,768]{1,0:T(8,128)(2,1)S(1)} %pad_maximum_fusion.refs_0_), channel_id=1, source_target_pairs={{0,8},{2,10},{4,12},{6,14},{8,0},{10,2},{12,4},{14,6},{1,9},{3,11}... | collective-permute-start | bytes 921608 | tf_op jit(solution)/shard_map/ppermute | solution.py:23
  7.4 15.8 %collective-permute-start.2 = (bf16[200,768]{1,0:T(8,128)(2,1)S(1)}, bf16[200,768]{1,0:T(8,128)(2,1)S(1)}, u32[]{:S(2)}, u32[]{:S(2)}) collective-permute-start(bf16[200,768]{1,0:T(8,128)(2,1)S(1)} %pad_maximum_fusion.refs_0_), channel_id=1, source_target_pairs={{0,2},{2,0},{4,6},{6,4},{8,10},{10,8},{12,14},{14,12},{1,3},{3,1},... | collective-permute-start | bytes 921608 | tf_op jit(solution)/shard_map/ppermute | solution.py:23
  9.0 15.8 %collective-permute-start.1 = (bf16[200,768]{1,0:T(8,128)(2,1)S(1)}, bf16[200,768]{1,0:T(8,128)(2,1)S(1)}, u32[]{:S(2)}, u32[]{:S(2)}) collective-permute-start(bf16[200,768]{1,0:T(8,128)(2,1)S(1)} %pad_maximum_fusion.refs_0_), channel_id=1, source_target_pairs={{0,1},{1,0},{2,3},{3,2},{4,5},{5,4},{6,7},{7,6},{8,9},{9,8},{10,11... | collective-permute-start | bytes 921608 | tf_op jit(solution)/shard_map/ppermute | solution.py:27
  18.6 10.5 %collective-permute-start.12 = (bf16[200,768]{1,0:T(8,128)(2,1)S(1)}, bf16[200,768]{1,0:T(8,128)(2,1)}, u32[]{:S(2)}, u32[]{:S(2)}) collective-permute-start(bf16[200,768]{1,0:T(8,128)(2,1)S(1)} %pad_maximum_fusion.refs_0_), channel_id=1, source_target_pairs={{0,12},{2,14},{4,8},{6,10},{8,4},{10,6},{12,0},{14,2},{1,13},{3,15... | collective-permute-start | bytes 921608 | tf_op jit(solution)/shard_map/ppermute | solution.py:23
  21.2 10.3 %collective-permute-start.6 = (bf16[200,768]{1,0:T(8,128)(2,1)S(1)}, bf16[200,768]{1,0:T(8,128)(2,1)}, u32[]{:S(2)}, u32[]{:S(2)}) collective-permute-start(bf16[200,768]{1,0:T(8,128)(2,1)S(1)} %collective-permute-done.4.refs_4_), channel_id=1, source_target_pairs={{0,2},{2,0},{4,6},{6,4},{8,10},{10,8},{12,14},{14,12},{1,3},{3,1},... | collective-permute-start | bytes 921608 | tf_op jit(solution)/shard_map/ppermute | solution.py:23
  22.8 13.0 %collective-permute-start.10 = (bf16[200,768]{1,0:T(8,128)(2,1)S(1)}, bf16[200,768]{1,0:T(8,128)(2,1)}, u32[]{:S(2)}, u32[]{:S(2)}) collective-permute-start(bf16[200,768]{1,0:T(8,128)(2,1)S(1)} %collective-permute-done.8.refs_8_), channel_id=1, source_target_pairs={{0,2},{2,0},{4,6},{6,4},{8,10},{10,8},{12,14},{14,12},{1,3},{3,1},... | collective-permute-start | bytes 921608 | tf_op jit(solution)/shard_map/ppermute | solution.py:23
  23.3 19.8 %collective-permute-start = (bf16[256,1408]{1,0:T(8,128)(2,1)}, bf16[256,1408]{1,0:T(8,128)(2,1)S(1)}, u32[]{:S(2)}, u32[]{:S(2)}) collective-permute-start(bf16[256,1408]{1,0:T(8,128)(2,1)} %own_ref.1), channel_id=1, source_target_pairs={{0,16},{16,0},{1,17},{17,1},{2,18},{18,2},{3,19},{19,3},{4,20},{20... | collective-permute-start | bytes 2162696 | tf_op jit(solution)/shard_map/ppermute | solution.py:31
  24.8 12.5 %collective-permute-start.5 = (bf16[200,768]{1,0:T(8,128)(2,1)S(1)}, bf16[200,768]{1,0:T(8,128)(2,1)S(1)}, u32[]{:S(2)}, u32[]{:S(2)}) collective-permute-start(bf16[200,768]{1,0:T(8,128)(2,1)S(1)} %collective-permute-done.4.refs_4_), channel_id=1, source_target_pairs={{0,1},{1,0},{2,3},{3,2},{4,5},{5,4},{6,7},{7,6},{8,9},{9,8},{10,11... | collective-permute-start | bytes 921608 | tf_op jit(solution)/shard_map/ppermute | solution.py:27
  29.1 8.3 %collective-permute-start.9 = (bf16[200,768]{1,0:T(8,128)(2,1)S(1)}, bf16[200,768]{1,0:T(8,128)(2,1)S(1)}, u32[]{:S(2)}, u32[]{:S(2)}) collective-permute-start(bf16[200,768]{1,0:T(8,128)(2,1)S(1)} %collective-permute-done.8.refs_8_), channel_id=1, source_target_pairs={{0,1},{1,0},{2,3},{3,2},{4,5},{5,4},{6,7},{7,6},{8,9},{9,8},{10,11... | collective-permute-start | bytes 921608 | tf_op jit(solution)/shard_map/ppermute | solution.py:27
  31.5 6.4 %collective-permute-start.3 = (bf16[200,768]{1,0:T(8,128)(2,1)S(1)}, bf16[200,768]{1,0:T(8,128)(2,1)S(1)}, u32[]{:S(2)}, u32[]{:S(2)}) collective-permute-start(bf16[200,768]{1,0:T(8,128)(2,1)S(1)} %collective-permute-done.2.refs_2_), channel_id=1, source_target_pairs={{0,1},{1,0},{2,3},{3,2},{4,5},{5,4},{6,7},{7,6},{8,9},{9,8},{10,11... | collective-permute-start | bytes 921608 | tf_op jit(solution)/shard_map/ppermute | solution.py:27
  35.8 7.3 %collective-permute-start.14 = (bf16[200,768]{1,0:T(8,128)(2,1)}, bf16[200,768]{1,0:T(8,128)(2,1)}, u32[]{:S(2)}, u32[]{:S(2)}) collective-permute-start(bf16[200,768]{1,0:T(8,128)(2,1)} %collective-permute-done.12.refs_12_), channel_id=1, source_target_pairs={{0,2},{2,0},{4,6},{6,4},{8,10},{10,8},{12,14},{14,12},{1,3},{3,1},... | collective-permute-start | bytes 921608 | tf_op jit(solution)/shard_map/ppermute | solution.py:23
  37.3 5.8 %collective-permute-start.13 = (bf16[200,768]{1,0:T(8,128)(2,1)}, bf16[200,768]{1,0:T(8,128)(2,1)}, u32[]{:S(2)}, u32[]{:S(2)}) collective-permute-start(bf16[200,768]{1,0:T(8,128)(2,1)} %collective-permute-done.12.refs_12_), channel_id=1, source_target_pairs={{0,1},{1,0},{2,3},{3,2},{4,5},{5,4},{6,7},{7,6},{8,9},{9,8},{10,11... | collective-permute-start | bytes 921608 | tf_op jit(solution)/shard_map/ppermute | solution.py:27
  37.3 5.8 %collective-permute-start.7 = (bf16[200,768]{1,0:T(8,128)(2,1)}, bf16[200,768]{1,0:T(8,128)(2,1)}, u32[]{:S(2)}, u32[]{:S(2)}) collective-permute-start(bf16[200,768]{1,0:T(8,128)(2,1)} %collective-permute-done.6.refs_6_), channel_id=1, source_target_pairs={{0,1},{1,0},{2,3},{3,2},{4,5},{5,4},{6,7},{7,6},{8,9},{9,8},{10,11... | collective-permute-start | bytes 921608 | tf_op jit(solution)/shard_map/ppermute | solution.py:27
  37.9 5.2 %collective-permute-start.11 = (bf16[200,768]{1,0:T(8,128)(2,1)}, bf16[200,768]{1,0:T(8,128)(2,1)}, u32[]{:S(2)}, u32[]{:S(2)}) collective-permute-start(bf16[200,768]{1,0:T(8,128)(2,1)} %collective-permute-done.10.refs_10_), channel_id=1, source_target_pairs={{0,1},{1,0},{2,3},{3,2},{4,5},{5,4},{6,7},{7,6},{8,9},{9,8},{10,11... | collective-permute-start | bytes 921608 | tf_op jit(solution)/shard_map/ppermute | solution.py:27
  51.1 10.8 %collective-permute-start.16 = (bf16[128,768]{1,0:T(8,128)(2,1)S(1)}, bf16[128,768]{1,0:T(8,128)(2,1)S(1)}, u32[]{:S(2)}, u32[]{:S(2)}) collective-permute-start(bf16[128,768]{1,0:T(8,128)(2,1)S(1)} %get-tuple-element.20), channel_id=1, source_target_pairs={{0,16},{16,0},{1,17},{17,1},{2,18},{18,2},{3,19},{19,3},{4,20},{20... | collective-permute-start | bytes 589832 | tf_op jit(solution)/shard_map/ppermute | solution.py:31
  53.4 15.7 %all-to-all-start = ((bf16[16,16,256]{2,1,0:T(8,128)(2,1)}), bf16[16,16,256]{2,1,0:T(8,128)(2,1)S(1)}, u32[]{:S(2)}, u32[]{:S(2)}) async-start(bf16[16,16,256]{2,1,0:T(8,128)(2,1)} %windows.1), calls=%async_computation | async-start | bytes 262144 | tf_op jit(solution)/shard_map/all_to_all | solution.py:329
  62.4 6.7 %collective-permute-start.26 = (bf16[128,320]{1,0:T(8,128)(2,1)S(1)}, bf16[128,320]{1,0:T(8,128)(2,1)S(1)}, u32[]{:S(2)}, u32[]{:S(2)}) collective-permute-start(bf16[128,320]{1,0:T(8,128)(2,1)S(1)} %get-tuple-element.22.refs_0_), channel_id=1, source_target_pairs={{0,4},{2,6},{4,0},{6,2},{8,12},{10,14},{12,8},{14,10},{1,5},{3,7},... | collective-permute-start | bytes 245768 | tf_op jit(solution)/shard_map/ppermute | solution.py:23
  64.4 8.6 %collective-permute-start.19 = (bf16[128,320]{1,0:T(8,128)(2,1)S(1)}, bf16[128,320]{1,0:T(8,128)(2,1)S(1)}, u32[]{:S(2)}, u32[]{:S(2)}) collective-permute-start(bf16[128,320]{1,0:T(8,128)(2,1)S(1)} %get-tuple-element.22.refs_0_), channel_id=1, source_target_pairs={{0,12},{2,14},{4,8},{6,10},{8,4},{10,6},{12,0},{14,2},{1,13},{3,15... | collective-permute-start | bytes 245768 | tf_op jit(solution)/shard_map/ppermute | solution.py:23
  66.8 7.8 %collective-permute-start.28 = (bf16[128,320]{1,0:T(8,128)(2,1)S(1)}, bf16[128,320]{1,0:T(8,128)(2,1)S(1)}, u32[]{:S(2)}, u32[]{:S(2)}) collective-permute-start(bf16[128,320]{1,0:T(8,128)(2,1)S(1)} %get-tuple-element.22.refs_0_), channel_id=1, source_target_pairs={{0,2},{2,0},{4,6},{6,4},{8,10},{10,8},{12,14},{14,12},{1,3},{3,1},... | collective-permute-start | bytes 245768 | tf_op jit(solution)/shard_map/ppermute | solution.py:23
  68.2 6.3 %collective-permute-start.25 = (bf16[128,320]{1,0:T(8,128)(2,1)S(1)}, bf16[128,320]{1,0:T(8,128)(2,1)S(1)}, u32[]{:S(2)}, u32[]{:S(2)}) collective-permute-start(bf16[128,320]{1,0:T(8,128)(2,1)S(1)} %get-tuple-element.22.refs_0_), channel_id=1, source_target_pairs={{0,1},{1,0},{2,3},{3,2},{4,5},{5,4},{6,7},{7,6},{8,9},{9,8},{10,11... | collective-permute-start | bytes 245768 | tf_op jit(solution)/shard_map/ppermute | solution.py:27
  68.3 8.2 %collective-permute-start.17 = (bf16[128,320]{1,0:T(8,128)(2,1)S(1)}, bf16[128,320]{1,0:T(8,128)(2,1)S(1)}, u32[]{:S(2)}, u32[]{:S(2)}) collective-permute-start(bf16[128,320]{1,0:T(8,128)(2,1)S(1)} %get-tuple-element.22.refs_0_), channel_id=1, source_target_pairs={{0,8},{2,10},{4,12},{6,14},{8,0},{10,2},{12,4},{14,6},{1,9},{3,11}... | collective-permute-start | bytes 245768 | tf_op jit(solution)/shard_map/ppermute | solution.py:23
  72.4 6.1 %collective-permute-start.30 = (bf16[128,320]{1,0:T(8,128)(2,1)S(1)}, bf16[128,320]{1,0:T(8,128)(2,1)S(1)}, u32[]{:S(2)}, u32[]{:S(2)}) collective-permute-start(bf16[128,320]{1,0:T(8,128)(2,1)S(1)} %collective-permute-done.26.refs_2_), channel_id=1, source_target_pairs={{0,2},{2,0},{4,6},{6,4},{8,10},{10,8},{12,14},{14,12},{1,3},{3,1},... | collective-permute-start | bytes 245768 | tf_op jit(solution)/shard_map/ppermute | solution.py:23
  73.0 5.0 %collective-permute-start.33 = (f32[3,1536]{1,0:T(4,128)S(1)}, f32[3,1536]{1,0:T(4,128)S(1)}, u32[]{:S(2)}, u32[]{:S(2)}) collective-permute-start(f32[3,1536]{1,0:T(4,128)S(1)} %add.48), channel_id=1, source_target_pairs={{0,2},{2,0},{4,6},{6,4},{8,10},{10,8},{12,14},{14,12},{1,3},{3,1},... | collective-permute-start | bytes 55304 | tf_op jit(solution)/shard_map/ppermute | solution.py:23
  76.5 5.7 %collective-permute-start.21 = (bf16[128,320]{1,0:T(8,128)(2,1)S(1)}, bf16[128,320]{1,0:T(8,128)(2,1)S(1)}, u32[]{:S(2)}, u32[]{:S(2)}) collective-permute-start(bf16[128,320]{1,0:T(8,128)(2,1)S(1)} %collective-permute-done.17.refs_0_), channel_id=1, source_target_pairs={{0,2},{2,0},{4,6},{6,4},{8,10},{10,8},{12,14},{14,12},{1,3},{3,1},... | collective-permute-start | bytes 245768 | tf_op jit(solution)/shard_map/ppermute | solution.py:23
  78.0 5.3 %collective-permute-start.23 = (bf16[128,320]{1,0:T(8,128)(2,1)S(1)}, bf16[128,320]{1,0:T(8,128)(2,1)S(1)}, u32[]{:S(2)}, u32[]{:S(2)}) collective-permute-start(bf16[128,320]{1,0:T(8,128)(2,1)S(1)} %collective-permute-done.19.refs_2_), channel_id=1, source_target_pairs={{0,2},{2,0},{4,6},{6,4},{8,10},{10,8},{12,14},{14,12},{1,3},{3,1},... | collective-permute-start | bytes 245768 | tf_op jit(solution)/shard_map/ppermute | solution.py:23
  78.6 7.2 %collective-permute-start.31 = (bf16[128,320]{1,0:T(8,128)(2,1)S(1)}, bf16[128,320]{1,0:T(8,128)(2,1)S(1)}, u32[]{:S(2)}, u32[]{:S(2)}) collective-permute-start(bf16[128,320]{1,0:T(8,128)(2,1)S(1)} %collective-permute-done.30.refs_6_), channel_id=1, source_target_pairs={{0,1},{1,0},{2,3},{3,2},{4,5},{5,4},{6,7},{7,6},{8,9},{9,8},{10,11... | collective-permute-start | bytes 245768 | tf_op jit(solution)/shard_map/ppermute | solution.py:27
  78.6 15.1 %collective-permute-start.18 = (bf16[128,320]{1,0:T(8,128)(2,1)S(1)}, bf16[128,320]{1,0:T(8,128)(2,1)S(1)}, u32[]{:S(2)}, u32[]{:S(2)}) collective-permute-start(bf16[128,320]{1,0:T(8,128)(2,1)S(1)} %collective-permute-done.17.refs_0_), channel_id=1, source_target_pairs={{0,1},{1,0},{2,3},{3,2},{4,5},{5,4},{6,7},{7,6},{8,9},{9,8},{10,11... | collective-permute-start | bytes 245768 | tf_op jit(solution)/shard_map/ppermute | solution.py:27
  79.1 14.6 %collective-permute-start.20 = (bf16[128,320]{1,0:T(8,128)(2,1)S(1)}, bf16[128,320]{1,0:T(8,128)(2,1)S(1)}, u32[]{:S(2)}, u32[]{:S(2)}) collective-permute-start(bf16[128,320]{1,0:T(8,128)(2,1)S(1)} %collective-permute-done.19.refs_2_), channel_id=1, source_target_pairs={{0,1},{1,0},{2,3},{3,2},{4,5},{5,4},{6,7},{7,6},{8,9},{9,8},{10,11... | collective-permute-start | bytes 245768 | tf_op jit(solution)/shard_map/ppermute | solution.py:27
  82.1 11.6 %collective-permute-start.22 = (bf16[128,320]{1,0:T(8,128)(2,1)S(1)}, bf16[128,320]{1,0:T(8,128)(2,1)S(1)}, u32[]{:S(2)}, u32[]{:S(2)}) collective-permute-start(bf16[128,320]{1,0:T(8,128)(2,1)S(1)} %collective-permute-done.21.refs_4_), channel_id=1, source_target_pairs={{0,1},{1,0},{2,3},{3,2},{4,5},{5,4},{6,7},{7,6},{8,9},{9,8},{10,11... | collective-permute-start | bytes 245768 | tf_op jit(solution)/shard_map/ppermute | solution.py:27
  83.3 10.4 %collective-permute-start.24 = (bf16[128,320]{1,0:T(8,128)(2,1)S(1)}, bf16[128,320]{1,0:T(8,128)(2,1)S(1)}, u32[]{:S(2)}, u32[]{:S(2)}) collective-permute-start(bf16[128,320]{1,0:T(8,128)(2,1)S(1)} %collective-permute-done.23.refs_6_), channel_id=1, source_target_pairs={{0,1},{1,0},{2,3},{3,2},{4,5},{5,4},{6,7},{7,6},{8,9},{9,8},{10,11... | collective-permute-start | bytes 245768 | tf_op jit(solution)/shard_map/ppermute | solution.py:27
  91.5 10.3 %collective-permute-start.35 = (f32[3,1536]{1,0:T(4,128)S(1)}, f32[3,1536]{1,0:T(4,128)S(1)}, u32[]{:S(2)}, u32[]{:S(2)}) collective-permute-start(f32[3,1536]{1,0:T(4,128)S(1)} %add.50), channel_id=1, source_target_pairs={{0,8},{2,10},{4,12},{6,14},{8,0},{10,2},{12,4},{14,6},{1,9},{3,11}... | collective-permute-start | bytes 55304 | tf_op jit(solution)/shard_map/ppermute | solution.py:23
  (23 other events, 507.9 us)

commit v3 on v2

--- a/solution.py
+++ b/solution.py
@@ -35,36 +35,80 @@
     return lax.optimization_barrier((value, *others))[0]
 
 
-def tokens_kernel(rows, extra, ids_ref, own_ref, partner_ref, *refs):
-    blocks, (own_out, partner_out, tracks_out, x_s, w_s, sems) = refs[:-6], refs[-6:]
+def bring(blocks, rows, extra, low, weight, tracks, sems):
     copies = []
     for at, block in enumerate(blocks):
-        spot = ids_ref[at]
         for which, (first, length, target) in enumerate(
-            ((0, rows, w_s), (rows, extra, tracks_out))
+            (
+                (0, rows, weight.at[pl.ds(pl.multiple_of((low ^ at) * rows, 8), rows)]),
+                (rows, extra, tracks.at[pl.ds(at * extra, extra)]),
+            )
         ):
             copy = pltpu.make_async_copy(
-                block.at[pl.ds(first, length)],
-                target.at[pl.ds(pl.multiple_of(spot * length, 8), length)],
-                sems.at[at, which],
+                block.at[pl.ds(first, length)], target, sems.at[2 * at + which]
             )
             copy.start()
             copies.append(copy)
-    pairs, width = own_ref.shape
+    return copies
+
+
+def first_tokens_kernel(rows, extra, place_ref, own_hbm, partner_hbm, *refs):
+    blocks, refs = refs[:-8], refs[-8:]
+    total_ref, last_ref, tracks_ref, in_s, x_s, w_s, in_sems, block_sems = refs
+    pair = x_s.shape[0]
+    inputs = [
+        pltpu.make_async_copy(ref, in_s.at[part], in_sems.at[part])
+        for part, ref in enumerate((own_hbm, partner_hbm))
+    ]
+    for copy in inputs:
+        copy.start()
+    copies = [
+        bring(
+            blocks[4 * mask : 4 * mask + 4],
+            rows,
+            extra,
+            place_ref[1],
+            w_s.at[mask],
+            tracks_ref.at[pl.ds(4 * mask * extra, 4 * extra)],
+            block_sems.at[mask],
+        )
+        for mask in range(pair - 1)
+    ]
+    pairs, width = in_s.shape[1:]
     half = pairs // 2
+    span = x_s.shape[2]
     line = lax.broadcasted_iota(jnp.int32, (half, pairs), 0)
     column = lax.broadcasted_iota(jnp.int32, (half, pairs), 1)
-    for tap in range(2):
-        pick = (column == 2 * line + tap).astype(jnp.bfloat16)
-        for part, ref in enumerate((own_ref, partner_ref)):
-            x_s[part * half : (part + 1) * half, tap * width : (tap + 1) * width] = jnp.dot(
-                pick, ref[...], preferred_element_type=jnp.float32
-            ).astype(jnp.bfloat16)
-    for copy in copies:
+    for part, copy in enumerate(inputs):
         copy.wait()
-    total = jnp.dot(x_s[...], w_s[...], preferred_element_type=jnp.float32).astype(jnp.bfloat16)
-    own_out[...] = total[:half]
-    partner_out[...] = total[half:]
+        for tap in range(2):
+            pick = (column == 2 * line + tap).astype(jnp.bfloat16)
+            cells = jnp.dot(pick, in_s[part], preferred_element_type=jnp.float32).astype(
+                jnp.bfloat16
+            )
+            for at in range(width // span):
+                x_s[tap * (width // span) + at, part * half : (part + 1) * half, :] = cells[
+                    :, at * span : (at + 1) * span
+                ]
+    total = jnp.zeros(total_ref.shape, jnp.float32)
+    for mask in range(pair - 1):
+        for copy in copies[mask]:
+            copy.wait()
+        total = total + jnp.dot(
+            x_s[place_ref[0] ^ mask], w_s[mask], preferred_element_type=jnp.float32
+        )
+    total_ref[...] = total
+    last_ref[...] = x_s[place_ref[0] ^ (pair - 1)]
+
+
+def last_tokens_kernel(rows, extra, place_ref, total_ref, last_ref, *refs):
+    blocks, (own_ref, partner_ref, tracks_ref, w_s, sems) = refs[:-5], refs[-5:]
+    for copy in bring(blocks, rows, extra, place_ref[1], w_s, tracks_ref, sems):
+        copy.wait()
+    half = own_ref.shape[0]
+    total = total_ref[...] + jnp.dot(last_ref[...], w_s[...], preferred_element_type=jnp.float32)
+    own_ref[...] = total[:half].astype(jnp.bfloat16)
+    partner_ref[...] = total[half:].astype(jnp.bfloat16)
 
 
 def windows_kernel(grad_ref, out_ref):
@@ -122,9 +166,10 @@
         old_top_ref, old_weighted_ref = refs[:2]
         refs = refs[2:]
     if last:
-        tok_ref, outw_ref, out_ref, k_s, v_s, s_s = refs
+        tok_ref, outw_hbm, out_ref, k_s, v_s, s_s, context_s, outw_s, sem = refs
         token_rows = tok_ref.shape[0]
-        total = tok_ref[...].astype(jnp.float32)
+        fetch = pltpu.make_async_copy(outw_hbm, outw_s, sem)
+        fetch.start()
     else:
         top_ref, weighted_ref, k_s, v_s, s_s = refs
     at = 0
@@ -170,38 +215,41 @@
             context = (weighted[:, :VDIM] / weighted[:, VDIM : VDIM + 1]).astype(jnp.bfloat16)
             for j in range(row_block // token_rows):
                 h = r // token_rows + j
-                total = total + jnp.dot(
-                    context[j * token_rows : (j + 1) * token_rows],
-                    outw_ref[h * VDIM : (h + 1) * VDIM, :],
-                    preferred_element_type=jnp.float32,
-                )
+                context_s[:, h * VDIM : (h + 1) * VDIM] = context[
+                    j * token_rows : (j + 1) * token_rows
+                ]
         else:
             top_ref[r : r + row_block, :] = jnp.broadcast_to(top, (row_block, top_ref.shape[1]))
             weighted_ref[r : r + row_block, :] = weighted
     if last:
-        out_ref[...] = total.astype(jnp.bfloat16)
-
-
-def decoder_kernel(extra, tok_ref, grads_ref, chosen_ref, tracks_ref, taps_ref, skip_ref, sums_ref):
+        fetch.wait()
+        added = jnp.dot(context_s[...], outw_s[...], preferred_element_type=jnp.float32)
+        out_ref[...] = (tok_ref[...].astype(jnp.float32) + added).astype(jnp.bfloat16)
+
+
+def decoder_kernel(extra, parts, tok_ref, grads_ref, taps_ref, *refs):
+    chosen_refs, track_refs, (skip_ref, sums_ref) = refs[:parts], refs[parts:-2], refs[-2:]
     token_rows = tok_ref.shape[0]
-    width = tracks_ref.shape[1]
+    width = track_refs[0].shape[1]
     root = math.sqrt(2.0 / math.pi)
-    masked = lax.dot_general(
-        grads_ref[...],
-        chosen_ref[...],
-        (((0,), (0,)), ((), ())),
-        preferred_element_type=jnp.float32,
-    )[: token_rows + 2 * SPAN]
-    column = lax.broadcasted_iota(jnp.int32, masked.shape, 1) % extra
+    masked = [
+        lax.dot_general(
+            grads_ref[...],
+            chosen_ref[...],
+            (((0,), (0,)), ((), ())),
+            preferred_element_type=jnp.float32,
+        )[: token_rows + 2 * SPAN]
+        for chosen_ref in chosen_refs
+    ]
     for side in range(2):
         at = side * width
-        ours = (column < extra // 2) if side == 0 else (column >= extra // 2)
-        rows = jnp.where(ours, masked, 0.0).astype(jnp.bfloat16)
-        head = (
-            jnp.dot(rows, tracks_ref[...], preferred_element_type=jnp.float32)
-            .astype(jnp.bfloat16)
-            .astype(jnp.float32)
-        )
+        head = jnp.zeros((token_rows + 2 * SPAN, width), jnp.float32)
+        for cells, tracks_ref in zip(masked, track_refs):
+            column = lax.broadcasted_iota(jnp.int32, cells.shape, 1) % extra
+            ours = (column < extra // 2) if side == 0 else (column >= extra // 2)
+            rows = jnp.where(ours, cells, 0.0).astype(jnp.bfloat16)
+            head = head + jnp.dot(rows, tracks_ref[...], preferred_element_type=jnp.float32)
+        head = head.astype(jnp.bfloat16).astype(jnp.float32)
         own, later, earlier = (
             head[:token_rows],
             head[token_rows : token_rows + SPAN],
@@ -261,63 +309,88 @@
     group = lax.axis_index("groups")
     me = lax.axis_index("chip") * 2 + lax.axis_index("core")
     shape = lambda *dims, kind=jnp.bfloat16: jax.ShapeDtypeStruct(dims, kind)
-    direct = pair <= 4 and pair & (pair - 1) == 0 and rows % 16 == 0
+    direct = pair == 4 and rows % 16 == 0
 
     own_half = lax.dynamic_slice_in_dim(enc_weight, group * width, width, axis=1)
     packed = jnp.concatenate([own_half, track_weight[:, :width], track_weight[:, width:]], axis=0)
+    partner_input = group_swap(enc_input)
     if direct:
-        lanes = {0: packed}
-        for mask in range(1, pair):
-            lanes[mask] = chip_swap(after(packed, lanes[1]) if mask == 3 else packed, 2 * mask)
-    partner_input = group_swap(enc_input)
+        nears = [packed, chip_swap(packed, 2), chip_swap(packed, 4)]
+        nears.append(chip_swap(after(packed, nears[1]), 6))
+        crossed = [core_swap(near) for near in nears]
+        fars = [chip_swap(near, 1) for near in nears]
+        fars[1], fars[2] = (after(far, crossed[3]) for far in fars[1:3])
+        blocks = [
+            cells
+            for near, other, far in zip(nears, crossed, fars)
+            for cells in (near, other, far, core_swap(far))
+        ]
+        ids = me ^ jnp.arange(count, dtype=jnp.int32)
+    else:
+        ids = jnp.arange(count, dtype=jnp.int32)
 
     lines = -(-tracks // 16) * 16
     windows = call(
         windows_kernel, shape(count, lines, 2 * token_rows), [VMEM], limit=16, name="windows"
     )(track_grad.T)
+    exchanged = lax.all_to_all(
+        after(windows, crossed[0]) if direct else windows, ("chip", "core"), 0, 0, tiled=True
+    )
     slots = jnp.pad(
         track_index.reshape(count, tracks), ((0, 0), (0, lines - tracks)), constant_values=-1
     )
     measured = jnp.pad(track_mask.reshape(count, tracks), ((0, 0), (0, lines - tracks)))
-    columns = jnp.arange(count * extra, dtype=jnp.int32)
-    column_tracks = columns // extra * tracks + columns % tracks
-    chosen = jnp.where(
-        slots.reshape(-1, 1) == column_tracks[None, :],
-        measured.reshape(-1, 1).astype(jnp.bfloat16),
-        0,
-    ).astype(jnp.bfloat16)
+    column_tracks = ids[:, None] * tracks + jnp.arange(extra, dtype=jnp.int32)[None, :] % tracks
+    chosen = [
+        jnp.where(
+            slots.reshape(-1, 1) == part.reshape(1, -1),
+            measured.reshape(-1, 1).astype(jnp.bfloat16),
+            0,
+        ).astype(jnp.bfloat16)
+        for part in ((column_tracks[:-4], column_tracks[-4:]) if direct else (column_tracks,))
+    ]
 
     if direct:
-        blocks = []
-        for mask in range(pair):
-            near = lanes[mask]
-            far = chip_swap(near, 1)
-            blocks += [
-                (4 * mask, near),
-                (4 * mask + 1, core_swap(near)),
-                (4 * mask + 2, far),
-                (4 * mask + 3, core_swap(far)),
-            ]
-        ids = me ^ jnp.array([mask for mask, _ in blocks], jnp.int32)
-        mine, partner, track_rows = call(
-            functools.partial(tokens_kernel, rows, extra),
+        place = jnp.stack([lax.axis_index("chip") // 2, me % 4]).astype(jnp.int32)
+        held = [pltpu.with_memory_space_constraint(block, pltpu.HBM) for block in blocks]
+        span = 4 * rows
+        total, last_cells, first_rows = call(
+            functools.partial(first_tokens_kernel, rows, extra),
             (
-                shape(token_rows, width),
-                shape(token_rows, width),
-                shape(count * extra, width),
+                shape(2 * token_rows, width, kind=jnp.float32),
+                shape(2 * token_rows, span),
+                shape((count - 4) * extra, width),
             ),
-            [SMEM, VMEM, VMEM] + [HBM] * count,
+            [SMEM] + [HBM] * (count - 2),
             scratch=(
-                pltpu.VMEM((2 * token_rows, count * rows), jnp.bfloat16),
-                pltpu.VMEM((count * rows, width), jnp.bfloat16),
-                pltpu.SemaphoreType.DMA((count, 2)),
+                pltpu.VMEM((2,) + enc_input.shape, jnp.bfloat16),
+                pltpu.VMEM((pair, 2 * token_rows, span), jnp.bfloat16),
+                pltpu.VMEM((pair - 1, span, width), jnp.bfloat16),
+                pltpu.SemaphoreType.DMA((2,)),
+                pltpu.SemaphoreType.DMA((pair - 1, 8)),
             ),
             limit=16,
-            name="tokens",
-        )(ids, enc_input, partner_input, *[pltpu.with_memory_space_constraint(block, pltpu.HBM) for _, block in blocks])
+            name="first_tokens",
+        )(
+            place,
+            *[
+                pltpu.with_memory_space_constraint(cells, pltpu.HBM)
+                for cells in (enc_input, partner_input)
+            ],
+            *held[:-4],
+        )
+        mine, partner, last_rows = call(
+            functools.partial(last_tokens_kernel, rows, extra),
+            (shape(token_rows, width), shape(token_rows, width), shape(4 * extra, width)),
+            [SMEM] + [VMEM] * 2 + [HBM] * 4,
+            scratch=(pltpu.VMEM((span, width), jnp.bfloat16), pltpu.SemaphoreType.DMA((8,))),
+            limit=12,
+            name="last_tokens",
+        )(place, total, last_cells, *held[-4:])
+        track_rows = [first_rows, last_rows]
     else:
         gathered = lax.all_gather(packed, ("chip", "core"), axis=0)
-        track_rows = gathered[:, rows:].reshape(count * extra, width)
+        track_rows = [gathered[:, rows:].reshape(count * extra, width)]
         weight = gathered[:, :rows].reshape(count * rows, width)
         mine, partner = (
             jnp.dot(
@@ -326,7 +399,6 @@
             for cells in (enc_input, partner_input)
         )
     theirs = group_swap(partner)
-    exchanged = lax.all_to_all(after(windows, partner), ("chip", "core"), 0, 0, tiled=True)
     tokens, normed, keyval = call(
         keyval_kernel,
         (shape(token_rows, dim), shape(token_rows, dim), shape(token_rows, QK + VDIM)),
@@ -338,32 +410,50 @@
     if direct:
         nears = [chip_swap(keyval, 2 * mask) if mask else keyval for mask in range(pair)]
         fars = [chip_swap(near, 1) for near in nears]
-        cut = max(1, pair // 2)
+        crossed = [core_swap(near) for near in nears]
         stages = [
-            [cells for piece in side for cells in (piece, core_swap(piece))]
-            for side in (nears[:cut] + fars[:cut], nears[cut:] + fars[cut:])
-            if side
+            [
+                cells
+                for mask in masks
+                for cells in (nears[mask], crossed[mask], fars[mask], core_swap(fars[mask]))
+            ]
+            for masks in ((0, 1), (2, 3))
         ]
     else:
-        nears = fars = [lax.all_gather(keyval, ("chip", "core"), axis=0, tiled=True)]
+        nears = crossed = [lax.all_gather(keyval, ("chip", "core"), axis=0, tiled=True)]
         stages = [nears]
 
     query = call(query_kernel, shape(HEADS * token_rows, QK), [VMEM] * 2, limit=8, name="query")(
         normed, q_weight
     )
     skip_grad, sums = call(
-        functools.partial(decoder_kernel, extra),
+        functools.partial(decoder_kernel, extra, len(chosen)),
         (shape(token_rows, dim), shape(3, dim, kind=jnp.float32)),
-        [VMEM] * 5,
+        [VMEM] * (3 + 2 * len(chosen)),
         limit=16,
         name="decoder",
-    )(after(tokens, nears[min(1, len(nears) - 1)]), exchanged.reshape(count * lines, 2 * token_rows), chosen, track_rows, dec_weight)
+    )(
+        after(tokens, nears[-1], query),
+        exchanged.reshape(count * lines, 2 * token_rows),
+        dec_weight,
+        *chosen,
+        *track_rows,
+    )
+    sums = sums + core_swap(sums)
+    step = 1
+    while step < chips:
+        sums = sums + chip_swap(after(sums, crossed[-1]) if step == 2 else sums, step)
+        step *= 2
+    dec_weight_grad = sums / jnp.float32(math.sqrt(token_rows * count))
+
     row_block = 2 * token_rows if direct else token_rows
     state = []
     for turn, pieces in enumerate(stages):
         last = turn + 1 == len(stages)
         keys = sum(piece.shape[0] for piece in pieces)
-        extras = [tokens, out_weight] if last else []
+        extras = (
+            [tokens, pltpu.with_memory_space_constraint(out_weight, pltpu.HBM)] if last else []
+        )
         held = (
             shape(token_rows, dim)
             if last
@@ -375,25 +465,24 @@
         state = call(
             functools.partial(attention_kernel, row_block, 512, len(pieces), turn == 0, last),
             held,
-            [VMEM] * (1 + len(pieces) + len(state) + len(extras)),
+            [VMEM] * (1 + len(pieces) + len(state)) + ([VMEM, HBM] if last else []),
             scratch=(
                 pltpu.VMEM((keys, QK), jnp.bfloat16),
                 pltpu.VMEM((keys, 256), jnp.bfloat16),
                 pltpu.VMEM((2, row_block, keys), jnp.float32),
+            )
+            + (
+                (
+                    pltpu.VMEM((token_rows, HEADS * VDIM), jnp.bfloat16),
+                    pltpu.VMEM(out_weight.shape, jnp.bfloat16),
+                    pltpu.SemaphoreType.DMA(()),
+                )
+                if last
+                else ()
             ),
-            limit=60 if len(stages) == 1 else 12,
+            limit=60 if len(stages) == 1 else 16,
             name="attention",
         )(query, *pieces, *state, *extras)
-        if turn == 0:
-            scored = state
-    sums = sums + core_swap(sums)
-    waits = [nears[-1], scored if direct else nears[-1]]
-    step = 1
-    while step < chips:
-        held = after(sums, waits.pop(0)) if waits and len(stages) > 1 else sums
-        sums = sums + chip_swap(held, step)
-        step *= 2
-    dec_weight_grad = sums / jnp.float32(math.sqrt(token_rows * count))
     return (state, skip_grad, dec_weight_grad)
 
 

time: 103 us -> 113 us (1.097)
  waiting for transfers between devices: 37.2 us -> 43.6 us
  Pallas kernels: 16.2 us -> 21 us
    ppermute x17, waiting for transfers between devices: 34.4 us -> 41.2 us  [chip_swap(): return lax.ppermute(cells, 'chip', [(i, i ^ mask) for i in range(count)])]
    pallas_call x2 -> x3, Pallas kernels: 6.91 us -> 9.72 us  [the longest x1 5.3 us: shards(): call(functools.partial(first_tokens_kernel, rows, extra), (shape(2 * toke...]
    all_to_all x1, starting transfers between devices: 6.43 us -> 3.76 us  [shards(): lax.all_to_all(after(windows, crossed[0]) if direct else windows, ('chip'...]
    ppermute x17, starting transfers between devices: 26.3 us -> 28.3 us  [chip_swap(): return lax.ppermute(cells, 'chip', [(i, i ^ mask) for i in range(count)])]
    ppermute x17, waiting for transfers between devices: 2.74 us -> 0.89 us  [core_swap(): return lax.ppermute(cells, 'core', [(0, 1), (1, 0)])]
    ppermute x2, waiting for transfers between devices: 0.01 us -> 1.51 us  [group_swap(): return lax.ppermute(cells, 'groups', [(0, 1), (1, 0)])]
    pallas_call x2, Pallas kernels: 7.43 us -> 8.71 us  [shards(): call(functools.partial(attention_kernel, row_block, 512, len(pieces), tur...]
    unnamed x36 -> x32, local copies, waits for them, and re-layouts: 5.55 us -> 6.09 us
  transfers between devices with their start and end apart: 37 -> 37, of which waited for: 12 -> 13; matrix products, arithmetic and copies ran while one was open for 3% -> 2% of each run, Pallas kernels for 11% -> 11%
where the time goes in v3:
time: 113 us
  waiting for transfers between devices  43.6 us (39%)
  starting transfers between devices  37.5 us (33%)
  Pallas kernels  21 us (19%)
  local copies, waits for them, and re-layouts  8.2 us (7%)
  between operations  1.17 us (1%)
    ppermute x17, waiting for transfers between devices, chip_swap(): return lax.ppermute(cells, 'chip', [(i, i ^ mask) for i in range(count)])  41.2 us
    ppermute x17, starting transfers between devices, chip_swap(): return lax.ppermute(cells, 'chip', [(i, i ^ mask) for i in range(count)])  28.3 us
    pallas_call x2, Pallas kernels, shards(): call(functools.partial(attention_kernel, row_block, 512, len(pieces), tur...  8.71 us
    unnamed x32, local copies, waits for them, and re-layouts  6.09 us
    pallas_call x1, Pallas kernels, shards(): call(functools.partial(first_tokens_kernel, rows, extra), (shape(2 * toke...  5.3 us
    all_to_all x1, starting transfers between devices, shards(): lax.all_to_all(after(windows, crossed[0]) if direct else windows, ('chip'...  3.76 us
    ppermute x2, starting transfers between devices, group_swap(): return lax.ppermute(cells, 'groups', [(0, 1), (1, 0)])  2.89 us
    ppermute x17, starting transfers between devices, core_swap(): return lax.ppermute(cells, 'core', [(0, 1), (1, 0)])  2.51 us
  transfers between devices with their start and end apart: 37, of which 13 were waited for; matrix products, arithmetic and copies ran while one was open for 2% of the time, Pallas kernels for 11%

profile of v3, /device:TPU:0, one launch (start us, length us, event | category | flops | bytes accessed | tf_op | source)
XLA Modules:
  0.0 112.5 jit_solution(14919988389915776489)
XLA Ops:
  1.8 3.1 %collective-permute-start.4 = (bf16[200,768]{1,0:T(8,128)(2,1)S(1)}, bf16[200,768]{1,0:T(8,128)(2,1)S(1)}, u32[]{:S(2)}, u32[]{:S(2)}) collective-permute-start(bf16[200,768]{1,0:T(8,128)(2,1)S(1)} %pad_maximum_fusion.refs_0_), channel_id=1, source_target_pairs={{0,4},{2,6},{4,0},{6,2},{8,12},{10,14},{12,8},{14,10},{1,5},{3,7},... | collective-permute-start | bytes 921608 | tf_op jit(solution)/shard_map/ppermute | solution.py:23
  4.9 2.6 %collective-permute-start.10 = (bf16[200,768]{1,0:T(8,128)(2,1)S(1)}, bf16[200,768]{1,0:T(8,128)(2,1)}, u32[]{:S(2)}, u32[]{:S(2)}) collective-permute-start(bf16[200,768]{1,0:T(8,128)(2,1)S(1)} %pad_maximum_fusion.refs_0_), channel_id=1, source_target_pairs={{0,8},{2,10},{4,12},{6,14},{8,0},{10,2},{12,4},{14,6},{1,9},{3,11}... | collective-permute-start | bytes 921608 | tf_op jit(solution)/shard_map/ppermute | solution.py:23
  7.5 11.1 %collective-permute-done.4.refs_4_ = bf16[200,768]{1,0:T(8,128)(2,1)S(1)} collective-permute-done((bf16[200,768]{1,0:T(8,128)(2,1)S(1)}, bf16[200,768]{1,0:T(8,128)(2,1)S(1)}, u32[]{:S(2)}, u32[]{:S(2)}) %collective-permute-start.4) | collective-permute-done | bytes 307232 | tf_op jit(solution)/shard_map/ppermute | solution.py:23
  18.6 2.6 %collective-permute-start.7 = (bf16[200,768]{1,0:T(8,128)(2,1)S(1)}, bf16[200,768]{1,0:T(8,128)(2,1)S(1)}, u32[]{:S(2)}, u32[]{:S(2)}) collective-permute-start(bf16[200,768]{1,0:T(8,128)(2,1)S(1)} %pad_maximum_fusion.refs_0_), channel_id=1, source_target_pairs={{0,12},{2,14},{4,8},{6,10},{8,4},{10,6},{12,0},{14,2},{1,13},{3,15... | collective-permute-start | bytes 921608 | tf_op jit(solution)/shard_map/ppermute | solution.py:23
  21.3 1.5 %collective-permute-start.2 = (bf16[200,768]{1,0:T(8,128)(2,1)S(1)}, bf16[200,768]{1,0:T(8,128)(2,1)}, u32[]{:S(2)}, u32[]{:S(2)}) collective-permute-start(bf16[200,768]{1,0:T(8,128)(2,1)S(1)} %pad_maximum_fusion.refs_0_), channel_id=1, source_target_pairs={{0,2},{2,0},{4,6},{6,4},{8,10},{10,8},{12,14},{14,12},{1,3},{3,1},... | collective-permute-start | bytes 921608 | tf_op jit(solution)/shard_map/ppermute | solution.py:23
  23.3 1.5 %collective-permute-start.12 = (bf16[200,768]{1,0:T(8,128)(2,1)}, bf16[200,768]{1,0:T(8,128)(2,1)}, u32[]{:S(2)}, u32[]{:S(2)}) collective-permute-start(bf16[200,768]{1,0:T(8,128)(2,1)} %collective-permute-done.10.refs_8_), channel_id=1, source_target_pairs={{0,2},{2,0},{4,6},{6,4},{8,10},{10,8},{12,14},{14,12},{1,3},{3,1},... | collective-permute-start | bytes 921608 | tf_op jit(solution)/shard_map/ppermute | solution.py:23
  24.8 4.3 %collective-permute-done.7.refs_0_ = bf16[200,768]{1,0:T(8,128)(2,1)S(1)} collective-permute-done((bf16[200,768]{1,0:T(8,128)(2,1)S(1)}, bf16[200,768]{1,0:T(8,128)(2,1)S(1)}, u32[]{:S(2)}, u32[]{:S(2)}) %collective-permute-start.7) | collective-permute-done | bytes 307232 | tf_op jit(solution)/shard_map/ppermute | solution.py:23
  29.1 1.3 %collective-permute-start = (bf16[256,1408]{1,0:T(8,128)(2,1)}, bf16[256,1408]{1,0:T(8,128)(2,1)S(1)}, u32[]{:S(2)}, u32[]{:S(2)}) collective-permute-start(bf16[256,1408]{1,0:T(8,128)(2,1)} %own_hbm.1), channel_id=1, source_target_pairs={{0,16},{16,0},{1,17},{17,1},{2,18},{18,2},{3,19},{19,3},{4,20},{20... | collective-permute-start | bytes 2162696 | tf_op jit(solution)/shard_map/ppermute | solution.py:31
  31.6 6.6 %collective-permute-done.6.refs_6_ = bf16[200,768]{1,0:T(8,128)(2,1)} collective-permute-done((bf16[200,768]{1,0:T(8,128)(2,1)S(1)}, bf16[200,768]{1,0:T(8,128)(2,1)}, u32[]{:S(2)}, u32[]{:S(2)}) %collective-permute-start.6) | collective-permute-done | bytes 307232 | tf_op jit(solution)/shard_map/ppermute | solution.py:23
  38.2 4.3 %collective-permute-done.12.refs_10_ = bf16[200,768]{1,0:T(8,128)(2,1)} collective-permute-done((bf16[200,768]{1,0:T(8,128)(2,1)}, bf16[200,768]{1,0:T(8,128)(2,1)}, u32[]{:S(2)}, u32[]{:S(2)}) %collective-permute-start.12) | collective-permute-done | bytes 307232 | tf_op jit(solution)/shard_map/ppermute | solution.py:23
  43.3 1.5 %collective-permute-start.14 = (bf16[200,768]{1,0:T(8,128)(2,1)S(1)}, bf16[200,768]{1,0:T(8,128)(2,1)}, u32[]{:S(2)}, u32[]{:S(2)}) collective-permute-start(bf16[200,768]{1,0:T(8,128)(2,1)S(1)} %collective-permute-done.7.refs_0_), channel_id=1, source_target_pairs={{0,2},{2,0},{4,6},{6,4},{8,10},{10,8},{12,14},{14,12},{1,3},{3,1},... | collective-permute-start | bytes 921608 | tf_op jit(solution)/shard_map/ppermute | solution.py:23
  47.8 5.2 %collective-permute-done.14.refs_2_ = bf16[200,768]{1,0:T(8,128)(2,1)} collective-permute-done((bf16[200,768]{1,0:T(8,128)(2,1)S(1)}, bf16[200,768]{1,0:T(8,128)(2,1)}, u32[]{:S(2)}, u32[]{:S(2)}) %collective-permute-start.14) | collective-permute-done | bytes 307232 | tf_op jit(solution)/shard_map/ppermute | solution.py:23
  54.9 5.3 %first_tokens.1 = (f32[256,768]{1,0:T(8,128)S(1)}, bf16[256,704]{1,0:T(8,128)(2,1)S(1)}, bf16[288,768]{1,0:T(8,128)(2,1)S(1)}) custom-call(s32[2]{0:T(128)S(1)} %pad_add_fusion.place_ref, bf16[256,1408]{1,0:T(8,128)(2,1)} %own_hbm.1, bf16[256,1408]{1,0:T(8,128)(2,1)} %copy-done.6, bf16[200,768]{1,0:T(8,128)(2,1)} %copy-done.5, ...), custom_call_target="tpu_custom_call" | custom-call | tf_op jit(solution)/shard_map/first_tokens/pallas_call | solution.py:357
  61.0 2.3 %last_tokens.1 = (bf16[128,768]{1,0:T(8,128)(2,1)S(1)}, bf16[128,768]{1,0:T(8,128)(2,1)S(1)}, bf16[96,768]{1,0:T(8,128)(2,1)S(1)}) custom-call(s32[2]{0:T(128)S(1)} %pad_add_fusion.place_ref, f32[256,768]{1,0:T(8,128)S(1)} %get-tuple-element.25.total_ref, bf16[256,704]{1,0:T(8,128)(2,1)S(1)} %get-tuple-element.26.last_ref, bf16[200,768]{1,0:T(8,128)(2,1)} %copy-done.7, ...), custom_call_target="tpu_custom_call" | custom-call | tf_op jit(solution)/shard_map/last_tokens/pallas_call | solution.py:382
  63.3 1.6 %collective-permute-start.16 = (bf16[128,768]{1,0:T(8,128)(2,1)S(1)}, bf16[128,768]{1,0:T(8,128)(2,1)S(1)}, u32[]{:S(2)}, u32[]{:S(2)}) collective-permute-start(bf16[128,768]{1,0:T(8,128)(2,1)S(1)} %get-tuple-element.28), channel_id=1, source_target_pairs={{0,16},{16,0},{1,17},{17,1},{2,18},{18,2},{3,19},{19,3},{4,20},{20... | collective-permute-start | bytes 589832 | tf_op jit(solution)/shard_map/ppermute | solution.py:31
  65.4 3.8 %all-to-all-start = ((bf16[16,16,256]{2,1,0:T(8,128)(2,1)}), bf16[16,16,256]{2,1,0:T(8,128)(2,1)S(1)}, u32[]{:S(2)}, u32[]{:S(2)}) async-start(bf16[16,16,256]{2,1,0:T(8,128)(2,1)} %windows.1), calls=%async_computation | async-start | bytes 262144 | tf_op jit(solution)/shard_map/all_to_all | solution.py:336
  69.2 1.5 %collective-permute-done.16.theirs_ref = bf16[128,768]{1,0:T(8,128)(2,1)S(1)} collective-permute-done((bf16[128,768]{1,0:T(8,128)(2,1)S(1)}, bf16[128,768]{1,0:T(8,128)(2,1)S(1)}, u32[]{:S(2)}, u32[]{:S(2)}) %collective-permute-start.16) | collective-permute-done | bytes 196640 | tf_op jit(solution)/shard_map/ppermute | solution.py:31
  71.9 2.2 %collective-permute-start.21 = (bf16[128,320]{1,0:T(8,128)(2,1)}, bf16[128,320]{1,0:T(8,128)(2,1)S(1)}, u32[]{:S(2)}, u32[]{:S(2)}) collective-permute-start(bf16[128,320]{1,0:T(8,128)(2,1)} %get-tuple-element.30.refs_0_), channel_id=1, source_target_pairs={{0,12},{2,14},{4,8},{6,10},{8,4},{10,6},{12,0},{14,2},{1,13},{3,15... | collective-permute-start | bytes 245768 | tf_op jit(solution)/shard_map/ppermute | solution.py:23
  74.4 1.5 %collective-permute-start.26 = (bf16[128,320]{1,0:T(8,128)(2,1)}, bf16[128,320]{1,0:T(8,128)(2,1)S(1)}, u32[]{:S(2)}, u32[]{:S(2)}) collective-permute-start(bf16[128,320]{1,0:T(8,128)(2,1)} %get-tuple-element.30.refs_0_), channel_id=1, source_target_pairs={{0,2},{2,0},{4,6},{6,4},{8,10},{10,8},{12,14},{14,12},{1,3},{3,1},... | collective-permute-start | bytes 245768 | tf_op jit(solution)/shard_map/ppermute | solution.py:23
  75.9 2.1 %collective-permute-start.17 = (bf16[128,320]{1,0:T(8,128)(2,1)}, bf16[128,320]{1,0:T(8,128)(2,1)S(1)}, u32[]{:S(2)}, u32[]{:S(2)}) collective-permute-start(bf16[128,320]{1,0:T(8,128)(2,1)} %get-tuple-element.30.refs_0_), channel_id=1, source_target_pairs={{0,8},{2,10},{4,12},{6,14},{8,0},{10,2},{12,4},{14,6},{1,9},{3,11}... | collective-permute-start | bytes 245768 | tf_op jit(solution)/shard_map/ppermute | solution.py:23
  78.1 1.4 %collective-permute-done.21.refs_4_ = bf16[128,320]{1,0:T(8,128)(2,1)S(1)} collective-permute-done((bf16[128,320]{1,0:T(8,128)(2,1)}, bf16[128,320]{1,0:T(8,128)(2,1)S(1)}, u32[]{:S(2)}, u32[]{:S(2)}) %collective-permute-start.21) | collective-permute-done | bytes 81952 | tf_op jit(solution)/shard_map/ppermute | solution.py:23
  79.6 1.9 %copy-done.1 = bf16[1536,1024]{1,0:T(8,128)(2,1)S(1)} copy-done((bf16[1536,1024]{1,0:T(8,128)(2,1)S(1)}, bf16[1536,1024]{1,0:T(8,128)(2,1)}, u32[]{:S(2)}) %copy-start.1) | copy-done | bytes 3145752
  82.1 2.1 %decoder.1 = (bf16[128,1536]{1,0:T(8,128)(2,1)}, f32[3,1536]{1,0:T(4,128)S(1)}) custom-call(bf16[128,1536]{1,0:T(8,128)(2,1)S(1)} %get-tuple-element.34.refs_10_.tok_ref, bf16[256,256]{1,0:T(8,128)(2,1)S(1)} %bitcast.8, f32[3,1536]{1,0:T(4,128)S(1)} %copy-done.4, bf16[256,288]{1,0:T(8,128)(2,1)S(1)} %compare_select_fusion.refs_0_, ...), custom_call_target="tpu_custom_call" | custom-call | tf_op jit(solution)/shard_map/decoder/pallas_call | solution.py:429
  85.5 1.6 %collective-permute-start.33 = (f32[3,1536]{1,0:T(4,128)S(1)}, f32[3,1536]{1,0:T(4,128)S(1)}, u32[]{:S(2)}, u32[]{:S(2)}) collective-permute-start(f32[3,1536]{1,0:T(4,128)S(1)} %add.58), channel_id=1, source_target_pairs={{0,2},{2,0},{4,6},{6,4},{8,10},{10,8},{12,14},{14,12},{1,3},{3,1},... | collective-permute-start | bytes 55304 | tf_op jit(solution)/shard_map/ppermute | solution.py:23
  87.1 2.3 %collective-permute-done.33 = f32[3,1536]{1,0:T(4,128)S(1)} collective-permute-done((f32[3,1536]{1,0:T(4,128)S(1)}, f32[3,1536]{1,0:T(4,128)S(1)}, u32[]{:S(2)}, u32[]{:S(2)}) %collective-permute-start.33) | collective-permute-done | bytes 18464 | tf_op jit(solution)/shard_map/ppermute | solution.py:23
  89.4 3.3 %collective-permute-start.34 = (f32[3,1536]{1,0:T(4,128)S(1)}, f32[3,1536]{1,0:T(4,128)S(1)}, u32[]{:S(2)}, u32[]{:S(2)}) collective-permute-start(f32[3,1536]{1,0:T(4,128)S(1)} %add.59), channel_id=1, source_target_pairs={{0,4},{2,6},{4,0},{6,2},{8,12},{10,14},{12,8},{14,10},{1,5},{3,7},... | collective-permute-start | bytes 55304 | tf_op jit(solution)/shard_map/ppermute | solution.py:23
  92.8 2.0 %collective-permute-start.30 = (bf16[128,320]{1,0:T(8,128)(2,1)S(1)}, bf16[128,320]{1,0:T(8,128)(2,1)S(1)}, u32[]{:S(2)}, u32[]{:S(2)}) collective-permute-start(bf16[128,320]{1,0:T(8,128)(2,1)S(1)} %collective-permute-done.28.refs_4_), channel_id=1, source_target_pairs={{0,2},{2,0},{4,6},{6,4},{8,10},{10,8},{12,14},{14,12},{1,3},{3,1},... | collective-permute-start | bytes 245768 | tf_op jit(solution)/shard_map/ppermute | solution.py:23
  95.4 1.7 %collective-permute-start.23 = (bf16[128,320]{1,0:T(8,128)(2,1)S(1)}, bf16[128,320]{1,0:T(8,128)(2,1)S(1)}, u32[]{:S(2)}, u32[]{:S(2)}) collective-permute-start(bf16[128,320]{1,0:T(8,128)(2,1)S(1)} %collective-permute-done.21.refs_4_), channel_id=1, source_target_pairs={{0,2},{2,0},{4,6},{6,4},{8,10},{10,8},{12,14},{14,12},{1,3},{3,1},... | collective-permute-start | bytes 245768 | tf_op jit(solution)/shard_map/ppermute | solution.py:23
  98.9 1.8 %collective-permute-done.19.refs_2_ = bf16[128,320]{1,0:T(8,128)(2,1)S(1)} collective-permute-done((bf16[128,320]{1,0:T(8,128)(2,1)S(1)}, bf16[128,320]{1,0:T(8,128)(2,1)S(1)}, u32[]{:S(2)}, u32[]{:S(2)}) %collective-permute-start.19) | collective-permute-done | bytes 81952 | tf_op jit(solution)/shard_map/ppermute | solution.py:23
  100.8 1.7 %collective-permute-done.23.refs_6_ = bf16[128,320]{1,0:T(8,128)(2,1)S(1)} collective-permute-done((bf16[128,320]{1,0:T(8,128)(2,1)S(1)}, bf16[128,320]{1,0:T(8,128)(2,1)S(1)}, u32[]{:S(2)}, u32[]{:S(2)}) %collective-permute-start.23) | collective-permute-done | bytes 81952 | tf_op jit(solution)/shard_map/ppermute | solution.py:23
  103.6 2.6 %attention.2 = (f32[1024,128]{1,0:T(8,128)S(1)}, f32[1024,256]{1,0:T(8,128)S(1)}) custom-call(bf16[1024,128]{1,0:T(8,128)(2,1)S(1)} %query.1.query_ref, bf16[128,320]{1,0:T(8,128)(2,1)} %get-tuple-element.30.refs_0_, bf16[128,320]{1,0:T(8,128)(2,1)S(1)} %collective-permute-done.25.refs_1_, bf16[128,320]{1,0:T(8,128)(2,1)S(1)} %collective-permute-done.26.refs_2_, ...), custom_call_target="tpu_custom_call" | custom-call | tf_op jit(solution)/shard_map/attention/pallas_call | solution.py:465
  106.3 6.1 %attention.3 = bf16[128,1536]{1,0:T(8,128)(2,1)} custom-call(bf16[1024,128]{1,0:T(8,128)(2,1)S(1)} %query.1.query_ref, bf16[128,320]{1,0:T(8,128)(2,1)S(1)} %collective-permute-done.17.refs_0_, bf16[128,320]{1,0:T(8,128)(2,1)S(1)} %collective-permute-done.18.refs_1_, bf16[128,320]{1,0:T(8,128)(2,1)S(1)} %collective-permute-done.19.refs_2_, ...), custom_call_target="tpu_custom_call" | custom-call | tf_op jit(solution)/shard_map/attention/pallas_call | solution.py:465
  (106 shorter events, 16.7 us)
Async XLA Ops:
  1.8 16.8 %collective-permute-start.4 = (bf16[200,768]{1,0:T(8,128)(2,1)S(1)}, bf16[200,768]{1,0:T(8,128)(2,1)S(1)}, u32[]{:S(2)}, u32[]{:S(2)}) collective-permute-start(bf16[200,768]{1,0:T(8,128)(2,1)S(1)} %pad_maximum_fusion.refs_0_), channel_id=1, source_target_pairs={{0,4},{2,6},{4,0},{6,2},{8,12},{10,14},{12,8},{14,10},{1,5},{3,7},... | collective-permute-start | bytes 921608 | tf_op jit(solution)/shard_map/ppermute | solution.py:23
  4.9 18.4 %collective-permute-start.10 = (bf16[200,768]{1,0:T(8,128)(2,1)S(1)}, bf16[200,768]{1,0:T(8,128)(2,1)}, u32[]{:S(2)}, u32[]{:S(2)}) collective-permute-start(bf16[200,768]{1,0:T(8,128)(2,1)S(1)} %pad_maximum_fusion.refs_0_), channel_id=1, source_target_pairs={{0,8},{2,10},{4,12},{6,14},{8,0},{10,2},{12,4},{14,6},{1,9},{3,11}... | collective-permute-start | bytes 921608 | tf_op jit(solution)/shard_map/ppermute | solution.py:23
  18.6 10.5 %collective-permute-start.7 = (bf16[200,768]{1,0:T(8,128)(2,1)S(1)}, bf16[200,768]{1,0:T(8,128)(2,1)S(1)}, u32[]{:S(2)}, u32[]{:S(2)}) collective-permute-start(bf16[200,768]{1,0:T(8,128)(2,1)S(1)} %pad_maximum_fusion.refs_0_), channel_id=1, source_target_pairs={{0,12},{2,14},{4,8},{6,10},{8,4},{10,6},{12,0},{14,2},{1,13},{3,15... | collective-permute-start | bytes 921608 | tf_op jit(solution)/shard_map/ppermute | solution.py:23
  21.3 10.3 %collective-permute-start.2 = (bf16[200,768]{1,0:T(8,128)(2,1)S(1)}, bf16[200,768]{1,0:T(8,128)(2,1)}, u32[]{:S(2)}, u32[]{:S(2)}) collective-permute-start(bf16[200,768]{1,0:T(8,128)(2,1)S(1)} %pad_maximum_fusion.refs_0_), channel_id=1, source_target_pairs={{0,2},{2,0},{4,6},{6,4},{8,10},{10,8},{12,14},{14,12},{1,3},{3,1},... | collective-permute-start | bytes 921608 | tf_op jit(solution)/shard_map/ppermute | solution.py:23
  22.8 15.4 %collective-permute-start.6 = (bf16[200,768]{1,0:T(8,128)(2,1)S(1)}, bf16[200,768]{1,0:T(8,128)(2,1)}, u32[]{:S(2)}, u32[]{:S(2)}) collective-permute-start(bf16[200,768]{1,0:T(8,128)(2,1)S(1)} %collective-permute-done.4.refs_4_), channel_id=1, source_target_pairs={{0,2},{2,0},{4,6},{6,4},{8,10},{10,8},{12,14},{14,12},{1,3},{3,1},... | collective-permute-start | bytes 921608 | tf_op jit(solution)/shard_map/ppermute | solution.py:23
  23.3 19.2 %collective-permute-start.12 = (bf16[200,768]{1,0:T(8,128)(2,1)}, bf16[200,768]{1,0:T(8,128)(2,1)}, u32[]{:S(2)}, u32[]{:S(2)}) collective-permute-start(bf16[200,768]{1,0:T(8,128)(2,1)} %collective-permute-done.10.refs_8_), channel_id=1, source_target_pairs={{0,2},{2,0},{4,6},{6,4},{8,10},{10,8},{12,14},{14,12},{1,3},{3,1},... | collective-permute-start | bytes 921608 | tf_op jit(solution)/shard_map/ppermute | solution.py:23
  29.1 13.4 %collective-permute-start.8 = (bf16[200,768]{1,0:T(8,128)(2,1)S(1)}, bf16[200,768]{1,0:T(8,128)(2,1)S(1)}, u32[]{:S(2)}, u32[]{:S(2)}) collective-permute-start(bf16[200,768]{1,0:T(8,128)(2,1)S(1)} %collective-permute-done.7.refs_0_), channel_id=1, source_target_pairs={{0,1},{1,0},{2,3},{3,2},{4,5},{5,4},{6,7},{7,6},{8,9},{9,8},{10,11... | collective-permute-start | bytes 921608 | tf_op jit(solution)/shard_map/ppermute | solution.py:27
  29.1 24.1 %collective-permute-start = (bf16[256,1408]{1,0:T(8,128)(2,1)}, bf16[256,1408]{1,0:T(8,128)(2,1)S(1)}, u32[]{:S(2)}, u32[]{:S(2)}) collective-permute-start(bf16[256,1408]{1,0:T(8,128)(2,1)} %own_hbm.1), channel_id=1, source_target_pairs={{0,16},{16,0},{1,17},{17,1},{2,18},{18,2},{3,19},{19,3},{4,20},{20... | collective-permute-start | bytes 2162696 | tf_op jit(solution)/shard_map/ppermute | solution.py:31
  31.6 15.5 %collective-permute-start.1 = (bf16[200,768]{1,0:T(8,128)(2,1)S(1)}, bf16[200,768]{1,0:T(8,128)(2,1)}, u32[]{:S(2)}, u32[]{:S(2)}) collective-permute-start(bf16[200,768]{1,0:T(8,128)(2,1)S(1)} %pad_maximum_fusion.refs_0_), channel_id=1, source_target_pairs={{0,1},{1,0},{2,3},{3,2},{4,5},{5,4},{6,7},{7,6},{8,9},{9,8},{10,11... | collective-permute-start | bytes 921608 | tf_op jit(solution)/shard_map/ppermute | solution.py:27
  38.2 9.2 %collective-permute-start.5 = (bf16[200,768]{1,0:T(8,128)(2,1)S(1)}, bf16[200,768]{1,0:T(8,128)(2,1)}, u32[]{:S(2)}, u32[]{:S(2)}) collective-permute-start(bf16[200,768]{1,0:T(8,128)(2,1)S(1)} %collective-permute-done.4.refs_4_), channel_id=1, source_target_pairs={{0,1},{1,0},{2,3},{3,2},{4,5},{5,4},{6,7},{7,6},{8,9},{9,8},{10,11... | collective-permute-start | bytes 921608 | tf_op jit(solution)/shard_map/ppermute | solution.py:27
  42.5 5.1 %collective-permute-start.11 = (bf16[200,768]{1,0:T(8,128)(2,1)}, bf16[200,768]{1,0:T(8,128)(2,1)}, u32[]{:S(2)}, u32[]{:S(2)}) collective-permute-start(bf16[200,768]{1,0:T(8,128)(2,1)} %collective-permute-done.10.refs_8_), channel_id=1, source_target_pairs={{0,1},{1,0},{2,3},{3,2},{4,5},{5,4},{6,7},{7,6},{8,9},{9,8},{10,11... | collective-permute-start | bytes 921608 | tf_op jit(solution)/shard_map/ppermute | solution.py:27
  43.3 9.8 %collective-permute-start.14 = (bf16[200,768]{1,0:T(8,128)(2,1)S(1)}, bf16[200,768]{1,0:T(8,128)(2,1)}, u32[]{:S(2)}, u32[]{:S(2)}) collective-permute-start(bf16[200,768]{1,0:T(8,128)(2,1)S(1)} %collective-permute-done.7.refs_0_), channel_id=1, source_target_pairs={{0,2},{2,0},{4,6},{6,4},{8,10},{10,8},{12,14},{14,12},{1,3},{3,1},... | collective-permute-start | bytes 921608 | tf_op jit(solution)/shard_map/ppermute | solution.py:23
  47.1 6.1 %collective-permute-start.3 = (bf16[200,768]{1,0:T(8,128)(2,1)}, bf16[200,768]{1,0:T(8,128)(2,1)S(1)}, u32[]{:S(2)}, u32[]{:S(2)}) collective-permute-start(bf16[200,768]{1,0:T(8,128)(2,1)} %collective-permute-done.2.refs_2_), channel_id=1, source_target_pairs={{0,1},{1,0},{2,3},{3,2},{4,5},{5,4},{6,7},{7,6},{8,9},{9,8},{10,11... | collective-permute-start | bytes 921608 | tf_op jit(solution)/shard_map/ppermute | solution.py:27
  47.3 5.9 %collective-permute-start.9 = (bf16[200,768]{1,0:T(8,128)(2,1)}, bf16[200,768]{1,0:T(8,128)(2,1)S(1)}, u32[]{:S(2)}, u32[]{:S(2)}) collective-permute-start(bf16[200,768]{1,0:T(8,128)(2,1)} %collective-permute-done.6.refs_6_), channel_id=1, source_target_pairs={{0,1},{1,0},{2,3},{3,2},{4,5},{5,4},{6,7},{7,6},{8,9},{9,8},{10,11... | collective-permute-start | bytes 921608 | tf_op jit(solution)/shard_map/ppermute | solution.py:27
  47.6 5.6 %collective-permute-start.13 = (bf16[200,768]{1,0:T(8,128)(2,1)}, bf16[200,768]{1,0:T(8,128)(2,1)S(1)}, u32[]{:S(2)}, u32[]{:S(2)}) collective-permute-start(bf16[200,768]{1,0:T(8,128)(2,1)} %collective-permute-done.12.refs_10_), channel_id=1, source_target_pairs={{0,1},{1,0},{2,3},{3,2},{4,5},{5,4},{6,7},{7,6},{8,9},{9,8},{10,11... | collective-permute-start | bytes 921608 | tf_op jit(solution)/shard_map/ppermute | solution.py:27
  53.0 7.2 %collective-permute-start.15 = (bf16[200,768]{1,0:T(8,128)(2,1)}, bf16[200,768]{1,0:T(8,128)(2,1)S(1)}, u32[]{:S(2)}, u32[]{:S(2)}) collective-permute-start(bf16[200,768]{1,0:T(8,128)(2,1)} %collective-permute-done.14.refs_2_), channel_id=1, source_target_pairs={{0,1},{1,0},{2,3},{3,2},{4,5},{5,4},{6,7},{7,6},{8,9},{9,8},{10,11... | collective-permute-start | bytes 921608 | tf_op jit(solution)/shard_map/ppermute | solution.py:27
  63.3 7.4 %collective-permute-start.16 = (bf16[128,768]{1,0:T(8,128)(2,1)S(1)}, bf16[128,768]{1,0:T(8,128)(2,1)S(1)}, u32[]{:S(2)}, u32[]{:S(2)}) collective-permute-start(bf16[128,768]{1,0:T(8,128)(2,1)S(1)} %get-tuple-element.28), channel_id=1, source_target_pairs={{0,16},{16,0},{1,17},{17,1},{2,18},{18,2},{3,19},{19,3},{4,20},{20... | collective-permute-start | bytes 589832 | tf_op jit(solution)/shard_map/ppermute | solution.py:31
  65.4 16.6 %all-to-all-start = ((bf16[16,16,256]{2,1,0:T(8,128)(2,1)}), bf16[16,16,256]{2,1,0:T(8,128)(2,1)S(1)}, u32[]{:S(2)}, u32[]{:S(2)}) async-start(bf16[16,16,256]{2,1,0:T(8,128)(2,1)} %windows.1), calls=%async_computation | async-start | bytes 262144 | tf_op jit(solution)/shard_map/all_to_all | solution.py:336
  71.9 7.5 %collective-permute-start.21 = (bf16[128,320]{1,0:T(8,128)(2,1)}, bf16[128,320]{1,0:T(8,128)(2,1)S(1)}, u32[]{:S(2)}, u32[]{:S(2)}) collective-permute-start(bf16[128,320]{1,0:T(8,128)(2,1)} %get-tuple-element.30.refs_0_), channel_id=1, source_target_pairs={{0,12},{2,14},{4,8},{6,10},{8,4},{10,6},{12,0},{14,2},{1,13},{3,15... | collective-permute-start | bytes 245768 | tf_op jit(solution)/shard_map/ppermute | solution.py:23
  74.4 18.4 %collective-permute-start.28 = (bf16[128,320]{1,0:T(8,128)(2,1)}, bf16[128,320]{1,0:T(8,128)(2,1)S(1)}, u32[]{:S(2)}, u32[]{:S(2)}) collective-permute-start(bf16[128,320]{1,0:T(8,128)(2,1)} %get-tuple-element.30.refs_0_), channel_id=1, source_target_pairs={{0,4},{2,6},{4,0},{6,2},{8,12},{10,14},{12,8},{14,10},{1,5},{3,7},... | collective-permute-start | bytes 245768 | tf_op jit(solution)/shard_map/ppermute | solution.py:23
  74.4 20.4 %collective-permute-start.26 = (bf16[128,320]{1,0:T(8,128)(2,1)}, bf16[128,320]{1,0:T(8,128)(2,1)S(1)}, u32[]{:S(2)}, u32[]{:S(2)}) collective-permute-start(bf16[128,320]{1,0:T(8,128)(2,1)} %get-tuple-element.30.refs_0_), channel_id=1, source_target_pairs={{0,2},{2,0},{4,6},{6,4},{8,10},{10,8},{12,14},{14,12},{1,3},{3,1},... | collective-permute-start | bytes 245768 | tf_op jit(solution)/shard_map/ppermute | solution.py:23
  75.9 19.1 %collective-permute-start.17 = (bf16[128,320]{1,0:T(8,128)(2,1)}, bf16[128,320]{1,0:T(8,128)(2,1)S(1)}, u32[]{:S(2)}, u32[]{:S(2)}) collective-permute-start(bf16[128,320]{1,0:T(8,128)(2,1)} %get-tuple-element.30.refs_0_), channel_id=1, source_target_pairs={{0,8},{2,10},{4,12},{6,14},{8,0},{10,2},{12,4},{14,6},{1,9},{3,11}... | collective-permute-start | bytes 245768 | tf_op jit(solution)/shard_map/ppermute | solution.py:23
  79.4 10.0 %collective-permute-start.22 = (bf16[128,320]{1,0:T(8,128)(2,1)S(1)}, bf16[128,320]{1,0:T(8,128)(2,1)S(1)}, u32[]{:S(2)}, u32[]{:S(2)}) collective-permute-start(bf16[128,320]{1,0:T(8,128)(2,1)S(1)} %collective-permute-done.21.refs_4_), channel_id=1, source_target_pairs={{0,1},{1,0},{2,3},{3,2},{4,5},{5,4},{6,7},{7,6},{8,9},{9,8},{10,11... | collective-permute-start | bytes 245768 | tf_op jit(solution)/shard_map/ppermute | solution.py:27
  85.5 3.9 %collective-permute-start.33 = (f32[3,1536]{1,0:T(4,128)S(1)}, f32[3,1536]{1,0:T(4,128)S(1)}, u32[]{:S(2)}, u32[]{:S(2)}) collective-permute-start(f32[3,1536]{1,0:T(4,128)S(1)} %add.58), channel_id=1, source_target_pairs={{0,2},{2,0},{4,6},{6,4},{8,10},{10,8},{12,14},{14,12},{1,3},{3,1},... | collective-permute-start | bytes 55304 | tf_op jit(solution)/shard_map/ppermute | solution.py:23
  89.4 5.9 %collective-permute-start.34 = (f32[3,1536]{1,0:T(4,128)S(1)}, f32[3,1536]{1,0:T(4,128)S(1)}, u32[]{:S(2)}, u32[]{:S(2)}) collective-permute-start(f32[3,1536]{1,0:T(4,128)S(1)} %add.59), channel_id=1, source_target_pairs={{0,4},{2,6},{4,0},{6,2},{8,12},{10,14},{12,8},{14,10},{1,5},{3,7},... | collective-permute-start | bytes 55304 | tf_op jit(solution)/shard_map/ppermute | solution.py:23
  92.8 4.3 %collective-permute-start.25 = (bf16[128,320]{1,0:T(8,128)(2,1)}, bf16[128,320]{1,0:T(8,128)(2,1)S(1)}, u32[]{:S(2)}, u32[]{:S(2)}) collective-permute-start(bf16[128,320]{1,0:T(8,128)(2,1)} %get-tuple-element.30.refs_0_), channel_id=1, source_target_pairs={{0,1},{1,0},{2,3},{3,2},{4,5},{5,4},{6,7},{7,6},{8,9},{9,8},{10,11... | collective-permute-start | bytes 245768 | tf_op jit(solution)/shard_map/ppermute | solution.py:27
  92.8 5.7 %collective-permute-start.30 = (bf16[128,320]{1,0:T(8,128)(2,1)S(1)}, bf16[128,320]{1,0:T(8,128)(2,1)S(1)}, u32[]{:S(2)}, u32[]{:S(2)}) collective-permute-start(bf16[128,320]{1,0:T(8,128)(2,1)S(1)} %collective-permute-done.28.refs_4_), channel_id=1, source_target_pairs={{0,2},{2,0},{4,6},{6,4},{8,10},{10,8},{12,14},{14,12},{1,3},{3,1},... | collective-permute-start | bytes 245768 | tf_op jit(solution)/shard_map/ppermute | solution.py:23
  95.0 5.7 %collective-permute-start.19 = (bf16[128,320]{1,0:T(8,128)(2,1)S(1)}, bf16[128,320]{1,0:T(8,128)(2,1)S(1)}, u32[]{:S(2)}, u32[]{:S(2)}) collective-permute-start(bf16[128,320]{1,0:T(8,128)(2,1)S(1)} %collective-permute-done.17.refs_0_), channel_id=1, source_target_pairs={{0,2},{2,0},{4,6},{6,4},{8,10},{10,8},{12,14},{14,12},{1,3},{3,1},... | collective-permute-start | bytes 245768 | tf_op jit(solution)/shard_map/ppermute | solution.py:23
  95.4 7.1 %collective-permute-start.23 = (bf16[128,320]{1,0:T(8,128)(2,1)S(1)}, bf16[128,320]{1,0:T(8,128)(2,1)S(1)}, u32[]{:S(2)}, u32[]{:S(2)}) collective-permute-start(bf16[128,320]{1,0:T(8,128)(2,1)S(1)} %collective-permute-done.21.refs_4_), channel_id=1, source_target_pairs={{0,2},{2,0},{4,6},{6,4},{8,10},{10,8},{12,14},{14,12},{1,3},{3,1},... | collective-permute-start | bytes 245768 | tf_op jit(solution)/shard_map/ppermute | solution.py:23
  97.1 5.4 %collective-permute-start.35 = (f32[3,1536]{1,0:T(4,128)S(1)}, f32[3,1536]{1,0:T(4,128)S(1)}, u32[]{:S(2)}, u32[]{:S(2)}) collective-permute-start(f32[3,1536]{1,0:T(4,128)S(1)} %add.60), channel_id=1, source_target_pairs={{0,8},{2,10},{4,12},{6,14},{8,0},{10,2},{12,4},{14,6},{1,9},{3,11}... | collective-permute-start | bytes 55304 | tf_op jit(solution)/shard_map/ppermute | solution.py:23
  98.4 5.2 %collective-permute-start.29 = (bf16[128,320]{1,0:T(8,128)(2,1)S(1)}, bf16[128,320]{1,0:T(8,128)(2,1)S(1)}, u32[]{:S(2)}, u32[]{:S(2)}) collective-permute-start(bf16[128,320]{1,0:T(8,128)(2,1)S(1)} %collective-permute-done.28.refs_4_), channel_id=1, source_target_pairs={{0,1},{1,0},{2,3},{3,2},{4,5},{5,4},{6,7},{7,6},{8,9},{9,8},{10,11... | collective-permute-start | bytes 245768 | tf_op jit(solution)/shard_map/ppermute | solution.py:27
  98.4 7.8 %collective-permute-start.18 = (bf16[128,320]{1,0:T(8,128)(2,1)S(1)}, bf16[128,320]{1,0:T(8,128)(2,1)S(1)}, u32[]{:S(2)}, u32[]{:S(2)}) collective-permute-start(bf16[128,320]{1,0:T(8,128)(2,1)S(1)} %collective-permute-done.17.refs_0_), channel_id=1, source_target_pairs={{0,1},{1,0},{2,3},{3,2},{4,5},{5,4},{6,7},{7,6},{8,9},{9,8},{10,11... | collective-permute-start | bytes 245768 | tf_op jit(solution)/shard_map/ppermute | solution.py:27
  (21 other events, 362.2 us)

commit v4 on v3

v4 whole, which is shorter than its diff:
```python
import functools
import math

import jax
import jax.numpy as jnp
from jax import lax
from jax.experimental import pallas as pl
from jax.experimental.pallas import tpu as pltpu
from jax.sharding import Mesh, PartitionSpec as P

HEADS = 8
QK = 128
VDIM = 192
SPAN = 8
MIB = 1 << 20
COST = 1000
VMEM = pl.BlockSpec(memory_space=pltpu.VMEM)
SMEM = pl.BlockSpec(memory_space=pltpu.SMEM)
HBM = pl.BlockSpec(memory_space=pltpu.HBM)


def chip_swap(cells, mask):
    count = lax.axis_size("chip")
    return lax.ppermute(cells, "chip", [(i, i ^ mask) for i in range(count)])


def core_swap(cells):
    return lax.ppermute(cells, "core", [(0, 1), (1, 0)])


def group_swap(cells):
    return lax.ppermute(cells, "groups", [(0, 1), (1, 0)])


def after(value, *others):
    return lax.optimization_barrier((value, *others))[0]


def bring(same, cross, rows, extra, core, weight, tracks, sems):
    copies = []
    for at, block in enumerate((same, cross)):
        for which, (first, length, target) in enumerate(
            (
                (0, rows, weight.at[pl.ds(pl.multiple_of((core ^ at) * rows, 8), rows)]),
                (rows, extra, tracks.at[pl.ds(at * extra, extra)]),
            )
        ):
            copy = pltpu.make_async_copy(
                block.at[pl.ds(first, length)], target, sems.at[2 * at + which]
            )
            copy.start()
            copies.append(copy)
    return copies


def first_tokens_kernel(rows, extra, place_ref, own_hbm, partner_hbm, *refs):
    blocks, refs = refs[:-8], refs[-8:]
    total_ref, last_ref, tracks_ref, in_s, x_s, w_s, in_sems, block_sems = refs
    chips = x_s.shape[0]
    inputs = [
        pltpu.make_async_copy(ref, in_s.at[part], in_sems.at[part])
        for part, ref in enumerate((own_hbm, partner_hbm))
    ]
    for copy in inputs:
        copy.start()
    copies = [
        bring(
            blocks[2 * at],
            blocks[2 * at + 1],
            rows,
            extra,
            place_ref[1],
            w_s.at[at],
            tracks_ref.at[pl.ds(2 * at * extra, 2 * extra)],
            block_sems.at[at],
        )
        for at in range(chips - 1)
    ]
    pairs, width = in_s.shape[1:]
    half = pairs // 2
    span = x_s.shape[2]
    line = lax.broadcasted_iota(jnp.int32, (half, pairs), 0)
    column = lax.broadcasted_iota(jnp.int32, (half, pairs), 1)
    for part, copy in enumerate(inputs):
        copy.wait()
        for tap in range(2):
            pick = (column == 2 * line + tap).astype(jnp.bfloat16)
            cells = jnp.dot(pick, in_s[part], preferred_element_type=jnp.float32).astype(
                jnp.bfloat16
            )
            for at in range(width // span):
                x_s[tap * (width // span) + at, part * half : (part + 1) * half, :] = cells[
                    :, at * span : (at + 1) * span
                ]
    total = jnp.zeros(total_ref.shape, jnp.float32)
    for at in range(chips - 1):
        for copy in copies[at]:
            copy.wait()
        total = total + jnp.dot(
            x_s[place_ref[0] ^ at], w_s[at], preferred_element_type=jnp.float32
        )
    total_ref[...] = total
    last_ref[...] = x_s[place_ref[0] ^ (chips - 1)]


def last_tokens_kernel(rows, extra, place_ref, total_ref, last_ref, same, cross, *refs):
    own_ref, partner_ref, tracks_ref, w_s, sems = refs
    for copy in bring(same, cross, rows, extra, place_ref[1], w_s, tracks_ref, sems):
        copy.wait()
    half = own_ref.shape[0]
    total = total_ref[...] + jnp.dot(last_ref[...], w_s[...], preferred_element_type=jnp.float32)
    own_ref[...] = total[:half].astype(jnp.bfloat16)
    partner_ref[...] = total[half:].astype(jnp.bfloat16)


def windows_kernel(grad_ref, out_ref):
    tracks = grad_ref.shape[0]
    count, lines, lanes = out_ref.shape
    rows = grad_ref.shape[1] // count
    lane = lax.broadcasted_iota(jnp.int32, (tracks, rows), 1)
    zero = jnp.zeros((tracks, rows), jnp.float32)
    out_ref[...] = jnp.zeros_like(out_ref)
    tiles = [grad_ref[:, at * rows : (at + 1) * rows].astype(jnp.float32) for at in range(count)]
    for at in range(count):
        after_it = tiles[at + 1] if at + 1 < count else zero
        before_it = pltpu.roll(tiles[at - 1], 2 * SPAN, 1) if at else zero
        edge = jnp.where(lane < SPAN, after_it, jnp.where(lane < 2 * SPAN, before_it, zero))
        out_ref[at, 0:tracks, 0:rows] = tiles[at].astype(out_ref.dtype)
        out_ref[at, 0:tracks, rows : 2 * rows] = edge.astype(out_ref.dtype)


def skip_terms(tok, head, taps):
    token_rows = tok.shape[0]
    root = math.sqrt(2.0 / math.pi)
    own, later, earlier = (
        head[:token_rows],
        head[token_rows : token_rows + SPAN],
        head[token_rows + SPAN :],
    )
    square = tok * tok
    curve = jnp.tanh(root * (tok + 0.044715 * square * tok))
    gate = 0.5 * (1.0 + curve)
    act = tok * gate
    slope = gate + 0.5 * tok * (1.0 - curve * curve) * (root * (1.0 + 3 * 0.044715 * square))
    convback = jnp.zeros_like(tok)
    sums = []
    for tap, shifted in enumerate(
        (
            jnp.concatenate([own[SPAN:], later], axis=0),
            own,
            jnp.concatenate([earlier, own[:-SPAN]], axis=0),
        )
    ):
        convback = convback + taps[tap : tap + 1] * shifted
        sums.append(jnp.sum(act * shifted, axis=0, keepdims=True))
    return (slope * convback).astype(jnp.bfloat16), sums


def decoder_kernel(extra, parts, group_ref, mine_ref, grads_ref, taps_ref, *refs):
    chosen_refs, track_refs, (skip_ref, sums_ref, head_ref) = (
        refs[:parts],
        refs[parts:-3],
        refs[-3:],
    )
    group = group_ref[0]
    token_rows, width = mine_ref.shape
    masked = [
        lax.dot_general(
            grads_ref[...],
            chosen_ref[...],
            (((0,), (0,)), ((), ())),
            preferred_element_type=jnp.float32,
        )[: token_rows + 2 * SPAN]
        for chosen_ref in chosen_refs
    ]
    heads = []
    for side in (group, 1 - group):
        head = jnp.zeros((token_rows + 2 * SPAN, width), jnp.float32)
        for cells, tracks_ref in zip(masked, track_refs):
            column = lax.broadcasted_iota(jnp.int32, cells.shape, 1) % extra // (extra // 2)
            rows = jnp.where(column == side, cells, 0.0).astype(jnp.bfloat16)
            head = head + jnp.dot(rows, tracks_ref[...], preferred_element_type=jnp.float32)
        heads.append(head.astype(jnp.bfloat16))
    head_ref[...] = heads[1]
    taps = taps_ref[:, pl.ds(pl.multiple_of(group * width, width), width)]
    skip, sums = skip_terms(mine_ref[...].astype(jnp.float32), heads[0].astype(jnp.float32), taps)
    skip_ref[...] = skip
    for tap, term in enumerate(sums):
        sums_ref[tap : tap + 1, :] = term


def keyval_kernel(
    group_ref,
    mine_ref,
    skip_mine_ref,
    sums_mine_ref,
    head_ref,
    taps_ref,
    gain_ref,
    kv_ref,
    theirs_ref,
    tok_ref,
    normed_ref,
    block_ref,
    skip_ref,
    sums_s,
):
    token_rows, width = mine_ref.shape
    group = group_ref[0]
    here = pl.ds(pl.multiple_of(group * width, width), width)
    there = pl.ds(pl.multiple_of((1 - group) * width, width), width)
    tok_ref[:, here] = mine_ref[...]
    tok_ref[:, there] = theirs_ref[...]
    tok_f = tok_ref[...].astype(jnp.float32)
    inverse = lax.rsqrt(jnp.mean(tok_f * tok_f, axis=-1, keepdims=True) + 1e-06)
    normed = (tok_f * inverse * gain_ref[...]).astype(jnp.bfloat16)
    normed_ref[...] = normed
    block_ref[0:token_rows, 0 : QK + VDIM] = lax.dot_general(
        normed, kv_ref[...], (((1,), (1,)), ((), ())), preferred_element_type=jnp.float32
    ).astype(jnp.bfloat16)
    block_ref[0:token_rows, QK + VDIM :] = jnp.zeros(
        (token_rows, block_ref.shape[1] - QK - VDIM), jnp.bfloat16
    )
    skip, sums = skip_terms(
        theirs_ref[...].astype(jnp.float32), head_ref[...].astype(jnp.float32), taps_ref[:, there]
    )
    skip_ref[:, here] = skip_mine_ref[...]
    skip_ref[:, there] = skip
    sums_s[0:3, here] = sums_mine_ref[...]
    for tap, term in enumerate(sums):
        sums_s[tap : tap + 1, there] = term
    lanes = block_ref.shape[1]
    rows = [
        sums_s[tap : tap + 1, at : at + lanes]
        for tap in range(3)
        for at in range(0, 2 * width, lanes)
    ]
    exact = jnp.concatenate(rows, axis=0)
    coarse = exact.astype(jnp.bfloat16).astype(jnp.float32)
    block_ref[token_rows:, :] = jnp.concatenate([coarse, exact - coarse], axis=0).astype(
        jnp.bfloat16
    )


def add_terms(blocks):
    if len(blocks) == 1:
        rows = blocks[0].astype(jnp.float32)
        return rows[: rows.shape[0] // 2] + rows[rows.shape[0] // 2 :]
    half = len(blocks) // 2
    return add_terms(blocks[:half]) + add_terms(blocks[half:])


def sweep(turns, step, body, carry):
    if turns <= 4:
        for turn in range(turns):
            carry = body(turn * step, carry)
        return carry
    return lax.fori_loop(
        0, turns, lambda turn, held: body(pl.multiple_of(turn * step, step), held), carry
    )


def query_kernel(normed_ref, weight_ref, out_ref):
    rows = normed_ref.shape[0]
    query = jnp.dot(normed_ref[...], weight_ref[...], preferred_element_type=jnp.float32).astype(
        jnp.bfloat16
    )
    for h in range(HEADS):
        out_ref[h * rows : (h + 1) * rows, :] = query[:, h * QK : (h + 1) * QK]


def attention_kernel(row_block, key_block, tokens_each, pieces, first, last, query_ref, *refs):
    kv_refs, refs = refs[:pieces], refs[pieces:]
    riders = kv_refs[0].shape[0] > tokens_each
    if not first:
        old_top_ref, old_weighted_ref, old_terms_ref = refs[:3]
        refs = refs[3:]
    if last:
        tok_ref, outw_hbm, out_ref = refs[:3]
        refs = refs[3:]
        if riders:
            sums_ref, refs = refs[0], refs[1:]
        k_s, v_s, s_s, context_s, outw_s, sem = refs
        token_rows = tok_ref.shape[0]
        fetch = pltpu.make_async_copy(outw_hbm, outw_s, sem)
        fetch.start()
    else:
        top_ref, weighted_ref, terms_ref, k_s, v_s, s_s = refs
    at = 0
    for ref in kv_refs:
        k_s[at : at + tokens_each, :] = ref[0:tokens_each, :QK]
        v_s[at : at + tokens_each, 0:VDIM] = ref[0:tokens_each, QK : QK + VDIM]
        at += tokens_each
    key_block = min(key_block, at)
    v_s[:, VDIM:] = jnp.ones((at, v_s.shape[1] - VDIM), jnp.bfloat16)
    if riders:
        terms = add_terms([ref[tokens_each:, :] for ref in kv_refs])
        if not first:
            terms = terms + old_terms_ref[...]
        if last:
            terms = terms * ((2 * pieces * tokens_each) ** (-0.5))
            lanes = terms.shape[1]
            turns = sums_ref.shape[1] // lanes
            for row in range(terms.shape[0]):
                tap, spot = row // turns, row % turns * lanes
                sums_ref[tap : tap + 1, spot : spot + lanes] = terms[row : row + 1, :]
        else:
            terms_ref[...] = terms
    scale = QK ** (-0.5) / math.log(2.0)
    for r in range(0, query_ref.shape[0], row_block):
        rows = query_ref[r : r + row_block, :]
        slot = (r // row_block) % 2

        def score(k, top):
            scores = lax.dot_general(
                rows,
                k_s[pl.ds(k, key_block), :],
                (((1,), (1,)), ((), ())),
                preferred_element_type=jnp.float32,
            )
            s_s[slot, :, pl.ds(k, key_block)] = scores
            return jnp.maximum(top, jnp.max(scores, axis=1, keepdims=True))

        def weigh(k, weighted):
            shifted = s_s[slot, :, pl.ds(k, key_block)] - top
            expw = jnp.exp2(shifted * scale).astype(jnp.bfloat16)
            return weighted + jnp.dot(
                expw, v_s[pl.ds(k, key_block), :], preferred_element_type=jnp.float32
            )

        if first:
            old_top = jnp.full((row_block, 1), -jnp.inf, jnp.float32)
            start = jnp.zeros((row_block, v_s.shape[1]), jnp.float32)
        else:
            old_top = old_top_ref[r : r + row_block, 0:1]
        top = sweep(at // key_block, key_block, score, old_top)
        if not first:
            start = old_weighted_ref[r : r + row_block, :] * jnp.exp2((old_top - top) * scale)
        weighted = sweep(at // key_block, key_block, weigh, start)
        if last:
            context = (weighted[:, :VDIM] / weighted[:, VDIM : VDIM + 1]).astype(jnp.bfloat16)
            for j in range(row_block // token_rows):
                h = r // token_rows + j
                context_s[:, h * VDIM : (h + 1) * VDIM] = context[
                    j * token_rows : (j + 1) * token_rows
                ]
        else:
            top_ref[r : r + row_block, :] = jnp.broadcast_to(top, (row_block, top_ref.shape[1]))
            weighted_ref[r : r + row_block, :] = weighted
    if last:
        fetch.wait()
        added = jnp.dot(context_s[...], outw_s[...], preferred_element_type=jnp.float32)
        out_ref[...] = (tok_ref[...].astype(jnp.float32) + added).astype(jnp.bfloat16)


def call(body, out, specs, scratch=(), limit=32, name=None, us=1):
    return pl.pallas_call(
        body,
        out_shape=out,
        in_specs=specs,
        out_specs=jax.tree.map(lambda _: VMEM, out),
        scratch_shapes=list(scratch),
        compiler_params=pltpu.CompilerParams(vmem_limit_bytes=limit * MIB),
        cost_estimate=pl.CostEstimate(
            flops=int(us * COST), transcendentals=0, bytes_accessed=int(us * 1e3)
        ),
        name=name,
    )


def shards(
    enc_input,
    enc_weight,
    norm_gain,
    q_weight,
    kv_weight,
    out_weight,
    dec_weight,
    track_weight,
    track_grad,
    track_index,
    track_mask,
):
    chips = lax.axis_size("chip")
    count = 2 * chips
    pair = chips // 2
    token_rows = enc_input.shape[0] // 2
    rows, dim = enc_weight.shape
    width = dim // 2
    tracks = track_weight.shape[0]
    extra = 2 * tracks
    group = lax.axis_index("groups")
    me = lax.axis_index("chip") * 2 + lax.axis_index("core")
    shape = lambda *dims, kind=jnp.bfloat16: jax.ShapeDtypeStruct(dims, kind)
    direct = pair == 4 and rows % 16 == 0

    own_half = lax.dynamic_slice_in_dim(enc_weight, group * width, width, axis=1)
    packed = jnp.concatenate([own_half, track_weight[:, :width], track_weight[:, width:]], axis=0)
    partner_input = group_swap(enc_input)
    if direct:
        nears = [packed] + [chip_swap(packed, 2 * mask) for mask in range(1, pair)]
        same = [cells for near in nears for cells in (near, chip_swap(near, 1))]
        blocks = [cells for part in same[:-1] for cells in (part, core_swap(part))]
        ids = me ^ jnp.arange(count, dtype=jnp.int32)
    else:
        ids = jnp.arange(count, dtype=jnp.int32)

    lines = -(-tracks // 16) * 16
    windows = call(
        windows_kernel, shape(count, lines, 2 * token_rows), [VMEM], limit=16, name="windows"
    )(track_grad.T)
    slots = jnp.pad(
        track_index.reshape(count, tracks), ((0, 0), (0, lines - tracks)), constant_values=-1
    )
    measured = jnp.pad(track_mask.reshape(count, tracks), ((0, 0), (0, lines - tracks)))
    column_tracks = ids[:, None] * tracks + jnp.arange(extra, dtype=jnp.int32)[None, :] % tracks
    chosen = [
        jnp.where(
            slots.reshape(-1, 1) == part.reshape(1, -1),
            measured.reshape(-1, 1).astype(jnp.bfloat16),
            0,
        ).astype(jnp.bfloat16)
        for part in ((column_tracks[:-2], column_tracks[-2:]) if direct else (column_tracks,))
    ]

    if direct:
        place = jnp.stack([lax.axis_index("chip"), lax.axis_index("core")]).astype(jnp.int32)
        here = lambda *cells: [pltpu.with_memory_space_constraint(c, pltpu.HBM) for c in cells]
        span = 2 * rows
        total, last_cells, first_rows = call(
            functools.partial(first_tokens_kernel, rows, extra),
            (
                shape(2 * token_rows, width, kind=jnp.float32),
                shape(2 * token_rows, span),
                shape((count - 2) * extra, width),
            ),
            [SMEM] + [HBM] * count,
            scratch=(
                pltpu.VMEM((2,) + enc_input.shape, jnp.bfloat16),
                pltpu.VMEM((chips, 2 * token_rows, span), jnp.bfloat16),
                pltpu.VMEM((chips - 1, span, width), jnp.bfloat16),
                pltpu.SemaphoreType.DMA((2,)),
                pltpu.SemaphoreType.DMA((chips - 1, 4)),
            ),
            limit=16,
            name="first_tokens",
            us=5,
        )(place, *here(enc_input, partner_input, *blocks))
        final, total = lax.optimization_barrier((same[-1], total))
        mine, partner, last_rows = call(
            functools.partial(last_tokens_kernel, rows, extra),
            (shape(token_rows, width), shape(token_rows, width), shape(2 * extra, width)),
            [SMEM] + [VMEM] * 2 + [HBM] * 2,
            scratch=(pltpu.VMEM((span, width), jnp.bfloat16), pltpu.SemaphoreType.DMA((4,))),
            limit=12,
            name="last_tokens",
            us=2,
        )(place, total, last_cells, *here(final, core_swap(final)))
        track_rows = [first_rows, last_rows]
    else:
        gathered = lax.all_gather(packed, ("chip", "core"), axis=0)
        track_rows = [gathered[:, rows:].reshape(count * extra, width)]
        weight = gathered[:, :rows].reshape(count * rows, width)
        mine, partner = (
            jnp.dot(
                cells.reshape(token_rows, count * rows), weight, preferred_element_type=jnp.float32
            ).astype(jnp.bfloat16)
            for cells in (enc_input, partner_input)
        )
    theirs = group_swap(partner)
    exchanged = lax.all_to_all(after(windows, partner), ("chip", "core"), 0, 0, tiled=True)
    skip_mine, sums_mine, head = call(
        functools.partial(decoder_kernel, extra, len(chosen)),
        (
            shape(token_rows, width),
            shape(3, width, kind=jnp.float32),
            shape(token_rows + 2 * SPAN, width),
        ),
        [SMEM] + [VMEM] * (3 + 2 * len(chosen)),
        limit=16,
        name="decoder",
        us=2,
    )(
        group.reshape(1),
        mine,
        exchanged.reshape(count * lines, 2 * token_rows),
        dec_weight,
        *chosen,
        *track_rows,
    )
    lanes = 384
    terms = 3 * dim // lanes
    tokens, normed, block, skip_grad = call(
        keyval_kernel,
        (
            shape(token_rows, dim),
            shape(token_rows, dim),
            shape(token_rows + 2 * terms, lanes),
            shape(token_rows, dim),
        ),
        [SMEM] + [VMEM] * 8,
        scratch=(pltpu.VMEM((8, dim), jnp.float32),),
        limit=12,
        name="keyval",
        us=2,
    )(
        group.reshape(1),
        mine,
        skip_mine,
        sums_mine,
        head,
        dec_weight,
        norm_gain.reshape(1, dim),
        kv_weight.T,
        theirs,
    )

    if direct:
        nears = [chip_swap(block, 2 * mask) if mask else block for mask in range(pair)]
        fars = [chip_swap(near, 1) for near in nears]
        stages = [
            [
                cells
                for mask in masks
                for cells in (nears[mask], core_swap(nears[mask]), fars[mask], core_swap(fars[mask]))
            ]
            for masks in ((0, 1), (2, 3))
        ]
        each = token_rows
    else:
        gathered = lax.all_gather(block, ("chip", "core"), axis=0)
        stages = [[gathered[:, :token_rows].reshape(count * token_rows, lanes)]]
        each = count * token_rows
        sums = jnp.sum(
            gathered[:, token_rows:].astype(jnp.float32).reshape(2 * count, terms, lanes), axis=0
        )
        dec_weight_grad = sums.reshape(3, dim) / jnp.float32(math.sqrt(token_rows * count))

    query = call(query_kernel, shape(HEADS * token_rows, QK), [VMEM] * 2, limit=8, name="query")(
        normed, q_weight
    )
    row_block = 2 * token_rows if direct else token_rows
    state = []
    for turn, pieces in enumerate(stages):
        last = turn + 1 == len(stages)
        keys = len(pieces) * each
        extras = (
            [tokens, pltpu.with_memory_space_constraint(out_weight, pltpu.HBM)] if last else []
        )
        if last:
            held = (shape(token_rows, dim),) + (
                (shape(3, dim, kind=jnp.float32),) if direct else ()
            )
        else:
            held = (
                shape(HEADS * token_rows, 128, kind=jnp.float32),
                shape(HEADS * token_rows, 256, kind=jnp.float32),
                shape(terms, lanes, kind=jnp.float32),
            )
        state = call(
            functools.partial(
                attention_kernel, row_block, 512, each, len(pieces), turn == 0, last
            ),
            held,
            [VMEM] * (1 + len(pieces) + len(state)) + ([VMEM, HBM] if last else []),
            scratch=(
                pltpu.VMEM((keys, QK), jnp.bfloat16),
                pltpu.VMEM((keys, 256), jnp.bfloat16),
                pltpu.VMEM((2, row_block, keys), jnp.float32),
            )
            + (
                (
                    pltpu.VMEM((token_rows, HEADS * VDIM), jnp.bfloat16),
                    pltpu.VMEM(out_weight.shape, jnp.bfloat16),
                    pltpu.SemaphoreType.DMA(()),
                )
                if last
                else ()
            ),
            limit=60 if len(stages) == 1 else 16,
            name="attention",
            us=5 if last else 2,
        )(query, *pieces, *state, *extras)
    if direct:
        return (state[0], skip_grad, state[1])
    return (state[0], skip_grad, dec_weight_grad)


def solution(mesh):
    groups, count = mesh.devices.shape
    inner = Mesh(mesh.devices.reshape(groups, count // 2, 2), ("groups", "chip", "core"))
    seq = ("chip", "core")
    every = ("groups", "chip", "core")
    return jax.shard_map(
        shards,
        mesh=inner,
        in_specs=(
            P(every, None),
            P(seq, None),
            P(),
            P(),
            P(),
            P(),
            P(),
            P(seq, None),
            P("groups", seq),
            P("groups"),
            P("groups"),
        ),
        out_specs=(P(every, None), P(every, None), P("groups", None)),
        check_vma=False,
    )
```

time: 113 us -> 105 us (0.929)
  waiting for transfers between devices: 43.6 us -> 38.6 us
  local copies, waits for them, and re-layouts: 8.2 us -> 5.2 us
    ppermute x17 -> x14, waiting for transfers between devices: 41.2 us -> 31.3 us  [chip_swap(): return lax.ppermute(cells, 'chip', [(i, i ^ mask) for i in range(count)])]
    all_to_all x1, waiting for transfers between devices: 0.01 us -> 5.99 us  [shards(): lax.all_to_all(after(windows, partner), ('chip', 'core'), 0, 0, tiled=True)]
    all_to_all x1, starting transfers between devices: 3.76 us -> 7.39 us  [shards(): lax.all_to_all(after(windows, partner), ('chip', 'core'), 0, 0, tiled=True)]
    ppermute x17 -> x14, starting transfers between devices: 28.3 us -> 25.4 us  [chip_swap(): return lax.ppermute(cells, 'chip', [(i, i ^ mask) for i in range(count)])]
    unnamed x32, local copies, waits for them, and re-layouts: 6.09 us -> 3.84 us
    ppermute x2, waiting for transfers between devices: 1.51 us -> 0.01 us  [group_swap(): return lax.ppermute(cells, 'groups', [(0, 1), (1, 0)])]
    pallas_call x1, Pallas kernels: 5.3 us -> 6.8 us  [shards(): call(functools.partial(first_tokens_kernel, rows, extra), (shape(2 * toke...]
    pallas_call x1, Pallas kernels: 2.08 us -> 0.87 us  [shards(): call(functools.partial(decoder_kernel, extra, len(chosen)), (shape(token_...]
  transfers between devices with their start and end apart: 37 -> 33, of which waited for: 13 -> 9; matrix products, arithmetic and copies ran while one was open for 2% -> 1% of each run, Pallas kernels for 11% -> 10%
where the time goes in v4:
time: 105 us; the launch traced here: 104 us
  waiting for transfers between devices  38.6 us (37%)
  starting transfers between devices  38.2 us (36%)
  Pallas kernels  20.8 us (20%)
  local copies, waits for them, and re-layouts  5.2 us (5%)
  between operations  1.14 us (1%)
    ppermute x14, waiting for transfers between devices, chip_swap(): return lax.ppermute(cells, 'chip', [(i, i ^ mask) for i in range(count)])  31.3 us
    ppermute x14, starting transfers between devices, chip_swap(): return lax.ppermute(cells, 'chip', [(i, i ^ mask) for i in range(count)])  25.4 us
    pallas_call x2, Pallas kernels, shards(): call(functools.partial(attention_kernel, row_block, 512, each, len(pieces...  7.91 us
    all_to_all x1, starting transfers between devices, shards(): lax.all_to_all(after(windows, partner), ('chip', 'core'), 0, 0, tiled=True)  7.39 us
    pallas_call x1, Pallas kernels, shards(): call(functools.partial(first_tokens_kernel, rows, extra), (shape(2 * toke...  6.8 us
    all_to_all x1, waiting for transfers between devices, shards(): lax.all_to_all(after(windows, partner), ('chip', 'core'), 0, 0, tiled=True)  5.99 us
    unnamed x32, local copies, waits for them, and re-layouts  3.84 us
    ppermute x2, starting transfers between devices, group_swap(): return lax.ppermute(cells, 'groups', [(0, 1), (1, 0)])  3.04 us
  transfers between devices with their start and end apart: 33, of which 9 were waited for; matrix products, arithmetic and copies ran while one was open for 1% of the time, Pallas kernels for 10%

profile of v4, /device:TPU:0, one launch (start us, length us, event | category | flops | bytes accessed | tf_op | source)
XLA Modules:
  0.0 104.5 jit_solution(878946238282873013)
XLA Ops:
  0.7 0.8 fusion
  1.8 4.1 %collective-permute-start.10 = (bf16[200,768]{1,0:T(8,128)(2,1)S(1)}, bf16[200,768]{1,0:T(8,128)(2,1)S(1)}, u32[]{:S(2)}, u32[]{:S(2)}) collective-permute-start(bf16[200,768]{1,0:T(8,128)(2,1)S(1)} %pad_maximum_fusion.refs_0_), channel_id=1, source_target_pairs={{0,8},{2,10},{4,12},{6,14},{8,0},{10,2},{12,4},{14,6},{1,9},{3,11}... | collective-permute-start | bytes 921608 | tf_op jit(solution)/shard_map/ppermute | solution.py:24
  5.9 1.6 %collective-permute-start.6 = (bf16[200,768]{1,0:T(8,128)(2,1)S(1)}, bf16[200,768]{1,0:T(8,128)(2,1)S(1)}, u32[]{:S(2)}, u32[]{:S(2)}) collective-permute-start(bf16[200,768]{1,0:T(8,128)(2,1)S(1)} %pad_maximum_fusion.refs_0_), channel_id=1, source_target_pairs={{0,4},{2,6},{4,0},{6,2},{8,12},{10,14},{12,8},{14,10},{1,5},{3,7},... | collective-permute-start | bytes 921608 | tf_op jit(solution)/shard_map/ppermute | solution.py:24
  7.5 1.7 %collective-permute-start.4 = (bf16[200,768]{1,0:T(8,128)(2,1)S(1)}, bf16[200,768]{1,0:T(8,128)(2,1)}, u32[]{:S(2)}, u32[]{:S(2)}) collective-permute-start(bf16[200,768]{1,0:T(8,128)(2,1)S(1)} %pad_maximum_fusion.refs_0_), channel_id=1, source_target_pairs={{0,2},{2,0},{4,6},{6,4},{8,10},{10,8},{12,14},{14,12},{1,3},{3,1},... | collective-permute-start | bytes 921608 | tf_op jit(solution)/shard_map/ppermute | solution.py:24
  9.2 12.3 %collective-permute-done.10.refs_8_ = bf16[200,768]{1,0:T(8,128)(2,1)S(1)} collective-permute-done((bf16[200,768]{1,0:T(8,128)(2,1)S(1)}, bf16[200,768]{1,0:T(8,128)(2,1)S(1)}, u32[]{:S(2)}, u32[]{:S(2)}) %collective-permute-start.10) | collective-permute-done | bytes 307232 | tf_op jit(solution)/shard_map/ppermute | solution.py:24
  21.5 7.6 %collective-permute-start.12 = (bf16[200,768]{1,0:T(8,128)(2,1)S(1)}, bf16[200,768]{1,0:T(8,128)(2,1)}, u32[]{:S(2)}, u32[]{:S(2)}) collective-permute-start(bf16[200,768]{1,0:T(8,128)(2,1)S(1)} %collective-permute-done.10.refs_8_), channel_id=1, source_target_pairs={{0,2},{2,0},{4,6},{6,4},{8,10},{10,8},{12,14},{14,12},{1,3},{3,1},... | collective-permute-start | bytes 921608 | tf_op jit(solution)/shard_map/ppermute | solution.py:24
  29.1 1.5 %collective-permute-start.2 = (bf16[256,1408]{1,0:T(8,128)(2,1)}, bf16[256,1408]{1,0:T(8,128)(2,1)S(1)}, u32[]{:S(2)}, u32[]{:S(2)}) collective-permute-start(bf16[256,1408]{1,0:T(8,128)(2,1)} %own_hbm.1), channel_id=1, source_target_pairs={{0,16},{16,0},{1,17},{17,1},{2,18},{18,2},{3,19},{19,3},{4,20},{20... | collective-permute-start | bytes 2162696 | tf_op jit(solution)/shard_map/ppermute | solution.py:32
  31.6 4.3 %collective-permute-done.12.refs_10_ = bf16[200,768]{1,0:T(8,128)(2,1)} collective-permute-done((bf16[200,768]{1,0:T(8,128)(2,1)S(1)}, bf16[200,768]{1,0:T(8,128)(2,1)}, u32[]{:S(2)}, u32[]{:S(2)}) %collective-permute-start.12) | collective-permute-done | bytes 307232 | tf_op jit(solution)/shard_map/ppermute | solution.py:24
  35.9 3.3 %collective-permute-done.8.refs_6_ = bf16[200,768]{1,0:T(8,128)(2,1)} collective-permute-done((bf16[200,768]{1,0:T(8,128)(2,1)S(1)}, bf16[200,768]{1,0:T(8,128)(2,1)}, u32[]{:S(2)}, u32[]{:S(2)}) %collective-permute-start.8) | collective-permute-done | bytes 307232 | tf_op jit(solution)/shard_map/ppermute | solution.py:24
  39.8 1.5 %collective-permute-start.1 = (bf16[200,768]{1,0:T(8,128)(2,1)}, bf16[200,768]{1,0:T(8,128)(2,1)}, u32[]{:S(2)}, u32[]{:S(2)}) collective-permute-start(bf16[200,768]{1,0:T(8,128)(2,1)} %collective-permute-done.refs_12_), channel_id=1, source_target_pairs={{0,2},{2,0},{4,6},{6,4},{8,10},{10,8},{12,14},{14,12},{1,3},{3,1},... | collective-permute-start | bytes 921608 | tf_op jit(solution)/shard_map/ppermute | solution.py:24
  41.3 0.8 copy-done.4
  42.2 0.7 windows.1
  43.0 0.8 copy-done.6
  43.9 6.8 %first_tokens.1 = (f32[256,768]{1,0:T(8,128)S(1)}, bf16[256,352]{1,0:T(8,128)(2,1)S(1)}, bf16[336,768]{1,0:T(8,128)(2,1)S(1)}) custom-call(s32[2]{0:T(128)S(1)} %pad_add_fusion.place_ref, bf16[256,1408]{1,0:T(8,128)(2,1)} %own_hbm.1, bf16[256,1408]{1,0:T(8,128)(2,1)} %copy-done.6, bf16[200,768]{1,0:T(8,128)(2,1)} %copy-done.5, bf16[200,768]{1,0:T(8,128)(2,1)} %copy-done.9, ...), custom_call_target="tpu_custom_call" | custom-call | flops 5000 | bytes 5000 | tf_op jit(solution)/shard_map/first_tokens/pallas_call | solution.py:430
  51.5 1.2 %collective-permute-done.15.cross = bf16[200,768]{1,0:T(8,128)(2,1)} collective-permute-done((bf16[200,768]{1,0:T(8,128)(2,1)}, bf16[200,768]{1,0:T(8,128)(2,1)}, u32[]{:S(2)}, u32[]{:S(2)}) %collective-permute-start.15) | collective-permute-done | bytes 307232 | tf_op jit(solution)/shard_map/ppermute | solution.py:28
  52.7 2.0 %last_tokens.1 = (bf16[128,768]{1,0:T(8,128)(2,1)S(1)}, bf16[128,768]{1,0:T(8,128)(2,1)S(1)}, bf16[48,768]{1,0:T(8,128)(2,1)S(1)}) custom-call(s32[2]{0:T(128)S(1)} %pad_add_fusion.place_ref, f32[256,768]{1,0:T(8,128)S(1)} %get-tuple-element.25.total_ref, bf16[256,352]{1,0:T(8,128)(2,1)S(1)} %get-tuple-element.26.last_ref, ...), custom_call_target="tpu_custom_call" | custom-call | flops 2000 | bytes 2000 | tf_op jit(solution)/shard_map/last_tokens/pallas_call | solution.py:450
  54.7 7.4 %all-to-all-start = ((bf16[16,16,256]{2,1,0:T(8,128)(2,1)}), bf16[16,16,256]{2,1,0:T(8,128)(2,1)S(1)}, u32[]{:S(2)}, u32[]{:S(2)}) async-start(bf16[16,16,256]{2,1,0:T(8,128)(2,1)} %windows.1), calls=%async_computation | async-start | bytes 262144 | tf_op jit(solution)/shard_map/all_to_all | solution.py:471
  62.4 1.6 %collective-permute-start.16 = (bf16[128,768]{1,0:T(8,128)(2,1)S(1)}, bf16[128,768]{1,0:T(8,128)(2,1)S(1)}, u32[]{:S(2)}, u32[]{:S(2)}) collective-permute-start(bf16[128,768]{1,0:T(8,128)(2,1)S(1)} %get-tuple-element.29), channel_id=1, source_target_pairs={{0,16},{16,0},{1,17},{17,1},{2,18},{18,2},{3,19},{19,3},{4,20},{20... | collective-permute-start | bytes 589832 | tf_op jit(solution)/shard_map/ppermute | solution.py:32
  64.0 6.0 %all-to-all-done = bf16[16,16,256]{2,1,0:T(8,128)(2,1)S(1)} async-done(((bf16[16,16,256]{2,1,0:T(8,128)(2,1)}), bf16[16,16,256]{2,1,0:T(8,128)(2,1)S(1)}, u32[]{:S(2)}, u32[]{:S(2)}) %all-to-all-start) | async-done | bytes 131104 | tf_op jit(solution)/shard_map/all_to_all | solution.py:471
  70.0 0.9 decoder.1
  70.9 1.9 %keyval.1 = (bf16[128,1536]{1,0:T(8,128)(2,1)S(1)}, bf16[128,1536]{1,0:T(8,128)(2,1)S(1)}, bf16[152,384]{1,0:T(8,128)(2,1)S(1)}, bf16[128,1536]{1,0:T(8,128)(2,1)}) custom-call(s32[1]{0:T(128)} %bitcast.group_ref, bf16[128,768]{1,0:T(8,128)(2,1)S(1)} %get-tuple-element.28.mine_ref, bf16[128,768]{1,0:T(8,128)(2,1)S(1)} %get-tuple-element.33.skip_mine_ref, ...), custom_call_target="tpu_custom_call" | custom-call | flops 2000 | bytes 2000 | tf_op jit(solution)/shard_map/keyval/pallas_call | solution.py:493
  73.2 1.5 %collective-permute-start.26 = (bf16[152,384]{1,0:T(8,128)(2,1)S(1)}, bf16[152,384]{1,0:T(8,128)(2,1)S(1)}, u32[]{:S(2)}, u32[]{:S(2)}) collective-permute-start(bf16[152,384]{1,0:T(8,128)(2,1)S(1)} %get-tuple-element.37.refs_0_), channel_id=1, source_target_pairs={{0,2},{2,0},{4,6},{6,4},{8,10},{10,8},{12,14},{14,12},{1,3},{3,1},... | collective-permute-start | bytes 350216 | tf_op jit(solution)/shard_map/ppermute | solution.py:24
  74.7 2.4 %collective-permute-start.17 = (bf16[152,384]{1,0:T(8,128)(2,1)S(1)}, bf16[152,384]{1,0:T(8,128)(2,1)S(1)}, u32[]{:S(2)}, u32[]{:S(2)}) collective-permute-start(bf16[152,384]{1,0:T(8,128)(2,1)S(1)} %get-tuple-element.37.refs_0_), channel_id=1, source_target_pairs={{0,8},{2,10},{4,12},{6,14},{8,0},{10,2},{12,4},{14,6},{1,9},{3,11}... | collective-permute-start | bytes 350216 | tf_op jit(solution)/shard_map/ppermute | solution.py:24
  77.7 1.6 %collective-permute-start.30 = (bf16[152,384]{1,0:T(8,128)(2,1)S(1)}, bf16[152,384]{1,0:T(8,128)(2,1)S(1)}, u32[]{:S(2)}, u32[]{:S(2)}) collective-permute-start(bf16[152,384]{1,0:T(8,128)(2,1)S(1)} %collective-permute-done.28.refs_4_), channel_id=1, source_target_pairs={{0,2},{2,0},{4,6},{6,4},{8,10},{10,8},{12,14},{14,12},{1,3},{3,1},... | collective-permute-start | bytes 350216 | tf_op jit(solution)/shard_map/ppermute | solution.py:24
  79.8 6.4 %collective-permute-done.17.refs_0_ = bf16[152,384]{1,0:T(8,128)(2,1)S(1)} collective-permute-done((bf16[152,384]{1,0:T(8,128)(2,1)S(1)}, bf16[152,384]{1,0:T(8,128)(2,1)S(1)}, u32[]{:S(2)}, u32[]{:S(2)}) %collective-permute-start.17) | collective-permute-done | bytes 116768 | tf_op jit(solution)/shard_map/ppermute | solution.py:24
  86.2 0.9 collective-permute-start.19
  87.1 1.1 %collective-permute-start.23 = (bf16[152,384]{1,0:T(8,128)(2,1)S(1)}, bf16[152,384]{1,0:T(8,128)(2,1)S(1)}, u32[]{:S(2)}, u32[]{:S(2)}) collective-permute-start(bf16[152,384]{1,0:T(8,128)(2,1)S(1)} %collective-permute-done.21.refs_4_), channel_id=1, source_target_pairs={{0,2},{2,0},{4,6},{6,4},{8,10},{10,8},{12,14},{14,12},{1,3},{3,1},... | collective-permute-start | bytes 350216 | tf_op jit(solution)/shard_map/ppermute | solution.py:24
  88.8 3.4 %collective-permute-done.19.refs_2_ = bf16[152,384]{1,0:T(8,128)(2,1)S(1)} collective-permute-done((bf16[152,384]{1,0:T(8,128)(2,1)S(1)}, bf16[152,384]{1,0:T(8,128)(2,1)S(1)}, u32[]{:S(2)}, u32[]{:S(2)}) %collective-permute-start.19) | collective-permute-done | bytes 116768 | tf_op jit(solution)/shard_map/ppermute | solution.py:24
  92.3 1.6 %collective-permute-done.23.refs_6_ = bf16[152,384]{1,0:T(8,128)(2,1)S(1)} collective-permute-done((bf16[152,384]{1,0:T(8,128)(2,1)S(1)}, bf16[152,384]{1,0:T(8,128)(2,1)S(1)}, u32[]{:S(2)}, u32[]{:S(2)}) %collective-permute-start.23) | collective-permute-done | bytes 116768 | tf_op jit(solution)/shard_map/ppermute | solution.py:24
  93.8 1.9 %copy-done.1 = bf16[1536,1024]{1,0:T(8,128)(2,1)S(1)} copy-done((bf16[1536,1024]{1,0:T(8,128)(2,1)S(1)}, bf16[1536,1024]{1,0:T(8,128)(2,1)}, u32[]{:S(2)}) %copy-start.1) | copy-done | bytes 3145752
  96.3 1.8 %attention.2 = (f32[1024,128]{1,0:T(8,128)S(1)}, f32[1024,256]{1,0:T(8,128)S(1)}, f32[12,384]{1,0:T(8,128)S(1)}) custom-call(bf16[1024,128]{1,0:T(8,128)(2,1)S(1)} %query.1.query_ref, bf16[152,384]{1,0:T(8,128)(2,1)S(1)} %get-tuple-element.37.refs_0_, bf16[152,384]{1,0:T(8,128)(2,1)S(1)} %collective-permute-done.25.refs_1_, ...), custom_call_target="tpu_custom_call" | custom-call | flops 2000 | bytes 2000 | tf_op jit(solution)/shard_map/attention/pallas_call | solution.py:560
  98.2 6.1 %attention.3 = (bf16[128,1536]{1,0:T(8,128)(2,1)}, f32[3,1536]{1,0:T(4,128)}) custom-call(bf16[1024,128]{1,0:T(8,128)(2,1)S(1)} %query.1.query_ref, bf16[152,384]{1,0:T(8,128)(2,1)S(1)} %collective-permute-done.17.refs_0_, bf16[152,384]{1,0:T(8,128)(2,1)S(1)} %collective-permute-done.18.refs_1_, bf16[152,384]{1,0:T(8,128)(2,1)S(1)} %collective-permute-done.19.refs_2_, ...), custom_call_target="tpu_custom_call" | custom-call | flops 5000 | bytes 5000 | tf_op jit(solution)/shard_map/attention/pallas_call | solution.py:560
  (94 shorter events, 5.8 us)
Async XLA Ops:
  1.8 19.7 %collective-permute-start.10 = (bf16[200,768]{1,0:T(8,128)(2,1)S(1)}, bf16[200,768]{1,0:T(8,128)(2,1)S(1)}, u32[]{:S(2)}, u32[]{:S(2)}) collective-permute-start(bf16[200,768]{1,0:T(8,128)(2,1)S(1)} %pad_maximum_fusion.refs_0_), channel_id=1, source_target_pairs={{0,8},{2,10},{4,12},{6,14},{8,0},{10,2},{12,4},{14,6},{1,9},{3,11}... | collective-permute-start | bytes 921608 | tf_op jit(solution)/shard_map/ppermute | solution.py:24
  5.9 23.2 %collective-permute-start.6 = (bf16[200,768]{1,0:T(8,128)(2,1)S(1)}, bf16[200,768]{1,0:T(8,128)(2,1)S(1)}, u32[]{:S(2)}, u32[]{:S(2)}) collective-permute-start(bf16[200,768]{1,0:T(8,128)(2,1)S(1)} %pad_maximum_fusion.refs_0_), channel_id=1, source_target_pairs={{0,4},{2,6},{4,0},{6,2},{8,12},{10,14},{12,8},{14,10},{1,5},{3,7},... | collective-permute-start | bytes 921608 | tf_op jit(solution)/shard_map/ppermute | solution.py:24
  7.5 23.1 %collective-permute-start = (bf16[200,768]{1,0:T(8,128)(2,1)S(1)}, bf16[200,768]{1,0:T(8,128)(2,1)}, u32[]{:S(2)}, u32[]{:S(2)}) collective-permute-start(bf16[200,768]{1,0:T(8,128)(2,1)S(1)} %pad_maximum_fusion.refs_0_), channel_id=1, source_target_pairs={{0,12},{2,14},{4,8},{6,10},{8,4},{10,6},{12,0},{14,2},{1,13},{3,15... | collective-permute-start | bytes 921608 | tf_op jit(solution)/shard_map/ppermute | solution.py:24
  7.5 23.6 %collective-permute-start.4 = (bf16[200,768]{1,0:T(8,128)(2,1)S(1)}, bf16[200,768]{1,0:T(8,128)(2,1)}, u32[]{:S(2)}, u32[]{:S(2)}) collective-permute-start(bf16[200,768]{1,0:T(8,128)(2,1)S(1)} %pad_maximum_fusion.refs_0_), channel_id=1, source_target_pairs={{0,2},{2,0},{4,6},{6,4},{8,10},{10,8},{12,14},{14,12},{1,3},{3,1},... | collective-permute-start | bytes 921608 | tf_op jit(solution)/shard_map/ppermute | solution.py:24
  9.2 21.9 %collective-permute-start.3 = (bf16[200,768]{1,0:T(8,128)(2,1)S(1)}, bf16[200,768]{1,0:T(8,128)(2,1)S(1)}, u32[]{:S(2)}, u32[]{:S(2)}) collective-permute-start(bf16[200,768]{1,0:T(8,128)(2,1)S(1)} %pad_maximum_fusion.refs_0_), channel_id=1, source_target_pairs={{0,1},{1,0},{2,3},{3,2},{4,5},{5,4},{6,7},{7,6},{8,9},{9,8},{10,11... | collective-permute-start | bytes 921608 | tf_op jit(solution)/shard_map/ppermute | solution.py:28
  21.5 14.4 %collective-permute-start.12 = (bf16[200,768]{1,0:T(8,128)(2,1)S(1)}, bf16[200,768]{1,0:T(8,128)(2,1)}, u32[]{:S(2)}, u32[]{:S(2)}) collective-permute-start(bf16[200,768]{1,0:T(8,128)(2,1)S(1)} %collective-permute-done.10.refs_8_), channel_id=1, source_target_pairs={{0,2},{2,0},{4,6},{6,4},{8,10},{10,8},{12,14},{14,12},{1,3},{3,1},... | collective-permute-start | bytes 921608 | tf_op jit(solution)/shard_map/ppermute | solution.py:24
  29.1 13.9 %collective-permute-start.2 = (bf16[256,1408]{1,0:T(8,128)(2,1)}, bf16[256,1408]{1,0:T(8,128)(2,1)S(1)}, u32[]{:S(2)}, u32[]{:S(2)}) collective-permute-start(bf16[256,1408]{1,0:T(8,128)(2,1)} %own_hbm.1), channel_id=1, source_target_pairs={{0,16},{16,0},{1,17},{17,1},{2,18},{18,2},{3,19},{19,3},{4,20},{20... | collective-permute-start | bytes 2162696 | tf_op jit(solution)/shard_map/ppermute | solution.py:32
  30.6 8.6 %collective-permute-start.8 = (bf16[200,768]{1,0:T(8,128)(2,1)S(1)}, bf16[200,768]{1,0:T(8,128)(2,1)}, u32[]{:S(2)}, u32[]{:S(2)}) collective-permute-start(bf16[200,768]{1,0:T(8,128)(2,1)S(1)} %collective-permute-done.6.refs_4_), channel_id=1, source_target_pairs={{0,2},{2,0},{4,6},{6,4},{8,10},{10,8},{12,14},{14,12},{1,3},{3,1},... | collective-permute-start | bytes 921608 | tf_op jit(solution)/shard_map/ppermute | solution.py:24
  31.1 8.1 %collective-permute-start.11 = (bf16[200,768]{1,0:T(8,128)(2,1)S(1)}, bf16[200,768]{1,0:T(8,128)(2,1)S(1)}, u32[]{:S(2)}, u32[]{:S(2)}) collective-permute-start(bf16[200,768]{1,0:T(8,128)(2,1)S(1)} %collective-permute-done.10.refs_8_), channel_id=1, source_target_pairs={{0,1},{1,0},{2,3},{3,2},{4,5},{5,4},{6,7},{7,6},{8,9},{9,8},{10,11... | collective-permute-start | bytes 921608 | tf_op jit(solution)/shard_map/ppermute | solution.py:28
  31.1 8.6 %collective-permute-start.14 = (bf16[200,768]{1,0:T(8,128)(2,1)}, bf16[200,768]{1,0:T(8,128)(2,1)S(1)}, u32[]{:S(2)}, u32[]{:S(2)}) collective-permute-start(bf16[200,768]{1,0:T(8,128)(2,1)} %collective-permute-done.refs_12_), channel_id=1, source_target_pairs={{0,1},{1,0},{2,3},{3,2},{4,5},{5,4},{6,7},{7,6},{8,9},{9,8},{10,11... | collective-permute-start | bytes 921608 | tf_op jit(solution)/shard_map/ppermute | solution.py:28
  35.9 3.9 %collective-permute-start.7 = (bf16[200,768]{1,0:T(8,128)(2,1)S(1)}, bf16[200,768]{1,0:T(8,128)(2,1)S(1)}, u32[]{:S(2)}, u32[]{:S(2)}) collective-permute-start(bf16[200,768]{1,0:T(8,128)(2,1)S(1)} %collective-permute-done.6.refs_4_), channel_id=1, source_target_pairs={{0,1},{1,0},{2,3},{3,2},{4,5},{5,4},{6,7},{7,6},{8,9},{9,8},{10,11... | collective-permute-start | bytes 921608 | tf_op jit(solution)/shard_map/ppermute | solution.py:28
  39.2 3.8 %collective-permute-start.5 = (bf16[200,768]{1,0:T(8,128)(2,1)}, bf16[200,768]{1,0:T(8,128)(2,1)}, u32[]{:S(2)}, u32[]{:S(2)}) collective-permute-start(bf16[200,768]{1,0:T(8,128)(2,1)} %collective-permute-done.4.refs_2_), channel_id=1, source_target_pairs={{0,1},{1,0},{2,3},{3,2},{4,5},{5,4},{6,7},{7,6},{8,9},{9,8},{10,11... | collective-permute-start | bytes 921608 | tf_op jit(solution)/shard_map/ppermute | solution.py:28
  39.2 3.8 %collective-permute-start.13 = (bf16[200,768]{1,0:T(8,128)(2,1)}, bf16[200,768]{1,0:T(8,128)(2,1)}, u32[]{:S(2)}, u32[]{:S(2)}) collective-permute-start(bf16[200,768]{1,0:T(8,128)(2,1)} %collective-permute-done.12.refs_10_), channel_id=1, source_target_pairs={{0,1},{1,0},{2,3},{3,2},{4,5},{5,4},{6,7},{7,6},{8,9},{9,8},{10,11... | collective-permute-start | bytes 921608 | tf_op jit(solution)/shard_map/ppermute | solution.py:28
  39.7 4.2 %collective-permute-start.9 = (bf16[200,768]{1,0:T(8,128)(2,1)}, bf16[200,768]{1,0:T(8,128)(2,1)}, u32[]{:S(2)}, u32[]{:S(2)}) collective-permute-start(bf16[200,768]{1,0:T(8,128)(2,1)} %collective-permute-done.8.refs_6_), channel_id=1, source_target_pairs={{0,1},{1,0},{2,3},{3,2},{4,5},{5,4},{6,7},{7,6},{8,9},{9,8},{10,11... | collective-permute-start | bytes 921608 | tf_op jit(solution)/shard_map/ppermute | solution.py:28
  39.8 10.9 %collective-permute-start.1 = (bf16[200,768]{1,0:T(8,128)(2,1)}, bf16[200,768]{1,0:T(8,128)(2,1)}, u32[]{:S(2)}, u32[]{:S(2)}) collective-permute-start(bf16[200,768]{1,0:T(8,128)(2,1)} %collective-permute-done.refs_12_), channel_id=1, source_target_pairs={{0,2},{2,0},{4,6},{6,4},{8,10},{10,8},{12,14},{14,12},{1,3},{3,1},... | collective-permute-start | bytes 921608 | tf_op jit(solution)/shard_map/ppermute | solution.py:24
  54.7 15.3 %all-to-all-start = ((bf16[16,16,256]{2,1,0:T(8,128)(2,1)}), bf16[16,16,256]{2,1,0:T(8,128)(2,1)S(1)}, u32[]{:S(2)}, u32[]{:S(2)}) async-start(bf16[16,16,256]{2,1,0:T(8,128)(2,1)} %windows.1), calls=%async_computation | async-start | bytes 262144 | tf_op jit(solution)/shard_map/all_to_all | solution.py:471
  62.4 8.6 %collective-permute-start.16 = (bf16[128,768]{1,0:T(8,128)(2,1)S(1)}, bf16[128,768]{1,0:T(8,128)(2,1)S(1)}, u32[]{:S(2)}, u32[]{:S(2)}) collective-permute-start(bf16[128,768]{1,0:T(8,128)(2,1)S(1)} %get-tuple-element.29), channel_id=1, source_target_pairs={{0,16},{16,0},{1,17},{17,1},{2,18},{18,2},{3,19},{19,3},{4,20},{20... | collective-permute-start | bytes 589832 | tf_op jit(solution)/shard_map/ppermute | solution.py:32
  72.9 4.8 %collective-permute-start.28 = (bf16[152,384]{1,0:T(8,128)(2,1)S(1)}, bf16[152,384]{1,0:T(8,128)(2,1)S(1)}, u32[]{:S(2)}, u32[]{:S(2)}) collective-permute-start(bf16[152,384]{1,0:T(8,128)(2,1)S(1)} %get-tuple-element.37.refs_0_), channel_id=1, source_target_pairs={{0,4},{2,6},{4,0},{6,2},{8,12},{10,14},{12,8},{14,10},{1,5},{3,7},... | collective-permute-start | bytes 350216 | tf_op jit(solution)/shard_map/ppermute | solution.py:24
  73.2 6.1 %collective-permute-start.26 = (bf16[152,384]{1,0:T(8,128)(2,1)S(1)}, bf16[152,384]{1,0:T(8,128)(2,1)S(1)}, u32[]{:S(2)}, u32[]{:S(2)}) collective-permute-start(bf16[152,384]{1,0:T(8,128)(2,1)S(1)} %get-tuple-element.37.refs_0_), channel_id=1, source_target_pairs={{0,2},{2,0},{4,6},{6,4},{8,10},{10,8},{12,14},{14,12},{1,3},{3,1},... | collective-permute-start | bytes 350216 | tf_op jit(solution)/shard_map/ppermute | solution.py:24
  74.7 4.6 %collective-permute-start.25 = (bf16[152,384]{1,0:T(8,128)(2,1)S(1)}, bf16[152,384]{1,0:T(8,128)(2,1)S(1)}, u32[]{:S(2)}, u32[]{:S(2)}) collective-permute-start(bf16[152,384]{1,0:T(8,128)(2,1)S(1)} %get-tuple-element.37.refs_0_), channel_id=1, source_target_pairs={{0,1},{1,0},{2,3},{3,2},{4,5},{5,4},{6,7},{7,6},{8,9},{9,8},{10,11... | collective-permute-start | bytes 350216 | tf_op jit(solution)/shard_map/ppermute | solution.py:28
  74.7 11.5 %collective-permute-start.17 = (bf16[152,384]{1,0:T(8,128)(2,1)S(1)}, bf16[152,384]{1,0:T(8,128)(2,1)S(1)}, u32[]{:S(2)}, u32[]{:S(2)}) collective-permute-start(bf16[152,384]{1,0:T(8,128)(2,1)S(1)} %get-tuple-element.37.refs_0_), channel_id=1, source_target_pairs={{0,8},{2,10},{4,12},{6,14},{8,0},{10,2},{12,4},{14,6},{1,9},{3,11}... | collective-permute-start | bytes 350216 | tf_op jit(solution)/shard_map/ppermute | solution.py:24
  77.0 10.1 %collective-permute-start.21 = (bf16[152,384]{1,0:T(8,128)(2,1)S(1)}, bf16[152,384]{1,0:T(8,128)(2,1)S(1)}, u32[]{:S(2)}, u32[]{:S(2)}) collective-permute-start(bf16[152,384]{1,0:T(8,128)(2,1)S(1)} %get-tuple-element.37.refs_0_), channel_id=1, source_target_pairs={{0,12},{2,14},{4,8},{6,10},{8,4},{10,6},{12,0},{14,2},{1,13},{3,15... | collective-permute-start | bytes 350216 | tf_op jit(solution)/shard_map/ppermute | solution.py:24
  77.7 10.6 %collective-permute-start.30 = (bf16[152,384]{1,0:T(8,128)(2,1)S(1)}, bf16[152,384]{1,0:T(8,128)(2,1)S(1)}, u32[]{:S(2)}, u32[]{:S(2)}) collective-permute-start(bf16[152,384]{1,0:T(8,128)(2,1)S(1)} %collective-permute-done.28.refs_4_), channel_id=1, source_target_pairs={{0,2},{2,0},{4,6},{6,4},{8,10},{10,8},{12,14},{14,12},{1,3},{3,1},... | collective-permute-start | bytes 350216 | tf_op jit(solution)/shard_map/ppermute | solution.py:24
  79.3 9.0 %collective-permute-start.27 = (bf16[152,384]{1,0:T(8,128)(2,1)S(1)}, bf16[152,384]{1,0:T(8,128)(2,1)S(1)}, u32[]{:S(2)}, u32[]{:S(2)}) collective-permute-start(bf16[152,384]{1,0:T(8,128)(2,1)S(1)} %collective-permute-done.26.refs_2_), channel_id=1, source_target_pairs={{0,1},{1,0},{2,3},{3,2},{4,5},{5,4},{6,7},{7,6},{8,9},{9,8},{10,11... | collective-permute-start | bytes 350216 | tf_op jit(solution)/shard_map/ppermute | solution.py:28
  79.3 9.5 %collective-permute-start.29 = (bf16[152,384]{1,0:T(8,128)(2,1)S(1)}, bf16[152,384]{1,0:T(8,128)(2,1)S(1)}, u32[]{:S(2)}, u32[]{:S(2)}) collective-permute-start(bf16[152,384]{1,0:T(8,128)(2,1)S(1)} %collective-permute-done.28.refs_4_), channel_id=1, source_target_pairs={{0,1},{1,0},{2,3},{3,2},{4,5},{5,4},{6,7},{7,6},{8,9},{9,8},{10,11... | collective-permute-start | bytes 350216 | tf_op jit(solution)/shard_map/ppermute | solution.py:28
  86.2 6.0 %collective-permute-start.19 = (bf16[152,384]{1,0:T(8,128)(2,1)S(1)}, bf16[152,384]{1,0:T(8,128)(2,1)S(1)}, u32[]{:S(2)}, u32[]{:S(2)}) collective-permute-start(bf16[152,384]{1,0:T(8,128)(2,1)S(1)} %collective-permute-done.17.refs_0_), channel_id=1, source_target_pairs={{0,2},{2,0},{4,6},{6,4},{8,10},{10,8},{12,14},{14,12},{1,3},{3,1},... | collective-permute-start | bytes 350216 | tf_op jit(solution)/shard_map/ppermute | solution.py:24
  87.1 6.7 %collective-permute-start.23 = (bf16[152,384]{1,0:T(8,128)(2,1)S(1)}, bf16[152,384]{1,0:T(8,128)(2,1)S(1)}, u32[]{:S(2)}, u32[]{:S(2)}) collective-permute-start(bf16[152,384]{1,0:T(8,128)(2,1)S(1)} %collective-permute-done.21.refs_4_), channel_id=1, source_target_pairs={{0,2},{2,0},{4,6},{6,4},{8,10},{10,8},{12,14},{14,12},{1,3},{3,1},... | collective-permute-start | bytes 350216 | tf_op jit(solution)/shard_map/ppermute | solution.py:24
  88.2 9.9 %collective-permute-start.18 = (bf16[152,384]{1,0:T(8,128)(2,1)S(1)}, bf16[152,384]{1,0:T(8,128)(2,1)S(1)}, u32[]{:S(2)}, u32[]{:S(2)}) collective-permute-start(bf16[152,384]{1,0:T(8,128)(2,1)S(1)} %collective-permute-done.17.refs_0_), channel_id=1, source_target_pairs={{0,1},{1,0},{2,3},{3,2},{4,5},{5,4},{6,7},{7,6},{8,9},{9,8},{10,11... | collective-permute-start | bytes 350216 | tf_op jit(solution)/shard_map/ppermute | solution.py:28
  88.3 8.1 %collective-permute-start.31 = (bf16[152,384]{1,0:T(8,128)(2,1)S(1)}, bf16[152,384]{1,0:T(8,128)(2,1)S(1)}, u32[]{:S(2)}, u32[]{:S(2)}) collective-permute-start(bf16[152,384]{1,0:T(8,128)(2,1)S(1)} %collective-permute-done.30.refs_6_), channel_id=1, source_target_pairs={{0,1},{1,0},{2,3},{3,2},{4,5},{5,4},{6,7},{7,6},{8,9},{9,8},{10,11... | collective-permute-start | bytes 350216 | tf_op jit(solution)/shard_map/ppermute | solution.py:28
  88.8 9.4 %collective-permute-start.22 = (bf16[152,384]{1,0:T(8,128)(2,1)S(1)}, bf16[152,384]{1,0:T(8,128)(2,1)S(1)}, u32[]{:S(2)}, u32[]{:S(2)}) collective-permute-start(bf16[152,384]{1,0:T(8,128)(2,1)S(1)} %collective-permute-done.21.refs_4_), channel_id=1, source_target_pairs={{0,1},{1,0},{2,3},{3,2},{4,5},{5,4},{6,7},{7,6},{8,9},{9,8},{10,11... | collective-permute-start | bytes 350216 | tf_op jit(solution)/shard_map/ppermute | solution.py:28
  92.3 5.9 %collective-permute-start.20 = (bf16[152,384]{1,0:T(8,128)(2,1)S(1)}, bf16[152,384]{1,0:T(8,128)(2,1)S(1)}, u32[]{:S(2)}, u32[]{:S(2)}) collective-permute-start(bf16[152,384]{1,0:T(8,128)(2,1)S(1)} %collective-permute-done.19.refs_2_), channel_id=1, source_target_pairs={{0,1},{1,0},{2,3},{3,2},{4,5},{5,4},{6,7},{7,6},{8,9},{9,8},{10,11... | collective-permute-start | bytes 350216 | tf_op jit(solution)/shard_map/ppermute | solution.py:28
  93.8 4.3 %collective-permute-start.24 = (bf16[152,384]{1,0:T(8,128)(2,1)S(1)}, bf16[152,384]{1,0:T(8,128)(2,1)S(1)}, u32[]{:S(2)}, u32[]{:S(2)}) collective-permute-start(bf16[152,384]{1,0:T(8,128)(2,1)S(1)} %collective-permute-done.23.refs_6_), channel_id=1, source_target_pairs={{0,1},{1,0},{2,3},{3,2},{4,5},{5,4},{6,7},{7,6},{8,9},{9,8},{10,11... | collective-permute-start | bytes 350216 | tf_op jit(solution)/shard_map/ppermute | solution.py:28
  (17 other events, 400.2 us)
